TPU v7x, 512 devices: a whole 4x4x16 slice. The times are simulated.
512 devices in a mesh: ctx: 16 (over z_lo, core), head: 32 (over x, y, z_hi).
Axes of the slice: x: 4, y: 4, z: 16 (z_hi: 2, z_lo: 8; z = z_hi * 8 + z_lo), core: 2. Of those that a mesh axis runs over, the one named last changes fastest.
Arguments:
- queries: bfloat16 [256, 24576], P('ctx', 'head'), may hold values from -8 to 8
- cache: bfloat16 [32768, 576], P(('ctx', 'head')), may hold values from -8 to 8
- key_up_weight: bfloat16 [128, 128, 512], P('head', None, 'ctx'), may hold values from -0.5 to 0.5
- value_up_weight: bfloat16 [128, 128, 512], P('head', None, 'ctx'), may hold values from -1.5 to 1.5
- prior_len: int32 [1], replicated, may hold values from 0 to 32512
Outputs:
- attended: bfloat16 [256, 16384], P('ctx', 'head')
All inputs are finite; a program needn't handle non-finite values.
Results may differ from a plain program's by a relative error of at most 0.02.
Values may be sent and summed in bfloat16 or wider, within the bound.
No kernel may reach another device: no remote copies, remote signals or barrier semaphores. Data moves between devices by JAX's collectives and lax.ppermute only.
A program may use at most 128 MiB of HBM per device.

v0:
```python
import jax
import jax.numpy as jnp
from jax import lax
from jax.sharding import PartitionSpec as P

PLAIN_WIDTH = 128
ROTARY_WIDTH = 64
LATENT_WIDTH = 512
VALUE_WIDTH = 128


def per_device(queries, cache, key_up_weight, value_up_weight, prior_len):
    heads_number = key_up_weight.shape[0]
    block_rows = queries.shape[0]
    combined_width = LATENT_WIDTH + ROTARY_WIDTH
    key_panel, value_panel = (
        lax.all_gather(key_up_weight, "ctx", axis=2, tiled=True),
        lax.all_gather(value_up_weight, "ctx", axis=2, tiled=True),
    )
    gathered = lax.all_gather(queries, "ctx", axis=0, tiled=True)
    split_rows = gathered.reshape(gathered.shape[0], heads_number, PLAIN_WIDTH + ROTARY_WIDTH)
    latent = jnp.einsum(
        "thn,hnc->thc",
        split_rows[:, :, :PLAIN_WIDTH],
        key_panel,
        preferred_element_type=jnp.float32,
    ).astype(jnp.bfloat16)
    flat_queries = jnp.concatenate([latent, split_rows[:, :, PLAIN_WIDTH:]], axis=2).reshape(
        -1, combined_width
    )
    flat_rows = flat_queries.shape[0]
    query_number = flat_rows // heads_number
    query_place = prior_len[0] + jnp.arange(flat_rows, dtype=jnp.int32) // heads_number
    group_slots = cache.shape[0] * lax.axis_size("head")
    block_base = lax.axis_index("ctx") * group_slots
    score_scale = (PLAIN_WIDTH + ROTARY_WIDTH) ** (-0.5)
    key_section = lax.all_gather(cache, "head", axis=0, tiled=True)
    row_peak = jnp.full((flat_rows,), -1e30, jnp.float32)
    key_count = key_section.shape[0]
    scores = (
        jnp.einsum("rc,nc->rn", flat_queries, key_section, preferred_element_type=jnp.float32)
        * score_scale
    )
    key_place = block_base + jnp.arange(key_count, dtype=jnp.int32)
    visible = key_place[None, :] <= query_place[:, None]
    scores = jnp.where(visible, scores, jnp.float32(-1e30))
    new_peak = jnp.maximum(row_peak, jnp.max(scores, axis=1))
    probabilities = jnp.where(visible, jnp.exp(scores - new_peak[:, None]), jnp.float32(0.0))
    row_total = jnp.sum(probabilities, axis=1)
    weighted_values = jnp.dot(
        probabilities.astype(jnp.bfloat16),
        key_section[:, :LATENT_WIDTH],
        preferred_element_type=jnp.float32,
    )
    row_peak, row_total, weighted_values = (new_peak, row_total, weighted_values)
    global_peak = lax.pmax(row_peak, "ctx")
    softmax_scale = jnp.exp(row_peak - global_peak)
    scaled_sums = (row_total * softmax_scale).reshape(query_number, heads_number)
    latent_scaled = (weighted_values * softmax_scale[:, None]).reshape(
        query_number, heads_number * LATENT_WIDTH
    )
    block_latent, own_totals = (
        lax.psum_scatter(
            latent_scaled.astype(jnp.bfloat16), "ctx", scatter_dimension=0, tiled=True
        ).astype(jnp.float32),
        lax.psum_scatter(
            scaled_sums.astype(jnp.bfloat16), "ctx", scatter_dimension=0, tiled=True
        ).astype(jnp.float32),
    )
    reshaped_queries = block_latent.reshape(block_rows, heads_number, LATENT_WIDTH)
    projected = jnp.einsum(
        "thc,hvc->thv",
        reshaped_queries,
        value_panel.astype(jnp.float32),
        precision=lax.Precision.HIGHEST,
    )
    result = projected / own_totals[:, :, None]
    return result.reshape(block_rows, heads_number * VALUE_WIDTH).astype(jnp.bfloat16)


def solution(mesh):
    in_specs = (
        P("ctx", "head"),
        P(("ctx", "head"), None),
        P("head", None, "ctx"),
        P("head", None, "ctx"),
        P(),
    )
    out_specs = P("ctx", "head")
    return jax.shard_map(
        per_device, mesh=mesh, in_specs=in_specs, out_specs=out_specs, check_vma=False
    )
```

profile of v0, /device:TPU:1, one launch (start us, length us, event | category | flops | bytes accessed | tf_op | source)
XLA Modules:
  0.0 416.8 jit_solution(6652268545688712268)
XLA Ops:
  6.5 0.0 all-gather.2.cloned.1.call-start
  6.5 0.7 all-gather.2.cloned.1.call-update
  7.3 0.0 reduce-scatter.7.cloned.1.call-start
  7.3 39.6 %all_gather.13 = bf16[256,768]{1,0:T(8,128)(2,1)S(1)} all-gather(bf16[16,768]{1,0:T(8,128)(2,1)} %param.5), channel_id=1, replica_groups=mesh['ctx'=16,'head'=32] {'ctx'}, dimensions={0}, use_global_device_ids=true | all-gather | bytes 417792 | tf_op jit(solution)/shard_map/all_gather | solution.py:20
  46.9 0.2 copy.25
  47.1 28.5 %all_gather.12 = bf16[4,128,512]{1,2,0:T(8,128)(2,1)S(1)} all-gather(bf16[4,128,32]{1,2,0:T(8,128)(2,1)} %param.7), channel_id=1, replica_groups=mesh['ctx'=16,'head'=32] {'ctx'}, dimensions={2}, use_global_device_ids=true | all-gather | bytes 557056 | tf_op jit(solution)/shard_map/all_gather | solution.py:17
  75.6 0.4 fusion.10
  76.1 0.1 pad_maximum_fusion
  76.2 1.4 copy.27
  77.6 0.7 reshape.39
  79.0 76.1 %all-gather.2.cloned.1.call-done = bf16[2048,576]{1,0:T(8,128)(2,1)} async-done(((bf16[64,576]{1,0:T(8,128)(2,1)}), bf16[2048,576]{1,0:T(8,128)(2,1)}) %all-gather.2.cloned.1.call-update) | async-done | bytes 2359312 | tf_op jit(solution)/shard_map/all_gather | solution.py:37
  155.0 7.8 %fusion = (f32[1024]{0:T(1024)S(1)}, f32[1024,2048]{1,0:T(8,128)}) fusion(s32[2048]{0:T(1024)S(1)} %iota_add_fusion, s32[1024]{0:T(1024)S(1)} %fusion.17, bf16[1024,576]{1,0:T(8,128)(2,1)S(1)} %reshape.39, bf16[2048,576]{1,0:T(8,128)(2,1)} %all-gather.2.cloned.1.call-done), kind=kOutput, calls=%fused_computation.2 | convolution fusion | flops 2424306688 | bytes 11943936 | tf_op jit(solution)/shard_map/rc,nc->rn/dot_general | solution.py:41
  162.8 48.9 %pmax.7 = f32[1024]{0:T(1024)S(1)} all-reduce(f32[1024]{0:T(1024)S(1)} %broadcast_maximum_fusion), channel_id=1, replica_groups=mesh['ctx'=16,'head'=32] {'ctx'}, use_global_device_ids=true, to_apply=%region_1.2 | all-reduce | flops 1024 | bytes 8192 | tf_op jit(solution)/shard_map/pmax | solution.py:56
  211.7 4.8 %fusion.1 = f32[1024]{0:T(1024)S(1)} fusion(f32[1024,2048]{1,0:T(8,128)} %get-tuple-element.8, f32[1024]{0:T(1024)S(1)} %broadcast_maximum_fusion, s32[2048]{0:T(1024)S(1)} %iota_add_fusion, s32[1024]{0:T(1024)S(1)} %fusion.17), kind=kLoop, calls=%fused_computation.3 | loop fusion | flops 12581888 | bytes 8409088 | tf_op jit(solution)/shard_map/reduce_sum | solution.py:49
  216.5 0.8 reshape.41
  217.3 0.0 reduce-scatter.7.cloned.1.call-update
  217.3 0.0 reduce-scatter.5.cloned.1.call-start
  217.3 0.0 copy-start
  217.3 6.4 %multiply_convert_fusion = bf16[1024,512]{1,0:T(8,128)(2,1)S(1)} fusion(bf16[2048,576]{1,0:T(8,128)(2,1)} %all-gather.2.cloned.1.call-done, f32[1024,2048]{1,0:T(8,128)} %get-tuple-element.8, f32[1024]{0:T(1024)S(1)} %broadcast_maximum_fusion, s32[2048]{0:T(1024)S(1)} %iota_add_fusion, s32[1024]{0:T(1024)S(1)} %fusion.17, f32[1024]{0:T(1024)S(1)} %get-tuple-element.6), kind=kOutput, calls=%fused_computation.7 | convolution fusion | flops 2161115136 | bytes 11554816 | tf_op jit(solution)/shard_map/dot_general | solution.py:50
  223.7 1.5 convert_element_type.36
  225.2 0.0 reduce-scatter.5.cloned.1.call-update
  225.2 0.0 copy-done
  225.2 28.4 %all_gather.15 = bf16[4,128,512]{1,2,0:T(8,128)(2,1)S(1)} all-gather(bf16[4,128,32]{1,2,0:T(8,128)(2,1)S(1)} %copy-done), channel_id=1, replica_groups=mesh['ctx'=16,'head'=32] {'ctx'}, dimensions={2}, use_global_device_ids=true | all-gather | bytes 557056 | tf_op jit(solution)/shard_map/all_gather | solution.py:18
  253.7 52.0 %reduce-scatter.7.cloned.1.call-done = bf16[16,4]{1,0:T(8,128)(2,1)} async-done(((bf16[256,4]{1,0:T(8,128)(2,1)}), bf16[16,4]{1,0:T(8,128)(2,1)}) %reduce-scatter.7.cloned.1.call-update) | async-done | bytes 144
  305.7 0.8 copy.32
  306.4 102.2 %reduce-scatter.5.cloned.1.call-done = bf16[16,2048]{1,0:T(8,128)(2,1)} async-done(((bf16[256,2048]{1,0:T(8,128)(2,1)}), bf16[16,2048]{1,0:T(8,128)(2,1)}) %reduce-scatter.5.cloned.1.call-update) | async-done | bytes 65552 | tf_op jit(solution)/shard_map/reduce_scatter | solution.py:63
  408.7 1.0 fusion.13
  409.7 0.6 copy.41
  (6 shorter events, 0.0 us)
Async XLA Ops:
  6.5 148.5 %all-gather.2.cloned.1.call-start = ((), (), s32[]{:S(2)}) async-start(), calls=%async_computation.2 | async-start | bytes 2703360 | tf_op jit(solution)/shard_map/all_gather | solution.py:37
  7.3 298.4 %reduce-scatter.7.cloned.1.call-start = ((), (), s32[]{:S(2)}) async-start(), calls=%async_computation.4 | async-start | bytes 69632
  217.3 191.4 %reduce-scatter.5.cloned.1.call-start = ((), (), s32[]{:S(2)}) async-start(), calls=%async_computation.3 | async-start | bytes 1114112 | tf_op jit(solution)/shard_map/reduce_scatter | solution.py:63
  217.3 7.9 %copy-start = (bf16[4,128,32]{1,2,0:T(8,128)(2,1)S(1)}, bf16[4,128,32]{1,2,0:T(8,128)(2,1)}, u32[]{:S(2)}) copy-start(bf16[4,128,32]{1,2,0:T(8,128)(2,1)} %param.8) | copy-start | bytes 98308
Sparse Core Ops, SparseCore 0:
  11.6 143.3 all-gather.1
  217.4 88.2 reduce-scatter.6
  308.7 99.8 reduce-scatter.4
where the time goes:
time: 424 us; the launch traced here: 417 us
  waiting for transfers between devices  231 us (54%)
  blocking collectives  145 us (34%)
  matrix products  15.6 us (4%)
  between operations  13.9 us (3%)
  local copies, waits for them, and re-layouts  5.9 us (1%)
  other arithmetic  4.91 us (1%)
    reduce_scatter x1, waiting for transfers between devices, per_device(): lax.psum_scatter(latent_scaled.astype(jnp.bfloat16), 'ctx', scatter_dimen...  102 us
    all_gather x1, waiting for transfers between devices, per_device(): key_section = lax.all_gather(cache, 'head', axis=0, tiled=True)  76.1 us
    unnamed x4, waiting for transfers between devices  52.8 us
    pmax x1, blocking collectives, per_device(): global_peak = lax.pmax(row_peak, 'ctx')  48.9 us
    all_gather x1, blocking collectives, per_device(): gathered = lax.all_gather(queries, 'ctx', axis=0, tiled=True)  39.6 us
    all_gather x1, blocking collectives, per_device(): lax.all_gather(key_up_weight, 'ctx', axis=2, tiled=True)  28.5 us
    all_gather x1, blocking collectives, per_device(): lax.all_gather(value_up_weight, 'ctx', axis=2, tiled=True)  28.4 us
  transfers between devices with their start and end apart: 3, of which 3 were waited for; matrix products, arithmetic and copies ran while one was open for 3% of the time, Pallas kernels for 0%

commit v1 on v0

v1 whole, which is shorter than its diff:
```python
import math

import jax
import jax.numpy as jnp
from jax import lax
from jax.experimental import pallas as pl
from jax.experimental.pallas import tpu as pltpu
from jax.sharding import Mesh
from jax.sharding import PartitionSpec as P

PLAIN = 128
ROT = 64
LATENT = 512
VALUE = 128
HEADS = 4
WIDTH = LATENT + ROT
TOK = 16
NEG = -1e30
LOG2_SCALE = (PLAIN + ROT) ** (-0.5) * math.log2(math.e)
VMEM_LIMIT = 48 * 1024 * 1024

f32 = jnp.float32
bf16 = jnp.bfloat16


def vmem():
    return pl.BlockSpec(memory_space=pltpu.VMEM)


def smem():
    return pl.BlockSpec(memory_space=pltpu.SMEM)


def chain_slot(zl, co, my_zl, my_co):
    dz = lax.bitwise_xor(my_zl, zl)
    dc = lax.bitwise_xor(my_co, co)
    a = lax.shift_right_logical(dz, 2)
    b = lax.bitwise_and(lax.shift_right_logical(dz, 1), 1)
    c = lax.bitwise_and(dz, 1)
    return dc * 8 + c * 4 + b * 2 + a


def query_kernel(place, pack, q_out, wv_out, pieces, panel):
    my_zl, my_co = place[0], place[1]
    for co in range(2):
        for zl in range(8):
            slot = chain_slot(jnp.int32(zl), jnp.int32(co), my_zl, my_co)
            rows = pl.ds((co * 8 + zl) * TOK, TOK)
            cols = pl.ds((zl * 2 + co) * 32, 32)
            for k in range(6):
                pieces[k, rows, :] = pack[slot, pl.ds(k * TOK, TOK), :]
            for h in range(HEADS):
                panel[h, cols, :] = pack[slot, pl.ds(96 + h * 32, 32), :]
                wv_out[h, cols, :] = pack[slot, pl.ds(224 + h * 32, 32), :]
    for h in range(HEADS):
        k = (h // 2) * 3
        if h % 2 == 0:
            plain = pieces[k]
            rot = pieces[k + 1][:, :ROT]
        else:
            plain = jnp.concatenate([pieces[k + 1][:, ROT:], pieces[k + 2][:, :ROT]], axis=1)
            rot = pieces[k + 2][:, ROT:]
        lat = lax.dot_general(
            plain, panel[h], (((1,), (1,)), ((), ())), preferred_element_type=f32
        )
        q_out[h, :, :LATENT] = lat.astype(bf16)
        q_out[h, :, LATENT:] = rot


def split3(x):
    hi = x.astype(bf16)
    r = x - hi.astype(f32)
    mid = r.astype(bf16)
    lo = (r - mid.astype(f32)).astype(bf16)
    return hi, mid, lo


def pack_lse(columns, shape):
    lane = lax.broadcasted_iota(jnp.int32, shape, len(shape) - 1)
    tile = jnp.zeros(shape, f32)
    for h, column in enumerate(columns):
        for p, part in enumerate(split3(column)):
            tile = jnp.where(lane == 3 * h + p, part.astype(f32), tile)
    return tile.astype(bf16)


def attention_kernel(prior, kpos, q, c0, c1, c2, c3, wv, out):
    row = lax.broadcasted_iota(jnp.int32, (256, 1), 0)
    zl = lax.bitwise_and(lax.shift_right_logical(row, 4), 7)
    co = lax.shift_right_logical(row, 7)
    token = zl * 32 + co * 16 + lax.bitwise_and(row, 15)
    limit = prior[0] + token
    chunks = (c0, c1, c2, c3)
    lses = []
    for h in range(HEADS):
        scores = []
        for j, c in enumerate(chunks):
            s = lax.dot_general(
                q[h], c[...], (((1,), (1,)), ((), ())), preferred_element_type=f32
            )
            seen = kpos[:, pl.ds(j * 512, 512)] <= limit
            scores.append(jnp.where(seen, s * LOG2_SCALE, NEG))
        peak = scores[0].max(axis=1, keepdims=True)
        for s in scores[1:]:
            peak = jnp.maximum(peak, s.max(axis=1, keepdims=True))
        total = jnp.zeros((256, 1), f32)
        acc = jnp.zeros((256, LATENT), f32)
        for s, c in zip(scores, chunks):
            p = jnp.exp2(s - peak)
            total = total + p.sum(axis=1, keepdims=True)
            acc = acc + jnp.dot(p.astype(bf16), c[:, :LATENT], preferred_element_type=f32)
        latent = (acc / total).astype(bf16)
        o = jnp.dot(latent, wv[h], preferred_element_type=f32).astype(bf16)
        for g in range(16):
            out[g // 8, g % 8, h] = o[g * TOK : (g + 1) * TOK]
        lses.append(peak + jnp.log2(total))
    tile = pack_lse(lses, (256, 128))
    for g in range(16):
        out[g // 8, g % 8, HEADS] = tile[g * TOK : (g + 1) * TOK]


def lse_column(tile, h):
    t = tile.astype(f32)
    k = 3 * h
    return t[:, k : k + 1] + t[:, k + 1 : k + 2] + t[:, k + 2 : k + 3]


def pair_kernel(a, b, out):
    for g in range(8):
        ta, tb = a[g, HEADS], b[g, HEADS]
        lses = []
        for h in range(HEADS):
            la, lb = lse_column(ta, h), lse_column(tb, h)
            top = jnp.maximum(la, lb)
            wa, wb = jnp.exp2(la - top), jnp.exp2(lb - top)
            total = wa + wb
            o = (a[g, h].astype(f32) * wa + b[g, h].astype(f32) * wb) / total
            out[g, h] = o.astype(bf16)
            lses.append(top + jnp.log2(total))
        out[g, HEADS] = pack_lse(lses, (TOK, 128))


def final_kernel(x, out):
    for h in range(HEADS):
        lses = [lse_column(x[g, HEADS], h) for g in range(8)]
        top = lses[0]
        for l in lses[1:]:
            top = jnp.maximum(top, l)
        acc = jnp.zeros((TOK, VALUE), f32)
        total = jnp.zeros((TOK, 1), f32)
        for g in range(8):
            w = jnp.exp2(lses[g] - top)
            total = total + w
            acc = acc + x[g, h].astype(f32) * w
        out[:, h * VALUE : (h + 1) * VALUE] = (acc / total).astype(bf16)


def swap(x, axis, n, d):
    return lax.ppermute(x, axis, [(i, i ^ d) for i in range(n)])


def call(kernel, shape, n_in, name, scratch=(), scalars=0):
    return pl.pallas_call(
        kernel,
        out_shape=shape,
        in_specs=[smem()] * scalars + [vmem()] * n_in,
        out_specs=jax.tree.map(lambda _: vmem(), shape),
        scratch_shapes=list(scratch),
        compiler_params=pltpu.CompilerParams(vmem_limit_bytes=VMEM_LIMIT),
        name=name,
    )


def per_device(queries, cache, key_up_weight, value_up_weight, prior_len):
    zl, co = lax.axis_index("zl"), lax.axis_index("co")
    x, y, zh = lax.axis_index("x"), lax.axis_index("y"), lax.axis_index("zh")

    pack = jnp.concatenate(
        [
            queries.reshape(TOK, 6, 128).transpose(1, 0, 2).reshape(96, 128),
            key_up_weight.transpose(0, 2, 1).reshape(128, 128),
            value_up_weight.transpose(0, 2, 1).reshape(128, 128),
        ],
        axis=0,
    )[None]
    mirror = lax.ppermute(cache, ("zl", "zh"), [(i, 15 - i) for i in range(16)])
    for d in (4, 2, 1):
        pack = jnp.concatenate([pack, swap(pack, "zl", 8, d)], axis=0)
    pack = jnp.concatenate([pack, swap(pack, "co", 2, 1)], axis=0)
    pair = jnp.concatenate([cache, mirror], axis=0)
    quad = jnp.concatenate([pair] + [swap(pair, "x", 4, d) for d in (1, 2, 3)], axis=0)
    chunks = [quad] + [swap(quad, "y", 4, d) for d in (1, 2, 3)]

    place = jnp.stack([zl, co]).astype(jnp.int32)
    q, wv = call(
        query_kernel,
        (
            jax.ShapeDtypeStruct((HEADS, 256, WIDTH), bf16),
            jax.ShapeDtypeStruct((HEADS, LATENT, VALUE), bf16),
        ),
        1,
        "query",
        (pltpu.VMEM((6, 256, 128), bf16), pltpu.VMEM((HEADS, LATENT, 128), bf16)),
        1,
    )(place, pack)

    n = jnp.arange(2048, dtype=jnp.int32)
    dy, dx, m, i = n >> 9, (n >> 7) & 3, (n >> 6) & 1, n & 63
    src_z, src_h = jnp.where(m == 1, 7 - zl, zl), jnp.where(m == 1, 1 - zh, zh)
    head = ((x ^ dx) * 4 + (y ^ dy)) * 2 + src_h
    kpos = (((src_z * 2 + co) * 32 + head) * 64 + i).astype(jnp.int32)[None]

    part = call(
        attention_kernel,
        jax.ShapeDtypeStruct((2, 8, HEADS + 1, TOK, 128), bf16),
        7,
        "attention",
        (),
        1,
    )(prior_len, kpos, q, *chunks, wv)

    mine = lax.dynamic_index_in_dim(part, co, 0, keepdims=False)
    other = lax.dynamic_index_in_dim(part, 1 - co, 0, keepdims=False)
    got = swap(other, "co", 2, 1)
    merged = call(
        pair_kernel, jax.ShapeDtypeStruct((8, HEADS + 1, TOK, 128), bf16), 2, "pair"
    )(mine, got)
    spread = lax.all_to_all(merged, "zl", 0, 0, tiled=True)
    return call(
        final_kernel, jax.ShapeDtypeStruct((TOK, HEADS * VALUE), bf16), 1, "final"
    )(spread)


def solution(mesh):
    fine = Mesh(mesh.devices.reshape(8, 2, 4, 4, 2), ("zl", "co", "x", "y", "zh"))
    ctx, head = ("zl", "co"), ("x", "y", "zh")
    return jax.shard_map(
        per_device,
        mesh=fine,
        in_specs=(P(ctx, head), P(ctx + head, None), P(head, None, ctx), P(head, None, ctx), P()),
        out_specs=P(ctx, head),
        check_vma=False,
    )
```

time: 424 us -> 128 us (0.30); the launches traced: 417 us -> 125 us
  waiting for transfers between devices: 231 us -> 29 us
  blocking collectives: 145 us -> 17.2 us
  starting transfers between devices: 0.08 us -> 53.2 us
  matrix products: 15.6 us -> 0 us
  between operations: 13.9 us -> 0.95 us
  Pallas kernels: 0 us -> 11.1 us
  local copies, waits for them, and re-layouts: 5.9 us -> 12 us
    reduce_scatter x1 -> x0, waiting for transfers between devices: 102 us -> none  [per_device(): lax.psum_scatter(latent_scaled.astype(jnp.bfloat16), 'ctx', scatter_dimen...]
    all_gather x3 -> x0, blocking collectives: 96.6 us -> none  [the longest x1 39.6 us: per_device(): gathered = lax.all_gather(queries, 'ctx', axis=0, tiled=True)]
    all_gather x1 -> x0, waiting for transfers between devices: 76.1 us -> none  [per_device(): key_section = lax.all_gather(cache, 'head', axis=0, tiled=True)]
    ppermute x0 -> x12, starting transfers between devices: none -> 53.2 us  [the longest x11 45.7 us: swap(): return lax.ppermute(x, axis, [(i, i ^ d) for i in range(n)])]
    unnamed x4 -> x0, waiting for transfers between devices: 52.8 us -> none
    pmax x1 -> x0, blocking collectives: 48.9 us -> none  [per_device(): global_peak = lax.pmax(row_peak, 'ctx')]
    ppermute x0 -> x12, waiting for transfers between devices: none -> 29 us  [the longest x11 29 us: swap(): return lax.ppermute(x, axis, [(i, i ^ d) for i in range(n)])]
    all_to_all x0 -> x1, blocking collectives: none -> 17.2 us  [per_device(): spread = lax.all_to_all(merged, 'zl', 0, 0, tiled=True)]
  transfers between devices with their start and end apart: 3 -> 12, of which waited for: 3 -> 6; matrix products, arithmetic and copies ran while one was open for 3% -> 6% of each run, Pallas kernels for 0% -> 0%
where the time goes in v1:
time: 128 us; the launch traced here: 125 us
  starting transfers between devices  53.2 us (42%)
  waiting for transfers between devices  29 us (23%)
  blocking collectives  17.2 us (13%)
  local copies, waits for them, and re-layouts  12 us (9%)
  Pallas kernels  11.1 us (9%)
  other arithmetic  1.96 us (2%)
    ppermute x11, starting transfers between devices, swap(): return lax.ppermute(x, axis, [(i, i ^ d) for i in range(n)])  45.7 us
    ppermute x11, waiting for transfers between devices, swap(): return lax.ppermute(x, axis, [(i, i ^ d) for i in range(n)])  29 us
    all_to_all x1, blocking collectives, per_device(): spread = lax.all_to_all(merged, 'zl', 0, 0, tiled=True)  17.2 us
    pallas_call x1, Pallas kernels, per_device(): call(attention_kernel, jax.ShapeDtypeStruct((2, 8, HEADS + 1, TOK, 128),...  7.89 us
    ppermute x1, starting transfers between devices, per_device(): mirror = lax.ppermute(cache, ('zl', 'zh'), [(i, 15 - i) for i in range(16)])  7.49 us
    unnamed x14, local copies, waits for them, and re-layouts  4.14 us
    ppermute x3, local copies, waits for them, and re-layouts, swap(): return lax.ppermute(x, axis, [(i, i ^ d) for i in range(n)])  4.07 us
  transfers between devices with their start and end apart: 12, of which 6 were waited for; matrix products, arithmetic and copies ran while one was open for 6% of the time, Pallas kernels for 0%

profile of v1, /device:TPU:1, one launch (start us, length us, event | category | flops | bytes accessed | tf_op | source)
XLA Modules:
  0.0 125.4 jit_solution(4986255087849001147)
XLA Ops:
  0.0 0.0 copy-start.2
  0.0 0.8 reshape.88
  0.8 0.0 copy-start.3
  0.8 0.8 maximum_bitcast_fusion
  1.6 9.6 %collective-permute-start = (bf16[1,352,128]{2,1,0:T(8,128)(2,1)S(1)}, bf16[1,352,128]{2,1,0:T(8,128)(2,1)S(1)}, u32[]{:S(2)}, u32[]{:S(2)}) collective-permute-start(bf16[1,352,128]{2,1,0:T(8,128)(2,1)S(1)} %maximum_bitcast_fusion), channel_id=1, source_target_pairs={{0,256},{64,320},{128,384},{192,448},{256,0},{320,64},{384,128},{4... | collective-permute-start | bytes 270344 | tf_op jit(solution)/shard_map/ppermute | solution.py:159
  11.3 7.5 %collective-permute-start.4 = (bf16[64,576]{1,0:T(8,128)(2,1)}, bf16[64,576]{1,0:T(8,128)(2,1)S(1)}, u32[]{:S(2)}, u32[]{:S(2)}) collective-permute-start(bf16[64,576]{1,0:T(8,128)(2,1)} %param.6), channel_id=1, source_target_pairs={{0,449},{1,448},{64,385},{65,384},{128,321},{129,320},{192,257},{1... | collective-permute-start | bytes 221192 | tf_op jit(solution)/shard_map/ppermute | solution.py:186
  18.8 0.0 collective-permute-done
  18.8 4.9 %collective-permute-start.1 = (bf16[2,352,128]{2,1,0:T(8,128)(2,1)S(1)}, bf16[2,352,128]{2,1,0:T(8,128)(2,1)S(1)}, u32[]{:S(2)}, u32[]{:S(2)}) collective-permute-start(bf16[2,352,128]{2,1,0:T(8,128)(2,1)S(1)} %pad_maximum_fusion.2), channel_id=1, source_target_pairs={{0,128},{64,192},{128,0},{192,64},{256,384},{320,448},{384,256},{4... | collective-permute-start | bytes 540680 | tf_op jit(solution)/shard_map/ppermute | solution.py:159
  23.7 1.5 %constant_dynamic-update-slice_fusion.6 = (bf16[128,576]{1,0:T(8,128)(2,1)}, bf16[512,576]{1,0:T(8,128)(2,1)S(1)}) fusion(bf16[64,576]{1,0:T(8,128)(2,1)} %param.6), kind=kLoop, calls=%fused_computation.12 | loop fusion | bytes 237568
  25.2 0.0 collective-permute-done.4
  25.2 0.6 constant_dynamic-update-slice_fusion.5
  25.9 3.1 %collective-permute-start.5 = (bf16[128,576]{1,0:T(8,128)(2,1)}, bf16[128,576]{1,0:T(8,128)(2,1)S(1)}, u32[]{:S(2)}, u32[]{:S(2)}) collective-permute-start(bf16[128,576]{1,0:T(8,128)(2,1)} %get-tuple-element.11), channel_id=1, source_target_pairs={{0,8},{8,0},{16,24},{24,16},{1,9},{9,1},{17,25},{25,17},{2,10},{10... | collective-permute-start | bytes 442376 | tf_op jit(solution)/shard_map/ppermute | solution.py:159
  29.0 5.0 %collective-permute-done.1 = bf16[2,352,128]{2,1,0:T(8,128)(2,1)S(1)} collective-permute-done((bf16[2,352,128]{2,1,0:T(8,128)(2,1)S(1)}, bf16[2,352,128]{2,1,0:T(8,128)(2,1)S(1)}, u32[]{:S(2)}, u32[]{:S(2)}) %collective-permute-start.1) | collective-permute-done | bytes 180256 | tf_op jit(solution)/shard_map/ppermute | solution.py:159
  34.1 2.5 %collective-permute-start.2 = (bf16[4,352,128]{2,1,0:T(8,128)(2,1)S(1)}, bf16[4,352,128]{2,1,0:T(8,128)(2,1)S(1)}, u32[]{:S(2)}, u32[]{:S(2)}) collective-permute-start(bf16[4,352,128]{2,1,0:T(8,128)(2,1)S(1)} %pad_maximum_fusion.1), channel_id=1, source_target_pairs={{0,64},{64,0},{128,192},{192,128},{256,320},{320,256},{384,448},{4... | collective-permute-start | bytes 1081352 | tf_op jit(solution)/shard_map/ppermute | solution.py:159
  36.6 4.7 %collective-permute-start.6 = (bf16[128,576]{1,0:T(8,128)(2,1)}, bf16[128,576]{1,0:T(8,128)(2,1)S(1)}, u32[]{:S(2)}, u32[]{:S(2)}) collective-permute-start(bf16[128,576]{1,0:T(8,128)(2,1)} %get-tuple-element.11), channel_id=1, source_target_pairs={{0,16},{8,24},{16,0},{24,8},{1,17},{9,25},{17,1},{25,9},{2,18},{10... | collective-permute-start | bytes 442376 | tf_op jit(solution)/shard_map/ppermute | solution.py:159
  41.3 0.0 copy-done.2
  41.3 0.0 copy-done.3
  41.3 2.8 %collective-permute-start.7 = (bf16[128,576]{1,0:T(8,128)(2,1)}, bf16[128,576]{1,0:T(8,128)(2,1)S(1)}, u32[]{:S(2)}, u32[]{:S(2)}) collective-permute-start(bf16[128,576]{1,0:T(8,128)(2,1)} %get-tuple-element.11), channel_id=1, source_target_pairs={{0,24},{8,16},{16,8},{24,0},{1,25},{9,17},{17,9},{25,1},{2,26},{10... | collective-permute-start | bytes 442376 | tf_op jit(solution)/shard_map/ppermute | solution.py:159
  44.1 0.0 collective-permute-done.5
  44.1 1.0 collective-permute-done.6
  45.2 0.0 collective-permute-done.2
  45.2 0.9 pad_maximum_fusion
  46.2 3.6 %collective-permute-start.3 = (bf16[8,352,128]{2,1,0:T(8,128)(2,1)}, bf16[8,352,128]{2,1,0:T(8,128)(2,1)}, u32[]{:S(2)}, u32[]{:S(2)}) collective-permute-start(bf16[8,352,128]{2,1,0:T(8,128)(2,1)} %pad_maximum_fusion), channel_id=1, source_target_pairs={{0,32},{32,0},{1,33},{33,1},{2,34},{34,2},{3,35},{35,3},{4,36},{36... | collective-permute-start | bytes 2162696 | tf_op jit(solution)/shard_map/ppermute | solution.py:159
  49.7 0.0 collective-permute-done.7
  49.8 0.2 copy.9
  50.0 3.2 %collective-permute-start.8 = (bf16[512,576]{0,1:T(8,128)(2,1)S(1)}, bf16[512,576]{0,1:T(8,128)(2,1)}, u32[]{:S(2)}, u32[]{:S(2)}) collective-permute-start(bf16[512,576]{0,1:T(8,128)(2,1)S(1)} %copy.9), channel_id=1, source_target_pairs={{0,2},{2,0},{4,6},{6,4},{1,3},{3,1},{5,7},{7,5},{8,10},{10,8},{12,... | collective-permute-start | bytes 1769480 | tf_op jit(solution)/shard_map/ppermute | solution.py:159
  53.2 4.5 %collective-permute-start.9 = (bf16[512,576]{0,1:T(8,128)(2,1)S(1)}, bf16[512,576]{0,1:T(8,128)(2,1)}, u32[]{:S(2)}, u32[]{:S(2)}) collective-permute-start(bf16[512,576]{0,1:T(8,128)(2,1)S(1)} %copy.9), channel_id=1, source_target_pairs={{0,4},{2,6},{4,0},{6,2},{1,5},{3,7},{5,1},{7,3},{8,12},{10,14},{12... | collective-permute-start | bytes 1769480 | tf_op jit(solution)/shard_map/ppermute | solution.py:159
  57.8 1.9 %collective-permute-start.10 = (bf16[512,576]{0,1:T(8,128)(2,1)S(1)}, bf16[512,576]{0,1:T(8,128)(2,1)}, u32[]{:S(2)}, u32[]{:S(2)}) collective-permute-start(bf16[512,576]{0,1:T(8,128)(2,1)S(1)} %copy.9), channel_id=1, source_target_pairs={{0,6},{2,4},{4,2},{6,0},{1,7},{3,5},{5,3},{7,1},{8,14},{10,12},{12... | collective-permute-start | bytes 1769480 | tf_op jit(solution)/shard_map/ppermute | solution.py:159
  59.7 0.1 pad_add_fusion.place
  60.4 0.1 and_add_fusion.kpos
  60.6 0.0 copy-start
  60.6 1.1 copy-done
  61.7 3.6 %collective-permute-done.8 = bf16[512,576]{0,1:T(8,128)(2,1)} collective-permute-done((bf16[512,576]{0,1:T(8,128)(2,1)S(1)}, bf16[512,576]{0,1:T(8,128)(2,1)}, u32[]{:S(2)}, u32[]{:S(2)}) %collective-permute-start.8) | collective-permute-done | bytes 589856 | tf_op jit(solution)/shard_map/ppermute | solution.py:159
  65.3 1.4 %copy.12.c1 = bf16[512,576]{1,0:T(8,128)(2,1)S(1)} copy(bf16[512,576]{0,1:T(8,128)(2,1)} %collective-permute-done.8) | data formatting | bytes 1179648 | tf_op jit(solution)/shard_map/ppermute | solution.py:159
  66.7 13.8 %collective-permute-done.9 = bf16[512,576]{0,1:T(8,128)(2,1)} collective-permute-done((bf16[512,576]{0,1:T(8,128)(2,1)S(1)}, bf16[512,576]{0,1:T(8,128)(2,1)}, u32[]{:S(2)}, u32[]{:S(2)}) %collective-permute-start.9) | collective-permute-done | bytes 589856 | tf_op jit(solution)/shard_map/ppermute | solution.py:159
  80.5 1.4 %copy.13.c2 = bf16[512,576]{1,0:T(8,128)(2,1)S(1)} copy(bf16[512,576]{0,1:T(8,128)(2,1)} %collective-permute-done.9) | data formatting | bytes 1179648 | tf_op jit(solution)/shard_map/ppermute | solution.py:159
  81.8 4.5 %collective-permute-done.10 = bf16[512,576]{0,1:T(8,128)(2,1)} collective-permute-done((bf16[512,576]{0,1:T(8,128)(2,1)S(1)}, bf16[512,576]{0,1:T(8,128)(2,1)}, u32[]{:S(2)}, u32[]{:S(2)}) %collective-permute-start.10) | collective-permute-done | bytes 589856 | tf_op jit(solution)/shard_map/ppermute | solution.py:159
  86.4 1.4 %copy.14.c3 = bf16[512,576]{1,0:T(8,128)(2,1)S(1)} copy(bf16[512,576]{0,1:T(8,128)(2,1)} %collective-permute-done.10) | data formatting | bytes 1179648 | tf_op jit(solution)/shard_map/ppermute | solution.py:159
  87.7 0.0 collective-permute-done.3
  87.7 2.0 %constant_dynamic-update-slice_fusion.pack = bf16[16,352,128]{2,1,0:T(8,128)(2,1)} fusion(bf16[16,352,128]{2,1,0:T(8,128)(2,1)} %copy-done, bf16[8,352,128]{2,1,0:T(8,128)(2,1)} %collective-permute-done.3), kind=kLoop, calls=%fused_computation.6 | loop fusion | bytes 1441792 | tf_op jit(solution)/shard_map/concatenate | solution.py:189
  89.8 0.0 copy-start.1
  89.8 1.4 %copy-done.1 = bf16[16,352,128]{2,1,0:T(8,128)(2,1)S(1)} copy-done((bf16[16,352,128]{2,1,0:T(8,128)(2,1)S(1)}, bf16[16,352,128]{2,1,0:T(8,128)(2,1)}, u32[]{:S(2)}) %copy-start.1) | copy-done | bytes 1441816
  91.1 1.0 query.1
  92.2 7.9 %attention.1 = bf16[2,8,5,16,128]{4,3,2,1,0:T(8,128)(2,1)S(1)} custom-call(s32[1]{0:T(128)S(6)} %copy.24.prior, s32[1,2048]{1,0:T(1,128)S(1)} %and_add_fusion.kpos, bf16[4,256,576]{2,1,0:T(8,128)(2,1)S(1)} %get-tuple-element.7.q, bf16[512,576]{1,0:T(8,128)(2,1)S(1)} %constant_dynamic-update-slice_fusion.7.c0, bf16[512,576]{1,0:T(8,128)(2,1)S(1)} %copy.12.c1, ...), custom_call_target="tpu_custom_call" | custom-call | tf_op jit(solution)/shard_map/attention/pallas_call | solution.py:213
  100.1 4.9 %collective-permute-start.11 = (bf16[8,5,16,128]{3,2,1,0:T(8,128)(2,1)S(1)}, bf16[8,5,16,128]{3,2,1,0:T(8,128)(2,1)S(1)}, u32[]{:S(2)}, u32[]{:S(2)}) collective-permute-start(bf16[8,5,16,128]{3,2,1,0:T(8,128)(2,1)S(1)} %get-tuple-element.9), channel_id=1, source_target_pairs={{0,32},{32,0},{1,33},{33,1},{2,34},{34,2},{3,35},{35,3},{4,36},{36... | collective-permute-start | bytes 491528 | tf_op jit(solution)/shard_map/ppermute | solution.py:159
  105.0 1.0 collective-permute-done.11.b
  106.0 1.2 pair.1
  107.2 17.2 %all_to_all.5.x = bf16[8,5,16,128]{3,2,1,0:T(8,128)(2,1)S(1)} all-to-all(bf16[8,5,16,128]{3,2,1,0:T(8,128)(2,1)S(1)} %pair.1), channel_id=1, replica_groups=mesh['zl'=8,'co'=2,'x'=4,'y'=4,'zh'=2] {'zl'}, dimensions={0} | all-to-all | bytes 327680 | tf_op jit(solution)/shard_map/all_to_all | solution.py:228
  124.4 0.9 final.1
  (11 shorter events, 0.3 us)
Async XLA Ops:
  0.0 41.3 %copy-start.2 = (bf16[4,128,32]{1,2,0:T(8,128)(2,1)S(1)}, bf16[4,128,32]{1,2,0:T(8,128)(2,1)}, u32[]{:S(2)}) copy-start(bf16[4,128,32]{1,2,0:T(8,128)(2,1)} %param.8) | copy-start | bytes 98308
  0.8 40.5 %copy-start.3 = (bf16[4,128,32]{1,2,0:T(8,128)(2,1)S(1)}, bf16[4,128,32]{1,2,0:T(8,128)(2,1)}, u32[]{:S(2)}) copy-start(bf16[4,128,32]{1,2,0:T(8,128)(2,1)} %param.7) | copy-start | bytes 98308
  1.6 17.1 %collective-permute-start = (bf16[1,352,128]{2,1,0:T(8,128)(2,1)S(1)}, bf16[1,352,128]{2,1,0:T(8,128)(2,1)S(1)}, u32[]{:S(2)}, u32[]{:S(2)}) collective-permute-start(bf16[1,352,128]{2,1,0:T(8,128)(2,1)S(1)} %maximum_bitcast_fusion), channel_id=1, source_target_pairs={{0,256},{64,320},{128,384},{192,448},{256,0},{320,64},{384,128},{4... | collective-permute-start | bytes 270344 | tf_op jit(solution)/shard_map/ppermute | solution.py:159
  11.3 14.0 %collective-permute-start.4 = (bf16[64,576]{1,0:T(8,128)(2,1)}, bf16[64,576]{1,0:T(8,128)(2,1)S(1)}, u32[]{:S(2)}, u32[]{:S(2)}) collective-permute-start(bf16[64,576]{1,0:T(8,128)(2,1)} %param.6), channel_id=1, source_target_pairs={{0,449},{1,448},{64,385},{65,384},{128,321},{129,320},{192,257},{1... | collective-permute-start | bytes 221192 | tf_op jit(solution)/shard_map/ppermute | solution.py:186
  18.8 15.2 %collective-permute-start.1 = (bf16[2,352,128]{2,1,0:T(8,128)(2,1)S(1)}, bf16[2,352,128]{2,1,0:T(8,128)(2,1)S(1)}, u32[]{:S(2)}, u32[]{:S(2)}) collective-permute-start(bf16[2,352,128]{2,1,0:T(8,128)(2,1)S(1)} %pad_maximum_fusion.2), channel_id=1, source_target_pairs={{0,128},{64,192},{128,0},{192,64},{256,384},{320,448},{384,256},{4... | collective-permute-start | bytes 540680 | tf_op jit(solution)/shard_map/ppermute | solution.py:159
  25.9 18.2 %collective-permute-start.5 = (bf16[128,576]{1,0:T(8,128)(2,1)}, bf16[128,576]{1,0:T(8,128)(2,1)S(1)}, u32[]{:S(2)}, u32[]{:S(2)}) collective-permute-start(bf16[128,576]{1,0:T(8,128)(2,1)} %get-tuple-element.11), channel_id=1, source_target_pairs={{0,8},{8,0},{16,24},{24,16},{1,9},{9,1},{17,25},{25,17},{2,10},{10... | collective-permute-start | bytes 442376 | tf_op jit(solution)/shard_map/ppermute | solution.py:159
  34.1 11.1 %collective-permute-start.2 = (bf16[4,352,128]{2,1,0:T(8,128)(2,1)S(1)}, bf16[4,352,128]{2,1,0:T(8,128)(2,1)S(1)}, u32[]{:S(2)}, u32[]{:S(2)}) collective-permute-start(bf16[4,352,128]{2,1,0:T(8,128)(2,1)S(1)} %pad_maximum_fusion.1), channel_id=1, source_target_pairs={{0,64},{64,0},{128,192},{192,128},{256,320},{320,256},{384,448},{4... | collective-permute-start | bytes 1081352 | tf_op jit(solution)/shard_map/ppermute | solution.py:159
  36.6 8.6 %collective-permute-start.6 = (bf16[128,576]{1,0:T(8,128)(2,1)}, bf16[128,576]{1,0:T(8,128)(2,1)S(1)}, u32[]{:S(2)}, u32[]{:S(2)}) collective-permute-start(bf16[128,576]{1,0:T(8,128)(2,1)} %get-tuple-element.11), channel_id=1, source_target_pairs={{0,16},{8,24},{16,0},{24,8},{1,17},{9,25},{17,1},{25,9},{2,18},{10... | collective-permute-start | bytes 442376 | tf_op jit(solution)/shard_map/ppermute | solution.py:159
  41.3 8.4 %collective-permute-start.7 = (bf16[128,576]{1,0:T(8,128)(2,1)}, bf16[128,576]{1,0:T(8,128)(2,1)S(1)}, u32[]{:S(2)}, u32[]{:S(2)}) collective-permute-start(bf16[128,576]{1,0:T(8,128)(2,1)} %get-tuple-element.11), channel_id=1, source_target_pairs={{0,24},{8,16},{16,8},{24,0},{1,25},{9,17},{17,9},{25,1},{2,26},{10... | collective-permute-start | bytes 442376 | tf_op jit(solution)/shard_map/ppermute | solution.py:159
  46.2 41.6 %collective-permute-start.3 = (bf16[8,352,128]{2,1,0:T(8,128)(2,1)}, bf16[8,352,128]{2,1,0:T(8,128)(2,1)}, u32[]{:S(2)}, u32[]{:S(2)}) collective-permute-start(bf16[8,352,128]{2,1,0:T(8,128)(2,1)} %pad_maximum_fusion), channel_id=1, source_target_pairs={{0,32},{32,0},{1,33},{33,1},{2,34},{34,2},{3,35},{35,3},{4,36},{36... | collective-permute-start | bytes 2162696 | tf_op jit(solution)/shard_map/ppermute | solution.py:159
  50.0 15.3 %collective-permute-start.8 = (bf16[512,576]{0,1:T(8,128)(2,1)S(1)}, bf16[512,576]{0,1:T(8,128)(2,1)}, u32[]{:S(2)}, u32[]{:S(2)}) collective-permute-start(bf16[512,576]{0,1:T(8,128)(2,1)S(1)} %copy.9), channel_id=1, source_target_pairs={{0,2},{2,0},{4,6},{6,4},{1,3},{3,1},{5,7},{7,5},{8,10},{10,8},{12,... | collective-permute-start | bytes 1769480 | tf_op jit(solution)/shard_map/ppermute | solution.py:159
  53.2 27.2 %collective-permute-start.9 = (bf16[512,576]{0,1:T(8,128)(2,1)S(1)}, bf16[512,576]{0,1:T(8,128)(2,1)}, u32[]{:S(2)}, u32[]{:S(2)}) collective-permute-start(bf16[512,576]{0,1:T(8,128)(2,1)S(1)} %copy.9), channel_id=1, source_target_pairs={{0,4},{2,6},{4,0},{6,2},{1,5},{3,7},{5,1},{7,3},{8,12},{10,14},{12... | collective-permute-start | bytes 1769480 | tf_op jit(solution)/shard_map/ppermute | solution.py:159
  57.8 28.6 %collective-permute-start.10 = (bf16[512,576]{0,1:T(8,128)(2,1)S(1)}, bf16[512,576]{0,1:T(8,128)(2,1)}, u32[]{:S(2)}, u32[]{:S(2)}) collective-permute-start(bf16[512,576]{0,1:T(8,128)(2,1)S(1)} %copy.9), channel_id=1, source_target_pairs={{0,6},{2,4},{4,2},{6,0},{1,7},{3,5},{5,3},{7,1},{8,14},{10,12},{12... | collective-permute-start | bytes 1769480 | tf_op jit(solution)/shard_map/ppermute | solution.py:159
  60.6 1.1 copy-start
  89.8 1.4 %copy-start.1 = (bf16[16,352,128]{2,1,0:T(8,128)(2,1)S(1)}, bf16[16,352,128]{2,1,0:T(8,128)(2,1)}, u32[]{:S(2)}) copy-start(bf16[16,352,128]{2,1,0:T(8,128)(2,1)} %constant_dynamic-update-slice_fusion.pack) | copy-start | bytes 4325380
  100.1 5.9 %collective-permute-start.11 = (bf16[8,5,16,128]{3,2,1,0:T(8,128)(2,1)S(1)}, bf16[8,5,16,128]{3,2,1,0:T(8,128)(2,1)S(1)}, u32[]{:S(2)}, u32[]{:S(2)}) collective-permute-start(bf16[8,5,16,128]{3,2,1,0:T(8,128)(2,1)S(1)} %get-tuple-element.9), channel_id=1, source_target_pairs={{0,32},{32,0},{1,33},{33,1},{2,34},{34,2},{3,35},{35,3},{4,36},{36... | collective-permute-start | bytes 491528 | tf_op jit(solution)/shard_map/ppermute | solution.py:159

commit v2 on v0

v2 whole, which is shorter than its diff:
```python
import math

import jax
import jax.numpy as jnp
from jax import lax
from jax.experimental import pallas as pl
from jax.experimental.pallas import tpu as pltpu
from jax.sharding import Mesh
from jax.sharding import PartitionSpec as P

PLAIN = 128
ROT = 64
LATENT = 512
VALUE = 128
HEADS = 4
WIDE = LATENT + 2 * ROT
TOK = 16
ROWS = 256
NEG = -1e30
LOG2_SCALE = (PLAIN + ROT) ** (-0.5) * math.log2(math.e)
VMEM_LIMIT = 40 * 1024 * 1024

CTX = ("zl", "co")
f32 = jnp.float32
bf16 = jnp.bfloat16


def vmem():
    return pl.BlockSpec(memory_space=pltpu.VMEM)


def call(kernel, shape, n_in, name, scratch=()):
    return pl.pallas_call(
        kernel,
        out_shape=shape,
        in_specs=[pl.BlockSpec(memory_space=pltpu.SMEM)] + [vmem()] * n_in,
        out_specs=jax.tree.map(lambda _: vmem(), shape),
        scratch_shapes=list(scratch),
        compiler_params=pltpu.CompilerParams(vmem_limit_bytes=VMEM_LIMIT),
        cost_estimate=pl.CostEstimate(flops=1, transcendentals=0, bytes_accessed=1),
        name=name,
    )


def shaped(shape, dtype=bf16):
    return jax.ShapeDtypeStruct(shape, dtype)


def prepare_kernel(queries_hbm, cache_hbm, wk_hbm, wv_hbm, shard, pack, queries, cache, sems):
    copies = [
        pltpu.make_async_copy(src, dst, sems.at[i])
        for i, (src, dst) in enumerate(
            (
                (cache_hbm, cache),
                (queries_hbm, queries),
                (wk_hbm, pack.at[0, 96:224, :]),
                (wv_hbm, pack.at[0, 224:352, :]),
            )
        )
    ]
    for c in copies:
        c.start()
    copies[0].wait()
    shard[0, :64, :] = cache[:, :LATENT]
    rot = cache[:, LATENT:]
    pairs = jnp.concatenate([rot[:32], rot[32:]], axis=1)
    for k in range(4):
        shard[0, 64:72, 128 * k : 128 * (k + 1)] = pairs[8 * k : 8 * (k + 1)]
    copies[1].wait()
    for k in range(6):
        pack[0, TOK * k : TOK * (k + 1), :] = queries[:, 128 * k : 128 * (k + 1)]
    copies[2].wait()
    copies[3].wait()


def prepare(queries, cache, wk, wv):
    return pl.pallas_call(
        prepare_kernel,
        out_shape=(shaped((1, 72, LATENT)), shaped((1, 352, 128))),
        in_specs=[pl.BlockSpec(memory_space=pltpu.HBM)] * 4,
        out_specs=(vmem(), vmem()),
        scratch_shapes=[
            pltpu.VMEM(queries.shape, bf16),
            pltpu.VMEM(cache.shape, bf16),
            pltpu.SemaphoreType.DMA((4,)),
        ],
        compiler_params=pltpu.CompilerParams(vmem_limit_bytes=VMEM_LIMIT),
        name="prepare",
    )(queries, cache, wk, wv)


def query_kernel(place, p0, p1, p2, p3, p4, q_out, wv_out, pieces, panel, values):
    me = place[0]
    sources = [
        (ref, i, lax.bitwise_xor(me, flip))
        for ref, flips in (
            (p0, (0,)),
            (p1, (8,)),
            (p2, (4, 12)),
            (p3, (2, 10, 6, 14)),
            (p4, (1, 9, 5, 13, 3, 11, 7, 15)),
        )
        for i, flip in enumerate(flips)
    ]
    for ref, i, src in sources:
        for k in range(6):
            pieces[k, src] = ref[i, TOK * k : TOK * (k + 1), :]
        for h in range(HEADS):
            panel[h, src] = ref[i, 96 + 32 * h : 128 + 32 * h, :]
            values[h, src] = ref[i, 224 + 32 * h : 256 + 32 * h, :]
    zero = jnp.zeros((ROWS, ROT), bf16)
    for h in range(HEADS):
        wv_out[h] = values[h].reshape(LATENT, VALUE)
        k = (h // 2) * 3
        tile = [pieces[k + n].reshape(ROWS, 128) for n in range(3)]
        if h % 2 == 0:
            plain, rot = tile[0], tile[1][:, :ROT]
        else:
            plain = jnp.concatenate([tile[1][:, ROT:], tile[2][:, :ROT]], axis=1)
            rot = tile[2][:, ROT:]
        lat = lax.dot_general(
            plain,
            panel[h].reshape(LATENT, PLAIN),
            (((1,), (1,)), ((), ())),
            preferred_element_type=f32,
        ).astype(bf16)
        for half in range(2):
            q_out[half, h, :, :LATENT] = lat
        q_out[0, h, :, LATENT:] = jnp.concatenate([rot, zero], axis=1)
        q_out[1, h, :, LATENT:] = jnp.concatenate([zero, rot], axis=1)


def split3(x):
    hi = x.astype(bf16)
    r = x - hi.astype(f32)
    mid = r.astype(bf16)
    lo = (r - mid.astype(f32)).astype(bf16)
    return hi, mid, lo


def pack_lse(columns, shape):
    lane = lax.broadcasted_iota(jnp.int32, shape, len(shape) - 1)
    tile = jnp.zeros(shape, f32)
    for h, column in enumerate(columns):
        for p, part in enumerate(split3(column)):
            tile = jnp.where(lane == 3 * h + p, part.astype(f32), tile)
    return tile.astype(bf16)


def lse_column(tile, h):
    t = tile.astype(f32)
    k = 3 * h
    return t[:, k : k + 1] + t[:, k + 1 : k + 2] + t[:, k + 2 : k + 3]


def attention_kernel(count, arrays, first, last, *refs):
    refs = list(refs)
    place, kpos, q = refs[:3]
    chunks = refs[3 : 3 + arrays]
    del refs[: 3 + arrays]
    if not first:
        acc_in, peak_in, total_in = refs[:3]
        del refs[:3]
    if last:
        wv = refs.pop(0)
        outs, (keys, parts) = refs[:4], refs[4:]
    else:
        acc_out, peak_out, total_out, keys = refs
    me, prior = place[0], place[1]

    for n, c in enumerate(chunks):
        shards = c.shape[0]
        start = n * 4 * 32 if shards == 4 else 0
        j = 0 if shards == 4 else n
        for half in range(2):
            keys[j, half, start : start + 32 * shards, :LATENT] = c[
                :, 32 * half : 32 * half + 32, :
            ].reshape(32 * shards, LATENT)
            for g in range(shards):
                for k in range(4):
                    at = start + 32 * g + 8 * k
                    keys[j, half, at : at + 8, LATENT:] = c[g, 64:72, 128 * k : 128 * (k + 1)]

    limit = prior + lax.broadcasted_iota(jnp.int32, (ROWS, 1), 0)
    blocks = [(j, half) for j in range(count) for half in range(2)]
    lses = []
    for h in range(HEADS):
        scores = []
        for n, (j, half) in enumerate(blocks):
            s = lax.dot_general(
                q[half, h], keys[j, half], (((1,), (1,)), ((), ())), preferred_element_type=f32
            )
            seen = kpos[:, 256 * n : 256 * (n + 1)] <= limit
            scores.append(jnp.where(seen, s * LOG2_SCALE, NEG))
        peak = scores[0].max(axis=1, keepdims=True)
        for s in scores[1:]:
            peak = jnp.maximum(peak, s.max(axis=1, keepdims=True))
        if first:
            total = jnp.zeros((ROWS, 1), f32)
            acc = jnp.zeros((ROWS, LATENT), f32)
        else:
            old = peak_in[h][:, :1]
            peak = jnp.maximum(peak, old)
            fade = jnp.exp2(old - peak)
            total = total_in[h][:, :1] * fade
            acc = acc_in[h] * fade
        for s, (j, half) in zip(scores, blocks):
            p = jnp.exp2(s - peak)
            total = total + p.sum(axis=1, keepdims=True)
            acc = acc + jnp.dot(
                p.astype(bf16), keys[j, half, :, :LATENT], preferred_element_type=f32
            )
        if not last:
            acc_out[h] = acc
            peak_out[h] = jnp.broadcast_to(peak, (ROWS, 128))
            total_out[h] = jnp.broadcast_to(total, (ROWS, 128))
            continue
        latent = (acc / total).astype(bf16)
        o = jnp.dot(latent, wv[h], preferred_element_type=f32).astype(bf16)
        for g in range(16):
            parts[g, h] = o[TOK * g : TOK * (g + 1)]
        lses.append(peak + jnp.log2(total))
    if last:
        tile = pack_lse(lses, (ROWS, 128))
        for g in range(16):
            parts[g, HEADS] = tile[TOK * g : TOK * (g + 1)]
        low = lax.bitwise_and(me, 3)
        for d in range(4):
            for high in range(4):
                outs[d][high] = parts[high * 4 + lax.bitwise_xor(low, d)]


def merge_heads(tiles):
    values, lses = [], []
    for h in range(HEADS):
        columns = [lse_column(t[HEADS], h) for t in tiles]
        top = columns[0]
        for c in columns[1:]:
            top = jnp.maximum(top, c)
        acc = jnp.zeros((TOK, VALUE), f32)
        total = jnp.zeros((TOK, 1), f32)
        for t, c in zip(tiles, columns):
            w = jnp.exp2(c - top)
            total = total + w
            acc = acc + t[h].astype(f32) * w
        values.append(acc / total)
        lses.append(top + jnp.log2(total))
    return values, lses


def middle_kernel(place, a, b, c, d, *outs):
    high = lax.shift_right_logical(place[0], 2)
    for j, out in enumerate(outs):
        g = lax.bitwise_xor(high, j)
        values, lses = merge_heads([r[g] for r in (a, b, c, d)])
        for h in range(HEADS):
            out[h] = values[h].astype(bf16)
        out[HEADS] = pack_lse(lses, (TOK, 128))


def final_kernel(place, a, b, c, d, out):
    values, _ = merge_heads([r[...] for r in (a, b, c, d)])
    for h in range(HEADS):
        out[:, h * VALUE : (h + 1) * VALUE] = values[h].astype(bf16)


def swap(x, axis, n, d):
    return lax.ppermute(x, axis, [(i, i ^ d) for i in range(n)])


def per_device(queries, cache, key_up_weight, value_up_weight, prior_len):
    zl, co = lax.axis_index("zl"), lax.axis_index("co")
    x, y, zh = lax.axis_index("x"), lax.axis_index("y"), lax.axis_index("zh")
    place = jnp.concatenate([(zl * 2 + co).astype(jnp.int32)[None], prior_len])

    shard, pack = prepare(
        queries,
        cache,
        key_up_weight.transpose(0, 2, 1).reshape(128, 128),
        value_up_weight.transpose(0, 2, 1).reshape(128, 128),
    )

    pieces = [pack]

    def widen(pack, d):
        got = swap(pack, CTX, 16, d)
        pieces.append(got)
        return jnp.concatenate([pack, got], axis=0)

    mirror = lax.ppermute(shard, ("zl", "zh"), [(i, 15 - i) for i in range(16)])
    pack = widen(pack, 8)
    mirror, pack = lax.optimization_barrier((mirror, pack))
    pair = jnp.concatenate([shard, mirror], axis=0)
    quad = jnp.concatenate([pair] + [swap(pair, "x", 4, d) for d in (1, 2, 3)], axis=0)
    pack = widen(pack, 4)
    quad, pack = lax.optimization_barrier((quad, pack))
    near, back = swap(quad, "y", 4, 1), swap(quad, "y", 4, 3)
    pack = widen(pack, 2)
    near, back, pack = lax.optimization_barrier((near, back, pack))
    far = (swap(near[:4], "y", 4, 3), swap(back[4:], "y", 4, 1))
    pieces.append(swap(pack, CTX, 16, 1))

    q, wv = call(
        query_kernel,
        (shaped((2, HEADS, ROWS, WIDE)), shaped((HEADS, LATENT, VALUE))),
        5,
        "query",
        (
            pltpu.VMEM((6, 16, TOK, 128), bf16),
            pltpu.VMEM((HEADS, 16, 32, 128), bf16),
            pltpu.VMEM((HEADS, 16, 32, 128), bf16),
        ),
    )(place, *pieces)

    n = jnp.arange(2048, dtype=jnp.int32)
    dy, half, dx, m, i = n >> 9, (n >> 8) & 1, (n >> 6) & 3, (n >> 5) & 1, n & 31
    dy = jnp.where(dy < 2, dy, 5 - dy)
    src_z, src_h = jnp.where(m == 1, 7 - zl, zl), jnp.where(m == 1, 1 - zh, zh)
    head = ((x ^ dx) * 4 + (y ^ dy)) * 2 + src_h
    kpos = (((src_z * 2 + co) * 32 + head) * 64 + half * 32 + i).astype(jnp.int32)[None]

    state = (
        shaped((HEADS, ROWS, LATENT), f32),
        shaped((HEADS, ROWS, 128), f32),
        shaped((HEADS, ROWS, 128), f32),
    )

    def attend(count, arrays, first, last, *operands):
        def kernel(*refs):
            attention_kernel(count, arrays, first, last, *refs)

        shape = state if not last else tuple(shaped((4, HEADS + 1, TOK, 128)) for _ in range(4))
        scratch = [pltpu.VMEM((count, 2, 256, WIDE), bf16)]
        if last:
            scratch.append(pltpu.VMEM((16, HEADS + 1, TOK, 128), bf16))
        return call(kernel, shape, len(operands) - 1, f"attend{count}{int(last)}", scratch)(*operands)

    run = attend(1, 1, True, False, place, kpos[:, :512], q, quad)
    run = attend(2, 2, False, False, place, kpos[:, 512:1536], q, near, back, *run)
    parts = attend(1, 2, False, True, place, kpos[:, 1536:], q, *far, *run, wv)

    got = [parts[0]] + [swap(parts[d], CTX, 16, d) for d in (1, 2, 3)]
    parts = call(middle_kernel, tuple(shaped((HEADS + 1, TOK, 128)) for _ in range(4)), 4, "middle")(place, *got)
    got = [parts[0]] + [swap(parts[d], CTX, 16, 4 * d) for d in (1, 2, 3)]
    return call(final_kernel, shaped((TOK, HEADS * VALUE)), 4, "final")(place, *got)


def solution(mesh):
    fine = Mesh(mesh.devices.reshape(8, 2, 4, 4, 2), ("zl", "co", "x", "y", "zh"))
    head = ("x", "y", "zh")
    return jax.shard_map(
        per_device,
        mesh=fine,
        in_specs=(P(CTX, head), P(CTX + head, None), P(head, None, CTX), P(head, None, CTX), P()),
        out_specs=P(CTX, head),
        check_vma=False,
    )
```

time: 424 us -> 124 us (0.29); the launches traced: 417 us -> 122 us
  waiting for transfers between devices: 231 us -> 24.3 us
  blocking collectives: 145 us -> 0 us
  starting transfers between devices: 0.08 us -> 76.8 us
  Pallas kernels: 0 us -> 15.8 us
  matrix products: 15.6 us -> 0 us
  between operations: 13.9 us -> 0.96 us
    reduce_scatter x1 -> x0, waiting for transfers between devices: 102 us -> none  [per_device(): lax.psum_scatter(latent_scaled.astype(jnp.bfloat16), 'ctx', scatter_dimen...]
    all_gather x3 -> x0, blocking collectives: 96.6 us -> none  [the longest x1 39.6 us: per_device(): gathered = lax.all_gather(queries, 'ctx', axis=0, tiled=True)]
    ppermute x0 -> x18, starting transfers between devices: none -> 76.8 us  [the longest x17 69.3 us: swap(): return lax.ppermute(x, axis, [(i, i ^ d) for i in range(n)])]
    all_gather x1 -> x0, waiting for transfers between devices: 76.1 us -> none  [per_device(): key_section = lax.all_gather(cache, 'head', axis=0, tiled=True)]
    unnamed x4 -> x0, waiting for transfers between devices: 52.8 us -> none
    pmax x1 -> x0, blocking collectives: 48.9 us -> none  [per_device(): global_peak = lax.pmax(row_peak, 'ctx')]
    ppermute x0 -> x18, waiting for transfers between devices: none -> 24.3 us  [the longest x17 18.9 us: swap(): return lax.ppermute(x, axis, [(i, i ^ d) for i in range(n)])]
    pallas_call x0 -> x7, Pallas kernels: none -> 15.8 us  [the longest x3 11.8 us: attend(): call(kernel, shape, len(operands) - 1, f'attend{count}{int(last)}', scratch)]
  transfers between devices with their start and end apart: 3 -> 18, of which waited for: 3 -> 8; matrix products, arithmetic and copies ran while one was open for 3% -> 1% of each run, Pallas kernels for 0% -> 7%
where the time goes in v2:
time: 124 us; the launch traced here: 122 us
  starting transfers between devices  76.8 us (62%)
  waiting for transfers between devices  24.3 us (20%)
  Pallas kernels  15.8 us (13%)
  local copies, waits for them, and re-layouts  3.24 us (3%)
    ppermute x17, starting transfers between devices, swap(): return lax.ppermute(x, axis, [(i, i ^ d) for i in range(n)])  69.3 us
    ppermute x17, waiting for transfers between devices, swap(): return lax.ppermute(x, axis, [(i, i ^ d) for i in range(n)])  18.9 us
    pallas_call x3, Pallas kernels, attend(): call(kernel, shape, len(operands) - 1, f'attend{count}{int(last)}', scratch)  11.8 us
    ppermute x1, starting transfers between devices, per_device(): mirror = lax.ppermute(shard, ('zl', 'zh'), [(i, 15 - i) for i in range(16)])  7.48 us
    ppermute x1, waiting for transfers between devices, per_device(): mirror = lax.ppermute(shard, ('zl', 'zh'), [(i, 15 - i) for i in range(16)])  5.38 us
    unnamed x11, local copies, waits for them, and re-layouts  3.17 us
  transfers between devices with their start and end apart: 18, of which 8 were waited for; matrix products, arithmetic and copies ran while one was open for 1% of the time, Pallas kernels for 7%

profile of v2, /device:TPU:1, one launch (start us, length us, event | category | flops | bytes accessed | tf_op | source)
XLA Modules:
  0.0 122.3 jit_solution(11620441090268321994)
XLA Ops:
  0.0 0.0 copy-start
  0.0 0.9 copy-done
  0.9 0.0 copy-start.1
  0.9 0.8 copy-done.1
  1.6 0.0 copy-start.2
  1.6 0.8 copy-done.2
  2.4 0.0 copy-start.3
  2.4 0.7 copy-done.3
  3.1 0.3 prepare.1
  3.5 9.6 %collective-permute-start = (bf16[1,352,128]{2,1,0:T(8,128)(2,1)S(1)}, bf16[1,352,128]{2,1,0:T(8,128)(2,1)S(1)}, u32[]{:S(2)}, u32[]{:S(2)}) collective-permute-start(bf16[1,352,128]{2,1,0:T(8,128)(2,1)S(1)} %get-tuple-element.30.p0), channel_id=1, source_target_pairs={{0,256},{32,288},{64,320},{96,352},{128,384},{160,416},{192,448},{... | collective-permute-start | bytes 270344 | tf_op jit(solution)/shard_map/ppermute | solution.py:268
  13.1 7.5 %collective-permute-start.1 = (bf16[1,72,512]{2,1,0:T(8,128)(2,1)S(1)}, bf16[1,72,512]{2,1,0:T(8,128)(2,1)S(1)}, u32[]{:S(2)}, u32[]{:S(2)}) collective-permute-start(bf16[1,72,512]{2,1,0:T(8,128)(2,1)S(1)} %get-tuple-element.31), channel_id=1, source_target_pairs={{0,449},{1,448},{64,385},{65,384},{128,321},{129,320},{192,257},{1... | collective-permute-start | bytes 221192 | tf_op jit(solution)/shard_map/ppermute | solution.py:290
  20.6 0.0 collective-permute-done.p1
  20.7 5.4 %collective-permute-done.1 = bf16[1,72,512]{2,1,0:T(8,128)(2,1)S(1)} collective-permute-done((bf16[1,72,512]{2,1,0:T(8,128)(2,1)S(1)}, bf16[1,72,512]{2,1,0:T(8,128)(2,1)S(1)}, u32[]{:S(2)}, u32[]{:S(2)}) %collective-permute-start.1) | collective-permute-done | bytes 73760 | tf_op jit(solution)/shard_map/ppermute | solution.py:290
  26.1 3.1 %collective-permute-start.3 = (bf16[2,72,512]{2,1,0:T(8,128)(2,1)S(1)}, bf16[2,72,512]{2,1,0:T(8,128)(2,1)S(1)}, u32[]{:S(2)}, u32[]{:S(2)}) collective-permute-start(bf16[2,72,512]{2,1,0:T(8,128)(2,1)S(1)} %get-tuple-element.55), channel_id=1, source_target_pairs={{0,8},{8,0},{16,24},{24,16},{1,9},{9,1},{17,25},{25,17},{2,10},{10... | collective-permute-start | bytes 442376 | tf_op jit(solution)/shard_map/ppermute | solution.py:268
  29.2 4.4 %collective-permute-start.4 = (bf16[2,72,512]{2,1,0:T(8,128)(2,1)S(1)}, bf16[2,72,512]{2,1,0:T(8,128)(2,1)S(1)}, u32[]{:S(2)}, u32[]{:S(2)}) collective-permute-start(bf16[2,72,512]{2,1,0:T(8,128)(2,1)S(1)} %get-tuple-element.55), channel_id=1, source_target_pairs={{0,16},{8,24},{16,0},{24,8},{1,17},{9,25},{17,1},{25,9},{2,18},{10... | collective-permute-start | bytes 442376 | tf_op jit(solution)/shard_map/ppermute | solution.py:268
  33.6 2.1 %collective-permute-start.5 = (bf16[2,72,512]{2,1,0:T(8,128)(2,1)S(1)}, bf16[2,72,512]{2,1,0:T(8,128)(2,1)S(1)}, u32[]{:S(2)}, u32[]{:S(2)}) collective-permute-start(bf16[2,72,512]{2,1,0:T(8,128)(2,1)S(1)} %get-tuple-element.55), channel_id=1, source_target_pairs={{0,24},{8,16},{16,8},{24,0},{1,25},{9,17},{17,9},{25,1},{2,26},{10... | collective-permute-start | bytes 442376 | tf_op jit(solution)/shard_map/ppermute | solution.py:268
  35.7 2.0 %collective-permute-start.2 = (bf16[2,352,128]{2,1,0:T(8,128)(2,1)S(1)}, bf16[2,352,128]{2,1,0:T(8,128)(2,1)S(1)}, u32[]{:S(2)}, u32[]{:S(2)}) collective-permute-start(bf16[2,352,128]{2,1,0:T(8,128)(2,1)S(1)} %pad_maximum_fusion.2), channel_id=1, source_target_pairs={{0,128},{32,160},{64,192},{96,224},{128,0},{160,32},{192,64},{224,... | collective-permute-start | bytes 540680 | tf_op jit(solution)/shard_map/ppermute | solution.py:268
  37.7 0.0 collective-permute-done.3
  37.7 0.2 collective-permute-done.4
  37.9 3.4 %collective-permute-done.5 = bf16[2,72,512]{2,1,0:T(8,128)(2,1)S(1)} collective-permute-done((bf16[2,72,512]{2,1,0:T(8,128)(2,1)S(1)}, bf16[2,72,512]{2,1,0:T(8,128)(2,1)S(1)}, u32[]{:S(2)}, u32[]{:S(2)}) %collective-permute-start.5) | collective-permute-done | bytes 147488 | tf_op jit(solution)/shard_map/ppermute | solution.py:268
  41.3 1.8 %collective-permute-done.2.p2 = bf16[2,352,128]{2,1,0:T(8,128)(2,1)S(1)} collective-permute-done((bf16[2,352,128]{2,1,0:T(8,128)(2,1)S(1)}, bf16[2,352,128]{2,1,0:T(8,128)(2,1)S(1)}, u32[]{:S(2)}, u32[]{:S(2)}) %collective-permute-start.2) | collective-permute-done | bytes 180256 | tf_op jit(solution)/shard_map/ppermute | solution.py:268
  43.1 3.2 %collective-permute-start.7 = (bf16[8,72,512]{2,1,0:T(8,128)(2,1)S(1)}, bf16[8,72,512]{2,1,0:T(8,128)(2,1)S(1)}, u32[]{:S(2)}, u32[]{:S(2)}) collective-permute-start(bf16[8,72,512]{2,1,0:T(8,128)(2,1)S(1)} %constant_dynamic-update-slice_fusion.2.refs_3_), channel_id=1, source_target_pairs={{0,2},{2,0},{4,6},{6,4},{1,3},{3,1},{5,7},{7,5},{8,10},{10,8},{12,... | collective-permute-start | bytes 1769480 | tf_op jit(solution)/shard_map/ppermute | solution.py:268
  46.4 3.8 %collective-permute-start.8 = (bf16[8,72,512]{2,1,0:T(8,128)(2,1)S(1)}, bf16[8,72,512]{2,1,0:T(8,128)(2,1)S(1)}, u32[]{:S(2)}, u32[]{:S(2)}) collective-permute-start(bf16[8,72,512]{2,1,0:T(8,128)(2,1)S(1)} %constant_dynamic-update-slice_fusion.2.refs_3_), channel_id=1, source_target_pairs={{0,6},{2,4},{4,2},{6,0},{1,7},{3,5},{5,3},{7,1},{8,14},{10,12},{12... | collective-permute-start | bytes 1769480 | tf_op jit(solution)/shard_map/ppermute | solution.py:268
  50.2 8.1 %collective-permute-start.6 = (bf16[4,352,128]{2,1,0:T(8,128)(2,1)S(1)}, bf16[4,352,128]{2,1,0:T(8,128)(2,1)S(1)}, u32[]{:S(2)}, u32[]{:S(2)}) collective-permute-start(bf16[4,352,128]{2,1,0:T(8,128)(2,1)S(1)} %pad_maximum_fusion.1), channel_id=1, source_target_pairs={{0,64},{32,96},{64,0},{96,32},{128,192},{160,224},{192,128},{224,1... | collective-permute-start | bytes 1081352 | tf_op jit(solution)/shard_map/ppermute | solution.py:268
  58.2 6.1 %collective-permute-done.6.p3 = bf16[4,352,128]{2,1,0:T(8,128)(2,1)S(1)} collective-permute-done((bf16[4,352,128]{2,1,0:T(8,128)(2,1)S(1)}, bf16[4,352,128]{2,1,0:T(8,128)(2,1)S(1)}, u32[]{:S(2)}, u32[]{:S(2)}) %collective-permute-start.6) | collective-permute-done | bytes 360480 | tf_op jit(solution)/shard_map/ppermute | solution.py:268
  64.4 0.9 pad_maximum_fusion
  65.3 0.0 collective-permute-done.7.refs_3_
  65.3 0.0 collective-permute-done.8.refs_4_
  65.3 5.1 %collective-permute-start.9 = (bf16[8,352,128]{2,1,0:T(8,128)(2,1)}, bf16[8,352,128]{2,1,0:T(8,128)(2,1)S(1)}, u32[]{:S(2)}, u32[]{:S(2)}) collective-permute-start(bf16[8,352,128]{2,1,0:T(8,128)(2,1)} %pad_maximum_fusion), channel_id=1, source_target_pairs={{0,32},{32,0},{64,96},{96,64},{128,160},{160,128},{192,224},{224,1... | collective-permute-start | bytes 2162696 | tf_op jit(solution)/shard_map/ppermute | solution.py:268
  71.1 0.1 and_add_fusion
  71.2 2.7 %collective-permute-start.10 = (bf16[4,72,512]{2,1,0:T(8,128)(2,1)S(1)}, bf16[4,72,512]{2,1,0:T(8,128)(2,1)S(1)}, u32[]{:S(2)}, u32[]{:S(2)}) collective-permute-start(bf16[4,72,512]{2,1,0:T(8,128)(2,1)S(1)} %slice.16), channel_id=1, source_target_pairs={{0,6},{2,4},{4,2},{6,0},{1,7},{3,5},{5,3},{7,1},{8,14},{10,12},{12... | collective-permute-start | bytes 884744 | tf_op jit(solution)/shard_map/ppermute | solution.py:268
  73.9 1.9 %collective-permute-start.11 = (bf16[4,72,512]{2,1,0:T(8,128)(2,1)S(1)}, bf16[4,72,512]{2,1,0:T(8,128)(2,1)S(1)}, u32[]{:S(2)}, u32[]{:S(2)}) collective-permute-start(bf16[4,72,512]{2,1,0:T(8,128)(2,1)S(1)} %slice.17), channel_id=1, source_target_pairs={{0,2},{2,0},{4,6},{6,4},{1,3},{3,1},{5,7},{7,5},{8,10},{10,8},{12,... | collective-permute-start | bytes 884744 | tf_op jit(solution)/shard_map/ppermute | solution.py:268
  75.9 0.1 pad_add_fusion.place.refs_0_
  75.9 0.0 collective-permute-done.9.p4
  75.9 1.1 query.1
  77.1 2.8 %attend10.1 = (f32[4,256,512]{2,1,0:T(8,128)S(1)}, f32[4,256,128]{2,1,0:T(8,128)S(1)}, f32[4,256,128]{2,1,0:T(8,128)S(1)}) custom-call(s32[2]{0:T(128)S(1)} %pad_add_fusion.place.refs_0_, s32[1,512]{1,0:T(1,128)S(1)} %get-tuple-element.59.refs_1_, bf16[2,4,256,640]{3,2,1,0:T(8,128)(2,1)S(1)} %get-tuple-element.37.refs_2_, ...), custom_call_target="tpu_custom_call" | custom-call | flops 1 | bytes 1 | tf_op jit(solution)/shard_map/attend10/pallas_call | solution.py:336
  79.9 5.2 %attend20.1 = (f32[4,256,512]{2,1,0:T(8,128)S(1)}, f32[4,256,128]{2,1,0:T(8,128)S(1)}, f32[4,256,128]{2,1,0:T(8,128)S(1)}) custom-call(s32[2]{0:T(128)S(1)} %pad_add_fusion.place.refs_0_, s32[1,1024]{1,0:T(1,128)S(1)} %slice.21.refs_1_, bf16[2,4,256,640]{3,2,1,0:T(8,128)(2,1)S(1)} %get-tuple-element.37.refs_2_, ...), custom_call_target="tpu_custom_call" | custom-call | flops 1 | bytes 1 | tf_op jit(solution)/shard_map/attend20/pallas_call | solution.py:336
  85.1 0.0 collective-permute-done.10.refs_3_
  85.1 0.0 collective-permute-done.11.refs_4_
  85.1 3.8 %attend11.1 = (bf16[4,5,16,128]{3,2,1,0:T(8,128)(2,1)S(1)}, bf16[4,5,16,128]{3,2,1,0:T(8,128)(2,1)S(1)}, bf16[4,5,16,128]{3,2,1,0:T(8,128)(2,1)S(1)}, bf16[4,5,16,128]{3,2,1,0:T(8,128)(2,1)S(1)}) custom-call(s32[2]{0:T(128)S(1)} %pad_add_fusion.place.refs_0_, s32[1,512]{1,0:T(1,128)S(1)} %get-tuple-element.60.refs_1_, ...), custom_call_target="tpu_custom_call" | custom-call | flops 1 | bytes 1 | tf_op jit(solution)/shard_map/attend11/pallas_call | solution.py:336
  88.9 2.2 %collective-permute-start.12 = (bf16[4,5,16,128]{3,2,1,0:T(8,128)(2,1)S(1)}, bf16[4,5,16,128]{3,2,1,0:T(8,128)(2,1)S(1)}, u32[]{:S(2)}, u32[]{:S(2)}) collective-permute-start(bf16[4,5,16,128]{3,2,1,0:T(8,128)(2,1)S(1)} %get-tuple-element.48), channel_id=1, source_target_pairs={{0,32},{32,0},{64,96},{96,64},{128,160},{160,128},{192,224},{224,1... | collective-permute-start | bytes 245768 | tf_op jit(solution)/shard_map/ppermute | solution.py:268
  91.1 5.9 %collective-permute-start.13 = (bf16[4,5,16,128]{3,2,1,0:T(8,128)(2,1)S(1)}, bf16[4,5,16,128]{3,2,1,0:T(8,128)(2,1)S(1)}, u32[]{:S(2)}, u32[]{:S(2)}) collective-permute-start(bf16[4,5,16,128]{3,2,1,0:T(8,128)(2,1)S(1)} %get-tuple-element.49), channel_id=1, source_target_pairs={{0,64},{32,96},{64,0},{96,32},{128,192},{160,224},{192,128},{224,1... | collective-permute-start | bytes 245768 | tf_op jit(solution)/shard_map/ppermute | solution.py:268
  97.0 2.0 %collective-permute-start.14 = (bf16[4,5,16,128]{3,2,1,0:T(8,128)(2,1)S(1)}, bf16[4,5,16,128]{3,2,1,0:T(8,128)(2,1)S(1)}, u32[]{:S(2)}, u32[]{:S(2)}) collective-permute-start(bf16[4,5,16,128]{3,2,1,0:T(8,128)(2,1)S(1)} %get-tuple-element.50), channel_id=1, source_target_pairs={{0,96},{32,64},{64,32},{96,0},{128,224},{160,192},{192,160},{224,1... | collective-permute-start | bytes 245768 | tf_op jit(solution)/shard_map/ppermute | solution.py:268
  99.0 0.0 collective-permute-done.12.b
  99.0 0.6 collective-permute-done.13.c
  99.7 3.9 %collective-permute-done.14.d = bf16[4,5,16,128]{3,2,1,0:T(8,128)(2,1)S(1)} collective-permute-done((bf16[4,5,16,128]{3,2,1,0:T(8,128)(2,1)S(1)}, bf16[4,5,16,128]{3,2,1,0:T(8,128)(2,1)S(1)}, u32[]{:S(2)}, u32[]{:S(2)}) %collective-permute-start.14) | collective-permute-done | bytes 81952 | tf_op jit(solution)/shard_map/ppermute | solution.py:268
  103.5 1.2 %middle.1 = (bf16[5,16,128]{2,1,0:T(8,128)(2,1)S(1)}, bf16[5,16,128]{2,1,0:T(8,128)(2,1)S(1)}, bf16[5,16,128]{2,1,0:T(8,128)(2,1)S(1)}, bf16[5,16,128]{2,1,0:T(8,128)(2,1)S(1)}) custom-call(s32[2]{0:T(128)S(1)} %pad_add_fusion.place.refs_0_, bf16[4,5,16,128]{3,2,1,0:T(8,128)(2,1)S(1)} %get-tuple-element.47.a, ...), custom_call_target="tpu_custom_call" | custom-call | flops 1 | bytes 1 | tf_op jit(solution)/shard_map/middle/pallas_call | solution.py:343
  104.8 4.0 %collective-permute-start.15 = (bf16[5,16,128]{2,1,0:T(8,128)(2,1)S(1)}, bf16[5,16,128]{2,1,0:T(8,128)(2,1)S(1)}, u32[]{:S(2)}, u32[]{:S(2)}) collective-permute-start(bf16[5,16,128]{2,1,0:T(8,128)(2,1)S(1)} %get-tuple-element.52), channel_id=1, source_target_pairs={{0,128},{32,160},{64,192},{96,224},{128,0},{160,32},{192,64},{224,... | collective-permute-start | bytes 61448 | tf_op jit(solution)/shard_map/ppermute | solution.py:268
  108.8 1.9 %collective-permute-start.16 = (bf16[5,16,128]{2,1,0:T(8,128)(2,1)S(1)}, bf16[5,16,128]{2,1,0:T(8,128)(2,1)S(1)}, u32[]{:S(2)}, u32[]{:S(2)}) collective-permute-start(bf16[5,16,128]{2,1,0:T(8,128)(2,1)S(1)} %get-tuple-element.53), channel_id=1, source_target_pairs={{0,256},{32,288},{64,320},{96,352},{128,384},{160,416},{192,448},{... | collective-permute-start | bytes 61448 | tf_op jit(solution)/shard_map/ppermute | solution.py:268
  110.7 7.3 %collective-permute-start.17 = (bf16[5,16,128]{2,1,0:T(8,128)(2,1)S(1)}, bf16[5,16,128]{2,1,0:T(8,128)(2,1)S(1)}, u32[]{:S(2)}, u32[]{:S(2)}) collective-permute-start(bf16[5,16,128]{2,1,0:T(8,128)(2,1)S(1)} %get-tuple-element.54), channel_id=1, source_target_pairs={{0,384},{32,416},{64,448},{96,480},{128,256},{160,288},{192,320},{... | collective-permute-start | bytes 61448 | tf_op jit(solution)/shard_map/ppermute | solution.py:268
  118.0 0.0 collective-permute-done.15.b
  118.0 0.0 collective-permute-done.16.c
  118.0 2.9 %collective-permute-done.17.d = bf16[5,16,128]{2,1,0:T(8,128)(2,1)S(1)} collective-permute-done((bf16[5,16,128]{2,1,0:T(8,128)(2,1)S(1)}, bf16[5,16,128]{2,1,0:T(8,128)(2,1)S(1)}, u32[]{:S(2)}, u32[]{:S(2)}) %collective-permute-start.17) | collective-permute-done | bytes 20512 | tf_op jit(solution)/shard_map/ppermute | solution.py:268
  120.9 1.4 %final.1 = bf16[16,512]{1,0:T(8,128)(2,1)} custom-call(s32[2]{0:T(128)S(1)} %pad_add_fusion.place.refs_0_, bf16[5,16,128]{2,1,0:T(8,128)(2,1)S(1)} %get-tuple-element.51.a, bf16[5,16,128]{2,1,0:T(8,128)(2,1)S(1)} %collective-permute-done.15.b, bf16[5,16,128]{2,1,0:T(8,128)(2,1)S(1)} %collective-permute-done.16.c, ...), custom_call_target="tpu_custom_call" | custom-call | flops 1 | bytes 1 | tf_op jit(solution)/shard_map/final/pallas_call | solution.py:345
  (11 shorter events, 0.2 us)
Async XLA Ops:
  0.0 0.9 copy-start
  0.9 0.8 copy-start.1
  1.6 0.8 copy-start.2
  2.4 0.7 copy-start.3
  3.5 17.2 %collective-permute-start = (bf16[1,352,128]{2,1,0:T(8,128)(2,1)S(1)}, bf16[1,352,128]{2,1,0:T(8,128)(2,1)S(1)}, u32[]{:S(2)}, u32[]{:S(2)}) collective-permute-start(bf16[1,352,128]{2,1,0:T(8,128)(2,1)S(1)} %get-tuple-element.30.p0), channel_id=1, source_target_pairs={{0,256},{32,288},{64,320},{96,352},{128,384},{160,416},{192,448},{... | collective-permute-start | bytes 270344 | tf_op jit(solution)/shard_map/ppermute | solution.py:268
  13.1 12.9 %collective-permute-start.1 = (bf16[1,72,512]{2,1,0:T(8,128)(2,1)S(1)}, bf16[1,72,512]{2,1,0:T(8,128)(2,1)S(1)}, u32[]{:S(2)}, u32[]{:S(2)}) collective-permute-start(bf16[1,72,512]{2,1,0:T(8,128)(2,1)S(1)} %get-tuple-element.31), channel_id=1, source_target_pairs={{0,449},{1,448},{64,385},{65,384},{128,321},{129,320},{192,257},{1... | collective-permute-start | bytes 221192 | tf_op jit(solution)/shard_map/ppermute | solution.py:290
  26.1 11.6 %collective-permute-start.3 = (bf16[2,72,512]{2,1,0:T(8,128)(2,1)S(1)}, bf16[2,72,512]{2,1,0:T(8,128)(2,1)S(1)}, u32[]{:S(2)}, u32[]{:S(2)}) collective-permute-start(bf16[2,72,512]{2,1,0:T(8,128)(2,1)S(1)} %get-tuple-element.55), channel_id=1, source_target_pairs={{0,8},{8,0},{16,24},{24,16},{1,9},{9,1},{17,25},{25,17},{2,10},{10... | collective-permute-start | bytes 442376 | tf_op jit(solution)/shard_map/ppermute | solution.py:268
  29.2 8.7 %collective-permute-start.4 = (bf16[2,72,512]{2,1,0:T(8,128)(2,1)S(1)}, bf16[2,72,512]{2,1,0:T(8,128)(2,1)S(1)}, u32[]{:S(2)}, u32[]{:S(2)}) collective-permute-start(bf16[2,72,512]{2,1,0:T(8,128)(2,1)S(1)} %get-tuple-element.55), channel_id=1, source_target_pairs={{0,16},{8,24},{16,0},{24,8},{1,17},{9,25},{17,1},{25,9},{2,18},{10... | collective-permute-start | bytes 442376 | tf_op jit(solution)/shard_map/ppermute | solution.py:268
  33.6 7.8 %collective-permute-start.5 = (bf16[2,72,512]{2,1,0:T(8,128)(2,1)S(1)}, bf16[2,72,512]{2,1,0:T(8,128)(2,1)S(1)}, u32[]{:S(2)}, u32[]{:S(2)}) collective-permute-start(bf16[2,72,512]{2,1,0:T(8,128)(2,1)S(1)} %get-tuple-element.55), channel_id=1, source_target_pairs={{0,24},{8,16},{16,8},{24,0},{1,25},{9,17},{17,9},{25,1},{2,26},{10... | collective-permute-start | bytes 442376 | tf_op jit(solution)/shard_map/ppermute | solution.py:268
  35.7 7.4 %collective-permute-start.2 = (bf16[2,352,128]{2,1,0:T(8,128)(2,1)S(1)}, bf16[2,352,128]{2,1,0:T(8,128)(2,1)S(1)}, u32[]{:S(2)}, u32[]{:S(2)}) collective-permute-start(bf16[2,352,128]{2,1,0:T(8,128)(2,1)S(1)} %pad_maximum_fusion.2), channel_id=1, source_target_pairs={{0,128},{32,160},{64,192},{96,224},{128,0},{160,32},{192,64},{224,... | collective-permute-start | bytes 540680 | tf_op jit(solution)/shard_map/ppermute | solution.py:268
  43.1 22.1 %collective-permute-start.7 = (bf16[8,72,512]{2,1,0:T(8,128)(2,1)S(1)}, bf16[8,72,512]{2,1,0:T(8,128)(2,1)S(1)}, u32[]{:S(2)}, u32[]{:S(2)}) collective-permute-start(bf16[8,72,512]{2,1,0:T(8,128)(2,1)S(1)} %constant_dynamic-update-slice_fusion.2.refs_3_), channel_id=1, source_target_pairs={{0,2},{2,0},{4,6},{6,4},{1,3},{3,1},{5,7},{7,5},{8,10},{10,8},{12,... | collective-permute-start | bytes 1769480 | tf_op jit(solution)/shard_map/ppermute | solution.py:268
  46.4 18.9 %collective-permute-start.8 = (bf16[8,72,512]{2,1,0:T(8,128)(2,1)S(1)}, bf16[8,72,512]{2,1,0:T(8,128)(2,1)S(1)}, u32[]{:S(2)}, u32[]{:S(2)}) collective-permute-start(bf16[8,72,512]{2,1,0:T(8,128)(2,1)S(1)} %constant_dynamic-update-slice_fusion.2.refs_3_), channel_id=1, source_target_pairs={{0,6},{2,4},{4,2},{6,0},{1,7},{3,5},{5,3},{7,1},{8,14},{10,12},{12... | collective-permute-start | bytes 1769480 | tf_op jit(solution)/shard_map/ppermute | solution.py:268
  50.2 14.2 %collective-permute-start.6 = (bf16[4,352,128]{2,1,0:T(8,128)(2,1)S(1)}, bf16[4,352,128]{2,1,0:T(8,128)(2,1)S(1)}, u32[]{:S(2)}, u32[]{:S(2)}) collective-permute-start(bf16[4,352,128]{2,1,0:T(8,128)(2,1)S(1)} %pad_maximum_fusion.1), channel_id=1, source_target_pairs={{0,64},{32,96},{64,0},{96,32},{128,192},{160,224},{192,128},{224,1... | collective-permute-start | bytes 1081352 | tf_op jit(solution)/shard_map/ppermute | solution.py:268
  65.3 10.6 %collective-permute-start.9 = (bf16[8,352,128]{2,1,0:T(8,128)(2,1)}, bf16[8,352,128]{2,1,0:T(8,128)(2,1)S(1)}, u32[]{:S(2)}, u32[]{:S(2)}) collective-permute-start(bf16[8,352,128]{2,1,0:T(8,128)(2,1)} %pad_maximum_fusion), channel_id=1, source_target_pairs={{0,32},{32,0},{64,96},{96,64},{128,160},{160,128},{192,224},{224,1... | collective-permute-start | bytes 2162696 | tf_op jit(solution)/shard_map/ppermute | solution.py:268
  71.2 13.9 %collective-permute-start.10 = (bf16[4,72,512]{2,1,0:T(8,128)(2,1)S(1)}, bf16[4,72,512]{2,1,0:T(8,128)(2,1)S(1)}, u32[]{:S(2)}, u32[]{:S(2)}) collective-permute-start(bf16[4,72,512]{2,1,0:T(8,128)(2,1)S(1)} %slice.16), channel_id=1, source_target_pairs={{0,6},{2,4},{4,2},{6,0},{1,7},{3,5},{5,3},{7,1},{8,14},{10,12},{12... | collective-permute-start | bytes 884744 | tf_op jit(solution)/shard_map/ppermute | solution.py:268
  73.9 11.1 %collective-permute-start.11 = (bf16[4,72,512]{2,1,0:T(8,128)(2,1)S(1)}, bf16[4,72,512]{2,1,0:T(8,128)(2,1)S(1)}, u32[]{:S(2)}, u32[]{:S(2)}) collective-permute-start(bf16[4,72,512]{2,1,0:T(8,128)(2,1)S(1)} %slice.17), channel_id=1, source_target_pairs={{0,2},{2,0},{4,6},{6,4},{1,3},{3,1},{5,7},{7,5},{8,10},{10,8},{12,... | collective-permute-start | bytes 884744 | tf_op jit(solution)/shard_map/ppermute | solution.py:268
  88.9 10.1 %collective-permute-start.12 = (bf16[4,5,16,128]{3,2,1,0:T(8,128)(2,1)S(1)}, bf16[4,5,16,128]{3,2,1,0:T(8,128)(2,1)S(1)}, u32[]{:S(2)}, u32[]{:S(2)}) collective-permute-start(bf16[4,5,16,128]{3,2,1,0:T(8,128)(2,1)S(1)} %get-tuple-element.48), channel_id=1, source_target_pairs={{0,32},{32,0},{64,96},{96,64},{128,160},{160,128},{192,224},{224,1... | collective-permute-start | bytes 245768 | tf_op jit(solution)/shard_map/ppermute | solution.py:268
  91.1 8.5 %collective-permute-start.13 = (bf16[4,5,16,128]{3,2,1,0:T(8,128)(2,1)S(1)}, bf16[4,5,16,128]{3,2,1,0:T(8,128)(2,1)S(1)}, u32[]{:S(2)}, u32[]{:S(2)}) collective-permute-start(bf16[4,5,16,128]{3,2,1,0:T(8,128)(2,1)S(1)} %get-tuple-element.49), channel_id=1, source_target_pairs={{0,64},{32,96},{64,0},{96,32},{128,192},{160,224},{192,128},{224,1... | collective-permute-start | bytes 245768 | tf_op jit(solution)/shard_map/ppermute | solution.py:268
  97.0 6.5 %collective-permute-start.14 = (bf16[4,5,16,128]{3,2,1,0:T(8,128)(2,1)S(1)}, bf16[4,5,16,128]{3,2,1,0:T(8,128)(2,1)S(1)}, u32[]{:S(2)}, u32[]{:S(2)}) collective-permute-start(bf16[4,5,16,128]{3,2,1,0:T(8,128)(2,1)S(1)} %get-tuple-element.50), channel_id=1, source_target_pairs={{0,96},{32,64},{64,32},{96,0},{128,224},{160,192},{192,160},{224,1... | collective-permute-start | bytes 245768 | tf_op jit(solution)/shard_map/ppermute | solution.py:268
  104.8 13.2 %collective-permute-start.15 = (bf16[5,16,128]{2,1,0:T(8,128)(2,1)S(1)}, bf16[5,16,128]{2,1,0:T(8,128)(2,1)S(1)}, u32[]{:S(2)}, u32[]{:S(2)}) collective-permute-start(bf16[5,16,128]{2,1,0:T(8,128)(2,1)S(1)} %get-tuple-element.52), channel_id=1, source_target_pairs={{0,128},{32,160},{64,192},{96,224},{128,0},{160,32},{192,64},{224,... | collective-permute-start | bytes 61448 | tf_op jit(solution)/shard_map/ppermute | solution.py:268
  108.8 9.2 %collective-permute-start.16 = (bf16[5,16,128]{2,1,0:T(8,128)(2,1)S(1)}, bf16[5,16,128]{2,1,0:T(8,128)(2,1)S(1)}, u32[]{:S(2)}, u32[]{:S(2)}) collective-permute-start(bf16[5,16,128]{2,1,0:T(8,128)(2,1)S(1)} %get-tuple-element.53), channel_id=1, source_target_pairs={{0,256},{32,288},{64,320},{96,352},{128,384},{160,416},{192,448},{... | collective-permute-start | bytes 61448 | tf_op jit(solution)/shard_map/ppermute | solution.py:268
  110.7 10.2 %collective-permute-start.17 = (bf16[5,16,128]{2,1,0:T(8,128)(2,1)S(1)}, bf16[5,16,128]{2,1,0:T(8,128)(2,1)S(1)}, u32[]{:S(2)}, u32[]{:S(2)}) collective-permute-start(bf16[5,16,128]{2,1,0:T(8,128)(2,1)S(1)} %get-tuple-element.54), channel_id=1, source_target_pairs={{0,384},{32,416},{64,448},{96,480},{128,256},{160,288},{192,320},{... | collective-permute-start | bytes 61448 | tf_op jit(solution)/shard_map/ppermute | solution.py:268

commit v3 on v2

--- a/solution.py
+++ b/solution.py
@@ -163,7 +163,7 @@
         del refs[:3]
     if last:
         wv = refs.pop(0)
-        outs, (keys, parts) = refs[:4], refs[4:]
+        outs, (keys, parts) = refs[:2], refs[2:]
     else:
         acc_out, peak_out, total_out, keys = refs
     me, prior = place[0], place[1]
@@ -224,10 +224,10 @@
         tile = pack_lse(lses, (ROWS, 128))
         for g in range(16):
             parts[g, HEADS] = tile[TOK * g : TOK * (g + 1)]
-        low = lax.bitwise_and(me, 3)
-        for d in range(4):
-            for high in range(4):
-                outs[d][high] = parts[high * 4 + lax.bitwise_xor(low, d)]
+        low = lax.bitwise_and(me, 1)
+        for d in range(2):
+            for zl in range(8):
+                outs[d][zl] = parts[zl * 2 + lax.bitwise_xor(low, d)]
 
 
 def merge_heads(tiles):
@@ -248,18 +248,16 @@
     return values, lses
 
 
-def middle_kernel(place, a, b, c, d, *outs):
-    high = lax.shift_right_logical(place[0], 2)
-    for j, out in enumerate(outs):
-        g = lax.bitwise_xor(high, j)
-        values, lses = merge_heads([r[g] for r in (a, b, c, d)])
+def pair_kernel(place, a, b, out):
+    for g in range(8):
+        values, lses = merge_heads([a[g], b[g]])
         for h in range(HEADS):
-            out[h] = values[h].astype(bf16)
-        out[HEADS] = pack_lse(lses, (TOK, 128))
-
-
-def final_kernel(place, a, b, c, d, out):
-    values, _ = merge_heads([r[...] for r in (a, b, c, d)])
+            out[g, h] = values[h].astype(bf16)
+        out[g, HEADS] = pack_lse(lses, (TOK, 128))
+
+
+def final_kernel(place, x, out):
+    values, _ = merge_heads([x[g] for g in range(8)])
     for h in range(HEADS):
         out[:, h * VALUE : (h + 1) * VALUE] = values[h].astype(bf16)
 
@@ -291,12 +289,13 @@
     pack = widen(pack, 8)
     mirror, pack = lax.optimization_barrier((mirror, pack))
     pair = jnp.concatenate([shard, mirror], axis=0)
-    quad = jnp.concatenate([pair] + [swap(pair, "x", 4, d) for d in (1, 2, 3)], axis=0)
+    sides = [swap(pair, "x", 4, d) for d in (1, 2, 3)]
     pack = widen(pack, 4)
-    quad, pack = lax.optimization_barrier((quad, pack))
+    *sides, _ = lax.optimization_barrier((*sides, pack))
+    quad = jnp.concatenate([pair] + sides, axis=0)
     near, back = swap(quad, "y", 4, 1), swap(quad, "y", 4, 3)
     pack = widen(pack, 2)
-    near, back, pack = lax.optimization_barrier((near, back, pack))
+    near, back, _ = lax.optimization_barrier((near, back, pack))
     far = (swap(near[:4], "y", 4, 3), swap(back[4:], "y", 4, 1))
     pieces.append(swap(pack, CTX, 16, 1))
 
@@ -329,7 +328,7 @@
         def kernel(*refs):
             attention_kernel(count, arrays, first, last, *refs)
 
-        shape = state if not last else tuple(shaped((4, HEADS + 1, TOK, 128)) for _ in range(4))
+        shape = state if not last else (shaped((8, HEADS + 1, TOK, 128)),) * 2
         scratch = [pltpu.VMEM((count, 2, 256, WIDE), bf16)]
         if last:
             scratch.append(pltpu.VMEM((16, HEADS + 1, TOK, 128), bf16))
@@ -339,10 +338,11 @@
     run = attend(2, 2, False, False, place, kpos[:, 512:1536], q, near, back, *run)
     parts = attend(1, 2, False, True, place, kpos[:, 1536:], q, *far, *run, wv)
 
-    got = [parts[0]] + [swap(parts[d], CTX, 16, d) for d in (1, 2, 3)]
-    parts = call(middle_kernel, tuple(shaped((HEADS + 1, TOK, 128)) for _ in range(4)), 4, "middle")(place, *got)
-    got = [parts[0]] + [swap(parts[d], CTX, 16, 4 * d) for d in (1, 2, 3)]
-    return call(final_kernel, shaped((TOK, HEADS * VALUE)), 4, "final")(place, *got)
+    merged = call(pair_kernel, shaped((8, HEADS + 1, TOK, 128)), 2, "pair")(
+        place, parts[0], swap(parts[1], CTX, 16, 1)
+    )
+    spread = lax.all_to_all(merged, "zl", 0, 0, tiled=True)
+    return call(final_kernel, shaped((TOK, HEADS * VALUE)), 1, "final")(place, spread)
 
 
 def solution(mesh):

time: 124 us -> 113 us (0.911)
  the two profiles are of different devices: /device:TPU:1 before, /device:TPU:12 now
where the time goes in v3:
time: 113 us; the launch traced here: 112 us
  starting transfers between devices  55.4 us (49%)
  blocking collectives  18 us (16%)
  Pallas kernels  16.3 us (14%)
  waiting for transfers between devices  16.2 us (14%)
  local copies, waits for them, and re-layouts  5.44 us (5%)
    ppermute x12, starting transfers between devices, swap(): return lax.ppermute(x, axis, [(i, i ^ d) for i in range(n)])  47.7 us
    all_to_all x1, blocking collectives, per_device(): spread = lax.all_to_all(merged, 'zl', 0, 0, tiled=True)  18 us
    pallas_call x3, Pallas kernels, attend(): call(kernel, shape, len(operands) - 1, f'attend{count}{int(last)}', scratch)  11.8 us
    ppermute x12, waiting for transfers between devices, swap(): return lax.ppermute(x, axis, [(i, i ^ d) for i in range(n)])  10.3 us
    ppermute x1, starting transfers between devices, per_device(): mirror = lax.ppermute(shard, ('zl', 'zh'), [(i, 15 - i) for i in range(16)])  7.76 us
    ppermute x1, waiting for transfers between devices, per_device(): mirror = lax.ppermute(shard, ('zl', 'zh'), [(i, 15 - i) for i in range(16)])  5.9 us
    unnamed x13, local copies, waits for them, and re-layouts  4.61 us
  transfers between devices with their start and end apart: 13, of which 6 were waited for; matrix products, arithmetic and copies ran while one was open for 2% of the time, Pallas kernels for 8%

profile of v3, /device:TPU:12, one launch (start us, length us, event | category | flops | bytes accessed | tf_op | source)
XLA Modules:
  0.0 112.4 jit_solution(1859157335951717270)
XLA Ops:
  0.0 0.0 copy-start
  0.0 0.9 copy-done
  0.9 0.0 copy-start.1
  0.9 0.8 copy-done.1
  1.6 0.0 copy-start.2
  1.6 0.8 copy-done.2
  2.4 0.0 copy-start.3
  2.4 0.7 copy-done.3
  3.1 0.3 prepare.1
  3.5 9.1 %collective-permute-start = (bf16[1,352,128]{2,1,0:T(8,128)(2,1)S(1)}, bf16[1,352,128]{2,1,0:T(8,128)(2,1)S(1)}, u32[]{:S(2)}, u32[]{:S(2)}) collective-permute-start(bf16[1,352,128]{2,1,0:T(8,128)(2,1)S(1)} %get-tuple-element.24.p0), channel_id=1, source_target_pairs={{0,256},{32,288},{64,320},{96,352},{128,384},{160,416},{192,448},{... | collective-permute-start | bytes 270344 | tf_op jit(solution)/shard_map/ppermute | solution.py:266
  12.6 7.8 %collective-permute-start.1 = (bf16[1,72,512]{2,1,0:T(8,128)(2,1)S(1)}, bf16[1,72,512]{2,1,0:T(8,128)(2,1)S(1)}, u32[]{:S(2)}, u32[]{:S(2)}) collective-permute-start(bf16[1,72,512]{2,1,0:T(8,128)(2,1)S(1)} %get-tuple-element.25), channel_id=1, source_target_pairs={{0,449},{1,448},{64,385},{65,384},{128,321},{129,320},{192,257},{1... | collective-permute-start | bytes 221192 | tf_op jit(solution)/shard_map/ppermute | solution.py:288
  20.4 0.6 collective-permute-done.p1
  21.0 5.9 %collective-permute-done.1 = bf16[1,72,512]{2,1,0:T(8,128)(2,1)S(1)} collective-permute-done((bf16[1,72,512]{2,1,0:T(8,128)(2,1)S(1)}, bf16[1,72,512]{2,1,0:T(8,128)(2,1)S(1)}, u32[]{:S(2)}, u32[]{:S(2)}) %collective-permute-start.1) | collective-permute-done | bytes 73760 | tf_op jit(solution)/shard_map/ppermute | solution.py:288
  26.9 2.0 %collective-permute-start.2 = (bf16[2,352,128]{2,1,0:T(8,128)(2,1)S(1)}, bf16[2,352,128]{2,1,0:T(8,128)(2,1)S(1)}, u32[]{:S(2)}, u32[]{:S(2)}) collective-permute-start(bf16[2,352,128]{2,1,0:T(8,128)(2,1)S(1)} %pad_maximum_fusion), channel_id=1, source_target_pairs={{0,128},{32,160},{64,192},{96,224},{128,0},{160,32},{192,64},{224,... | collective-permute-start | bytes 540680 | tf_op jit(solution)/shard_map/ppermute | solution.py:266
  29.0 3.1 %collective-permute-start.5 = (bf16[2,72,512]{2,1,0:T(8,128)(2,1)S(1)}, bf16[2,72,512]{2,1,0:T(8,128)(2,1)S(1)}, u32[]{:S(2)}, u32[]{:S(2)}) collective-permute-start(bf16[2,72,512]{2,1,0:T(8,128)(2,1)S(1)} %get-tuple-element.47), channel_id=1, source_target_pairs={{0,8},{8,0},{16,24},{24,16},{1,9},{9,1},{17,25},{25,17},{2,10},{10... | collective-permute-start | bytes 442376 | tf_op jit(solution)/shard_map/ppermute | solution.py:266
  32.1 2.7 %collective-permute-start.6 = (bf16[2,72,512]{2,1,0:T(8,128)(2,1)S(1)}, bf16[2,72,512]{2,1,0:T(8,128)(2,1)S(1)}, u32[]{:S(2)}, u32[]{:S(2)}) collective-permute-start(bf16[2,72,512]{2,1,0:T(8,128)(2,1)S(1)} %get-tuple-element.47), channel_id=1, source_target_pairs={{0,16},{8,24},{16,0},{24,8},{1,17},{9,25},{17,1},{25,9},{2,18},{10... | collective-permute-start | bytes 442376 | tf_op jit(solution)/shard_map/ppermute | solution.py:266
  34.8 3.4 %collective-permute-start.7 = (bf16[2,72,512]{2,1,0:T(8,128)(2,1)S(1)}, bf16[2,72,512]{2,1,0:T(8,128)(2,1)S(1)}, u32[]{:S(2)}, u32[]{:S(2)}) collective-permute-start(bf16[2,72,512]{2,1,0:T(8,128)(2,1)S(1)} %get-tuple-element.47), channel_id=1, source_target_pairs={{0,24},{8,16},{16,8},{24,0},{1,25},{9,17},{17,9},{25,1},{2,26},{10... | collective-permute-start | bytes 442376 | tf_op jit(solution)/shard_map/ppermute | solution.py:266
  38.2 0.7 constant_dynamic-update-slice_fusion.4
  38.9 0.0 collective-permute-done.2.p2
  38.9 0.7 constant_dynamic-update-slice_fusion.3
  39.6 8.7 %collective-permute-start.3 = (bf16[4,352,128]{2,1,0:T(8,128)(2,1)S(1)}, bf16[4,352,128]{2,1,0:T(8,128)(2,1)S(1)}, u32[]{:S(2)}, u32[]{:S(2)}) collective-permute-start(bf16[4,352,128]{2,1,0:T(8,128)(2,1)S(1)} %get-tuple-element.44), channel_id=1, source_target_pairs={{0,64},{32,96},{64,0},{96,32},{128,192},{160,224},{192,128},{224,1... | collective-permute-start | bytes 1081352 | tf_op jit(solution)/shard_map/ppermute | solution.py:266
  48.4 0.0 collective-permute-done.5
  48.4 0.0 collective-permute-done.6
  48.4 0.0 collective-permute-done.7
  48.4 2.4 %collective-permute-start.8 = (bf16[8,72,512]{2,1,0:T(8,128)(2,1)S(1)}, bf16[8,72,512]{2,1,0:T(8,128)(2,1)S(1)}, u32[]{:S(2)}, u32[]{:S(2)}) collective-permute-start(bf16[8,72,512]{2,1,0:T(8,128)(2,1)S(1)} %constant_dynamic-update-slice_fusion.7.refs_3_), channel_id=1, source_target_pairs={{0,2},{2,0},{4,6},{6,4},{1,3},{3,1},{5,7},{7,5},{8,10},{10,8},{12,... | collective-permute-start | bytes 1769480 | tf_op jit(solution)/shard_map/ppermute | solution.py:266
  50.8 4.3 %collective-permute-start.9 = (bf16[8,72,512]{2,1,0:T(8,128)(2,1)S(1)}, bf16[8,72,512]{2,1,0:T(8,128)(2,1)S(1)}, u32[]{:S(2)}, u32[]{:S(2)}) collective-permute-start(bf16[8,72,512]{2,1,0:T(8,128)(2,1)S(1)} %constant_dynamic-update-slice_fusion.7.refs_3_), channel_id=1, source_target_pairs={{0,6},{2,4},{4,2},{6,0},{1,7},{3,5},{5,3},{7,1},{8,14},{10,12},{12... | collective-permute-start | bytes 1769480 | tf_op jit(solution)/shard_map/ppermute | solution.py:266
  55.1 0.6 collective-permute-done.3.p3
  55.7 0.8 constant_dynamic-update-slice_fusion.2
  56.5 1.9 %collective-permute-start.4 = (bf16[8,352,128]{2,1,0:T(8,128)(2,1)}, bf16[8,352,128]{2,1,0:T(8,128)(2,1)S(1)}, u32[]{:S(2)}, u32[]{:S(2)}) collective-permute-start(bf16[8,352,128]{2,1,0:T(8,128)(2,1)} %constant_dynamic-update-slice_fusion.2), channel_id=1, source_target_pairs={{0,32},{32,0},{64,96},{96,64},{128,160},{160,128},{192,224},{224,1... | collective-permute-start | bytes 2162696 | tf_op jit(solution)/shard_map/ppermute | solution.py:266
  59.0 0.1 and_add_fusion
  59.1 5.0 %collective-permute-done.8.refs_3_ = bf16[8,72,512]{2,1,0:T(8,128)(2,1)S(1)} collective-permute-done((bf16[8,72,512]{2,1,0:T(8,128)(2,1)S(1)}, bf16[8,72,512]{2,1,0:T(8,128)(2,1)S(1)}, u32[]{:S(2)}, u32[]{:S(2)}) %collective-permute-start.8) | collective-permute-done | bytes 589856 | tf_op jit(solution)/shard_map/ppermute | solution.py:266
  64.1 2.8 %collective-permute-done.9.refs_4_ = bf16[8,72,512]{2,1,0:T(8,128)(2,1)S(1)} collective-permute-done((bf16[8,72,512]{2,1,0:T(8,128)(2,1)S(1)}, bf16[8,72,512]{2,1,0:T(8,128)(2,1)S(1)}, u32[]{:S(2)}, u32[]{:S(2)}) %collective-permute-start.9) | collective-permute-done | bytes 589856 | tf_op jit(solution)/shard_map/ppermute | solution.py:266
  66.9 3.6 %collective-permute-start.10 = (bf16[4,72,512]{2,1,0:T(8,128)(2,1)S(1)}, bf16[4,72,512]{2,1,0:T(8,128)(2,1)S(1)}, u32[]{:S(2)}, u32[]{:S(2)}) collective-permute-start(bf16[4,72,512]{2,1,0:T(8,128)(2,1)S(1)} %slice.16), channel_id=1, source_target_pairs={{0,6},{2,4},{4,2},{6,0},{1,7},{3,5},{5,3},{7,1},{8,14},{10,12},{12... | collective-permute-start | bytes 884744 | tf_op jit(solution)/shard_map/ppermute | solution.py:266
  70.6 4.5 %collective-permute-start.11 = (bf16[4,72,512]{2,1,0:T(8,128)(2,1)S(1)}, bf16[4,72,512]{2,1,0:T(8,128)(2,1)S(1)}, u32[]{:S(2)}, u32[]{:S(2)}) collective-permute-start(bf16[4,72,512]{2,1,0:T(8,128)(2,1)S(1)} %slice.17), channel_id=1, source_target_pairs={{0,2},{2,0},{4,6},{6,4},{1,3},{3,1},{5,7},{7,5},{8,10},{10,8},{12,... | collective-permute-start | bytes 884744 | tf_op jit(solution)/shard_map/ppermute | solution.py:266
  75.0 0.1 pad_add_fusion.place.refs_0_
  75.1 0.0 collective-permute-done.4.p4
  75.1 1.1 query.1
  76.2 2.8 %attend10.1 = (f32[4,256,512]{2,1,0:T(8,128)S(1)}, f32[4,256,128]{2,1,0:T(8,128)S(1)}, f32[4,256,128]{2,1,0:T(8,128)S(1)}) custom-call(s32[2]{0:T(128)S(1)} %pad_add_fusion.place.refs_0_, s32[1,512]{1,0:T(1,128)S(1)} %get-tuple-element.51.refs_1_, bf16[2,4,256,640]{3,2,1,0:T(8,128)(2,1)S(1)} %get-tuple-element.27.refs_2_, ...), custom_call_target="tpu_custom_call" | custom-call | flops 1 | bytes 1 | tf_op jit(solution)/shard_map/attend10/pallas_call | solution.py:335
  79.0 5.2 %attend20.1 = (f32[4,256,512]{2,1,0:T(8,128)S(1)}, f32[4,256,128]{2,1,0:T(8,128)S(1)}, f32[4,256,128]{2,1,0:T(8,128)S(1)}) custom-call(s32[2]{0:T(128)S(1)} %pad_add_fusion.place.refs_0_, s32[1,1024]{1,0:T(1,128)S(1)} %slice.21.refs_1_, bf16[2,4,256,640]{3,2,1,0:T(8,128)(2,1)S(1)} %get-tuple-element.27.refs_2_, ...), custom_call_target="tpu_custom_call" | custom-call | flops 1 | bytes 1 | tf_op jit(solution)/shard_map/attend20/pallas_call | solution.py:335
  84.2 0.0 collective-permute-done.10.refs_3_
  84.2 0.0 collective-permute-done.11.refs_4_
  84.2 3.8 %attend11.1 = (bf16[8,5,16,128]{3,2,1,0:T(8,128)(2,1)S(1)}, bf16[8,5,16,128]{3,2,1,0:T(8,128)(2,1)S(1)}) custom-call(s32[2]{0:T(128)S(1)} %pad_add_fusion.place.refs_0_, s32[1,512]{1,0:T(1,128)S(1)} %get-tuple-element.52.refs_1_, bf16[2,4,256,640]{3,2,1,0:T(8,128)(2,1)S(1)} %get-tuple-element.27.refs_2_, ...), custom_call_target="tpu_custom_call" | custom-call | flops 1 | bytes 1 | tf_op jit(solution)/shard_map/attend11/pallas_call | solution.py:335
  88.1 1.9 %collective-permute-start.12 = (bf16[8,5,16,128]{3,2,1,0:T(8,128)(2,1)S(1)}, bf16[8,5,16,128]{3,2,1,0:T(8,128)(2,1)S(1)}, u32[]{:S(2)}, u32[]{:S(2)}) collective-permute-start(bf16[8,5,16,128]{3,2,1,0:T(8,128)(2,1)S(1)} %get-tuple-element.42), channel_id=1, source_target_pairs={{0,32},{32,0},{64,96},{96,64},{128,160},{160,128},{192,224},{224,1... | collective-permute-start | bytes 491528 | tf_op jit(solution)/shard_map/ppermute | solution.py:266
  90.0 1.4 %collective-permute-done.12.b = bf16[8,5,16,128]{3,2,1,0:T(8,128)(2,1)S(1)} collective-permute-done((bf16[8,5,16,128]{3,2,1,0:T(8,128)(2,1)S(1)}, bf16[8,5,16,128]{3,2,1,0:T(8,128)(2,1)S(1)}, u32[]{:S(2)}, u32[]{:S(2)}) %collective-permute-start.12) | collective-permute-done | bytes 163872 | tf_op jit(solution)/shard_map/ppermute | solution.py:266
  91.4 1.7 %pair.1 = bf16[8,5,16,128]{3,2,1,0:T(8,128)(2,1)S(1)} custom-call(s32[2]{0:T(128)S(1)} %pad_add_fusion.place.refs_0_, bf16[8,5,16,128]{3,2,1,0:T(8,128)(2,1)S(1)} %get-tuple-element.41.a, bf16[8,5,16,128]{3,2,1,0:T(8,128)(2,1)S(1)} %collective-permute-done.12.b), custom_call_target="tpu_custom_call" | custom-call | flops 1 | bytes 1 | tf_op jit(solution)/shard_map/pair/pallas_call | solution.py:341
  93.1 18.0 %all_to_all.5.x = bf16[8,5,16,128]{3,2,1,0:T(8,128)(2,1)S(1)} all-to-all(bf16[8,5,16,128]{3,2,1,0:T(8,128)(2,1)S(1)} %pair.1), channel_id=1, replica_groups=mesh['zl'=8,'co'=2,'x'=4,'y'=4,'zh'=2] {'zl'}, dimensions={0} | all-to-all | bytes 327680 | tf_op jit(solution)/shard_map/all_to_all | solution.py:344
  111.0 1.4 %final.1 = bf16[16,512]{1,0:T(8,128)(2,1)} custom-call(s32[2]{0:T(128)S(1)} %pad_add_fusion.place.refs_0_, bf16[8,5,16,128]{3,2,1,0:T(8,128)(2,1)S(1)} %all_to_all.5.x), custom_call_target="tpu_custom_call" | custom-call | flops 1 | bytes 1 | tf_op jit(solution)/shard_map/final/pallas_call | solution.py:345
  (10 shorter events, 0.1 us)
Async XLA Ops:
  0.0 0.9 copy-start
  0.9 0.8 copy-start.1
  1.6 0.8 copy-start.2
  2.4 0.7 copy-start.3
  3.5 17.5 %collective-permute-start = (bf16[1,352,128]{2,1,0:T(8,128)(2,1)S(1)}, bf16[1,352,128]{2,1,0:T(8,128)(2,1)S(1)}, u32[]{:S(2)}, u32[]{:S(2)}) collective-permute-start(bf16[1,352,128]{2,1,0:T(8,128)(2,1)S(1)} %get-tuple-element.24.p0), channel_id=1, source_target_pairs={{0,256},{32,288},{64,320},{96,352},{128,384},{160,416},{192,448},{... | collective-permute-start | bytes 270344 | tf_op jit(solution)/shard_map/ppermute | solution.py:266
  12.6 14.3 %collective-permute-start.1 = (bf16[1,72,512]{2,1,0:T(8,128)(2,1)S(1)}, bf16[1,72,512]{2,1,0:T(8,128)(2,1)S(1)}, u32[]{:S(2)}, u32[]{:S(2)}) collective-permute-start(bf16[1,72,512]{2,1,0:T(8,128)(2,1)S(1)} %get-tuple-element.25), channel_id=1, source_target_pairs={{0,449},{1,448},{64,385},{65,384},{128,321},{129,320},{192,257},{1... | collective-permute-start | bytes 221192 | tf_op jit(solution)/shard_map/ppermute | solution.py:288
  26.9 12.0 %collective-permute-start.2 = (bf16[2,352,128]{2,1,0:T(8,128)(2,1)S(1)}, bf16[2,352,128]{2,1,0:T(8,128)(2,1)S(1)}, u32[]{:S(2)}, u32[]{:S(2)}) collective-permute-start(bf16[2,352,128]{2,1,0:T(8,128)(2,1)S(1)} %pad_maximum_fusion), channel_id=1, source_target_pairs={{0,128},{32,160},{64,192},{96,224},{128,0},{160,32},{192,64},{224,... | collective-permute-start | bytes 540680 | tf_op jit(solution)/shard_map/ppermute | solution.py:266
  29.0 19.4 %collective-permute-start.5 = (bf16[2,72,512]{2,1,0:T(8,128)(2,1)S(1)}, bf16[2,72,512]{2,1,0:T(8,128)(2,1)S(1)}, u32[]{:S(2)}, u32[]{:S(2)}) collective-permute-start(bf16[2,72,512]{2,1,0:T(8,128)(2,1)S(1)} %get-tuple-element.47), channel_id=1, source_target_pairs={{0,8},{8,0},{16,24},{24,16},{1,9},{9,1},{17,25},{25,17},{2,10},{10... | collective-permute-start | bytes 442376 | tf_op jit(solution)/shard_map/ppermute | solution.py:266
  32.1 16.3 %collective-permute-start.6 = (bf16[2,72,512]{2,1,0:T(8,128)(2,1)S(1)}, bf16[2,72,512]{2,1,0:T(8,128)(2,1)S(1)}, u32[]{:S(2)}, u32[]{:S(2)}) collective-permute-start(bf16[2,72,512]{2,1,0:T(8,128)(2,1)S(1)} %get-tuple-element.47), channel_id=1, source_target_pairs={{0,16},{8,24},{16,0},{24,8},{1,17},{9,25},{17,1},{25,9},{2,18},{10... | collective-permute-start | bytes 442376 | tf_op jit(solution)/shard_map/ppermute | solution.py:266
  34.8 13.6 %collective-permute-start.7 = (bf16[2,72,512]{2,1,0:T(8,128)(2,1)S(1)}, bf16[2,72,512]{2,1,0:T(8,128)(2,1)S(1)}, u32[]{:S(2)}, u32[]{:S(2)}) collective-permute-start(bf16[2,72,512]{2,1,0:T(8,128)(2,1)S(1)} %get-tuple-element.47), channel_id=1, source_target_pairs={{0,24},{8,16},{16,8},{24,0},{1,25},{9,17},{17,9},{25,1},{2,26},{10... | collective-permute-start | bytes 442376 | tf_op jit(solution)/shard_map/ppermute | solution.py:266
  39.6 16.1 %collective-permute-start.3 = (bf16[4,352,128]{2,1,0:T(8,128)(2,1)S(1)}, bf16[4,352,128]{2,1,0:T(8,128)(2,1)S(1)}, u32[]{:S(2)}, u32[]{:S(2)}) collective-permute-start(bf16[4,352,128]{2,1,0:T(8,128)(2,1)S(1)} %get-tuple-element.44), channel_id=1, source_target_pairs={{0,64},{32,96},{64,0},{96,32},{128,192},{160,224},{192,128},{224,1... | collective-permute-start | bytes 1081352 | tf_op jit(solution)/shard_map/ppermute | solution.py:266
  48.4 15.6 %collective-permute-start.8 = (bf16[8,72,512]{2,1,0:T(8,128)(2,1)S(1)}, bf16[8,72,512]{2,1,0:T(8,128)(2,1)S(1)}, u32[]{:S(2)}, u32[]{:S(2)}) collective-permute-start(bf16[8,72,512]{2,1,0:T(8,128)(2,1)S(1)} %constant_dynamic-update-slice_fusion.7.refs_3_), channel_id=1, source_target_pairs={{0,2},{2,0},{4,6},{6,4},{1,3},{3,1},{5,7},{7,5},{8,10},{10,8},{12,... | collective-permute-start | bytes 1769480 | tf_op jit(solution)/shard_map/ppermute | solution.py:266
  50.8 16.0 %collective-permute-start.9 = (bf16[8,72,512]{2,1,0:T(8,128)(2,1)S(1)}, bf16[8,72,512]{2,1,0:T(8,128)(2,1)S(1)}, u32[]{:S(2)}, u32[]{:S(2)}) collective-permute-start(bf16[8,72,512]{2,1,0:T(8,128)(2,1)S(1)} %constant_dynamic-update-slice_fusion.7.refs_3_), channel_id=1, source_target_pairs={{0,6},{2,4},{4,2},{6,0},{1,7},{3,5},{5,3},{7,1},{8,14},{10,12},{12... | collective-permute-start | bytes 1769480 | tf_op jit(solution)/shard_map/ppermute | solution.py:266
  56.5 18.6 %collective-permute-start.4 = (bf16[8,352,128]{2,1,0:T(8,128)(2,1)}, bf16[8,352,128]{2,1,0:T(8,128)(2,1)S(1)}, u32[]{:S(2)}, u32[]{:S(2)}) collective-permute-start(bf16[8,352,128]{2,1,0:T(8,128)(2,1)} %constant_dynamic-update-slice_fusion.2), channel_id=1, source_target_pairs={{0,32},{32,0},{64,96},{96,64},{128,160},{160,128},{192,224},{224,1... | collective-permute-start | bytes 2162696 | tf_op jit(solution)/shard_map/ppermute | solution.py:266
  66.9 17.4 %collective-permute-start.10 = (bf16[4,72,512]{2,1,0:T(8,128)(2,1)S(1)}, bf16[4,72,512]{2,1,0:T(8,128)(2,1)S(1)}, u32[]{:S(2)}, u32[]{:S(2)}) collective-permute-start(bf16[4,72,512]{2,1,0:T(8,128)(2,1)S(1)} %slice.16), channel_id=1, source_target_pairs={{0,6},{2,4},{4,2},{6,0},{1,7},{3,5},{5,3},{7,1},{8,14},{10,12},{12... | collective-permute-start | bytes 884744 | tf_op jit(solution)/shard_map/ppermute | solution.py:266
  70.6 13.7 %collective-permute-start.11 = (bf16[4,72,512]{2,1,0:T(8,128)(2,1)S(1)}, bf16[4,72,512]{2,1,0:T(8,128)(2,1)S(1)}, u32[]{:S(2)}, u32[]{:S(2)}) collective-permute-start(bf16[4,72,512]{2,1,0:T(8,128)(2,1)S(1)} %slice.17), channel_id=1, source_target_pairs={{0,2},{2,0},{4,6},{6,4},{1,3},{3,1},{5,7},{7,5},{8,10},{10,8},{12,... | collective-permute-start | bytes 884744 | tf_op jit(solution)/shard_map/ppermute | solution.py:266
  88.1 3.3 %collective-permute-start.12 = (bf16[8,5,16,128]{3,2,1,0:T(8,128)(2,1)S(1)}, bf16[8,5,16,128]{3,2,1,0:T(8,128)(2,1)S(1)}, u32[]{:S(2)}, u32[]{:S(2)}) collective-permute-start(bf16[8,5,16,128]{3,2,1,0:T(8,128)(2,1)S(1)} %get-tuple-element.42), channel_id=1, source_target_pairs={{0,32},{32,0},{64,96},{96,64},{128,160},{160,128},{192,224},{224,1... | collective-permute-start | bytes 491528 | tf_op jit(solution)/shard_map/ppermute | solution.py:266

commit v4 on v3

v4 whole, which is shorter than its diff:
```python
import math

import jax
import jax.numpy as jnp
from jax import lax
from jax.experimental import pallas as pl
from jax.experimental.pallas import tpu as pltpu
from jax.sharding import Mesh
from jax.sharding import PartitionSpec as P

PLAIN = 128
ROT = 64
LATENT = 512
VALUE = 128
HEADS = 4
WIDE = LATENT + 2 * ROT
TOK = 16
ROWS = 256
NEG = -1e30
LOG2_SCALE = (PLAIN + ROT) ** (-0.5) * math.log2(math.e)
VMEM_LIMIT = 40 * 1024 * 1024

ZL = ("zq", "zr")
CTX = ("zq", "zr", "co")
f32 = jnp.float32
bf16 = jnp.bfloat16


def vmem():
    return pl.BlockSpec(memory_space=pltpu.VMEM)


def call(kernel, shape, n_in, name, scratch=()):
    return pl.pallas_call(
        kernel,
        out_shape=shape,
        in_specs=[pl.BlockSpec(memory_space=pltpu.SMEM)] + [vmem()] * n_in,
        out_specs=jax.tree.map(lambda _: vmem(), shape),
        scratch_shapes=list(scratch),
        compiler_params=pltpu.CompilerParams(vmem_limit_bytes=VMEM_LIMIT),
        cost_estimate=pl.CostEstimate(flops=1, transcendentals=0, bytes_accessed=1),
        name=name,
    )


def shaped(shape, dtype=bf16):
    return jax.ShapeDtypeStruct(shape, dtype)


def prepare_kernel(queries_hbm, cache_hbm, wk_hbm, wv_hbm, shard, pack, queries, cache, sems):
    copies = [
        pltpu.make_async_copy(src, dst, sems.at[i])
        for i, (src, dst) in enumerate(
            (
                (cache_hbm, cache),
                (queries_hbm, queries),
                (wk_hbm, pack.at[0, 96:224, :]),
                (wv_hbm, pack.at[0, 224:352, :]),
            )
        )
    ]
    for c in copies:
        c.start()
    copies[0].wait()
    shard[0, :64, :] = cache[:, :LATENT]
    rot = cache[:, LATENT:]
    pairs = jnp.concatenate([rot[:32], rot[32:]], axis=1)
    for k in range(4):
        shard[0, 64:72, 128 * k : 128 * (k + 1)] = pairs[8 * k : 8 * (k + 1)]
    copies[1].wait()
    for k in range(6):
        pack[0, TOK * k : TOK * (k + 1), :] = queries[:, 128 * k : 128 * (k + 1)]
    copies[2].wait()
    copies[3].wait()


def prepare(queries, cache, wk, wv):
    return pl.pallas_call(
        prepare_kernel,
        out_shape=(shaped((1, 72, LATENT)), shaped((1, 352, 128))),
        in_specs=[pl.BlockSpec(memory_space=pltpu.HBM)] * 4,
        out_specs=(vmem(), vmem()),
        scratch_shapes=[
            pltpu.VMEM(queries.shape, bf16),
            pltpu.VMEM(cache.shape, bf16),
            pltpu.SemaphoreType.DMA((4,)),
        ],
        compiler_params=pltpu.CompilerParams(vmem_limit_bytes=VMEM_LIMIT),
        name="prepare",
    )(*(pltpu.with_memory_space_constraint(v, pltpu.HBM) for v in (queries, cache, wk, wv)))


def query_kernel(place, p0, p1, p2, p3, p4, q_out, wv_out, pieces, panel):
    me = place[0]
    sources = [
        (ref, i, lax.bitwise_xor(me, flip))
        for ref, flips in (
            (p0, (0, 8)),
            (p1, (2, 10)),
            (p2, (4, 12)),
            (p3, (6, 14)),
            (p4, (1, 9, 3, 11, 5, 13, 7, 15)),
        )
        for i, flip in enumerate(flips)
    ]
    for ref, i, src in sources:
        for k in range(6):
            pieces[k, src] = ref[i, TOK * k : TOK * (k + 1), :]
        for h in range(HEADS):
            panel[h, src] = ref[i, 96 + 32 * h : 128 + 32 * h, :]
            wv_out[h, src] = ref[i, 224 + 32 * h : 256 + 32 * h, :]
    zero = jnp.zeros((ROWS, ROT), bf16)
    for h in range(HEADS):
        k = (h // 2) * 3
        tile = [pieces[k + n].reshape(ROWS, 128) for n in range(3)]
        if h % 2 == 0:
            plain, rot = tile[0], tile[1][:, :ROT]
        else:
            plain = jnp.concatenate([tile[1][:, ROT:], tile[2][:, :ROT]], axis=1)
            rot = tile[2][:, ROT:]
        lat = lax.dot_general(
            plain,
            panel[h].reshape(LATENT, PLAIN),
            (((1,), (1,)), ((), ())),
            preferred_element_type=f32,
        ).astype(bf16)
        for half in range(2):
            q_out[half, h, :, :LATENT] = lat
        q_out[0, h, :, LATENT:] = jnp.concatenate([rot, zero], axis=1)
        q_out[1, h, :, LATENT:] = jnp.concatenate([zero, rot], axis=1)


def split3(x):
    hi = x.astype(bf16)
    r = x - hi.astype(f32)
    mid = r.astype(bf16)
    lo = (r - mid.astype(f32)).astype(bf16)
    return hi, mid, lo


def pack_lse(columns, shape):
    lane = lax.broadcasted_iota(jnp.int32, shape, len(shape) - 1)
    tile = jnp.zeros(shape, f32)
    for h, column in enumerate(columns):
        for p, part in enumerate(split3(column)):
            tile = jnp.where(lane == 3 * h + p, part.astype(f32), tile)
    return tile.astype(bf16)


def lse_column(tile, h):
    t = tile.astype(f32)
    k = 3 * h
    return t[..., k : k + 1] + t[..., k + 1 : k + 2] + t[..., k + 2 : k + 3]


def attention_kernel(last, place, q, chunk, *refs):
    me, zh, prior = place[0], place[1], place[2]
    zl, co = lax.shift_right_logical(me, 1), lax.bitwise_and(me, 1)
    if last:
        acc_in, peak_in, total_in, values, keep, send, keys, parts = refs
        zl, zh = 7 - zl, 1 - zh
    else:
        acc_out, peak_out, total_out, keys = refs

    for half in range(2):
        keys[half, :, :LATENT] = chunk[:, 32 * half : 32 * half + 32, :].reshape(512, LATENT)
        for g in range(16):
            for k in range(4):
                at = 32 * g + 8 * k
                keys[half, at : at + 8, LATENT:] = chunk[g, 64:72, 128 * k : 128 * (k + 1)]

    limit = prior + lax.broadcasted_iota(jnp.int32, (ROWS, 1), 0)
    n = lax.broadcasted_iota(jnp.int32, (1, 512), 1)
    slot = ((zl * 2 + co) * 32 + zh) * 64 + lax.shift_right_logical(n, 5) * 128 + lax.bitwise_and(n, 31)
    lses = []
    for h in range(HEADS):
        scores = []
        for half in range(2):
            s = lax.dot_general(
                q[half, h], keys[half], (((1,), (1,)), ((), ())), preferred_element_type=f32
            )
            scores.append(jnp.where(slot + 32 * half <= limit, s * LOG2_SCALE, NEG))
        peak = jnp.maximum(scores[0], scores[1]).max(axis=1, keepdims=True)
        if last:
            old = peak_in[h][:, :1]
            peak = jnp.maximum(peak, old)
            fade = jnp.exp2(old - peak)
            total = total_in[h][:, :1] * fade
            acc = acc_in[h] * fade
        else:
            total = jnp.zeros((ROWS, 1), f32)
            acc = jnp.zeros((ROWS, LATENT), f32)
        for half in range(2):
            p = jnp.exp2(scores[half] - peak)
            total = total + p.sum(axis=1, keepdims=True)
            acc = acc + jnp.dot(p.astype(bf16), keys[half, :, :LATENT], preferred_element_type=f32)
        if not last:
            acc_out[h] = acc
            peak_out[h] = jnp.broadcast_to(peak, (ROWS, 128))
            total_out[h] = jnp.broadcast_to(total, (ROWS, 128))
            continue
        latent = (acc / total).astype(bf16)
        o = jnp.dot(latent, values[h].reshape(LATENT, VALUE), preferred_element_type=f32).astype(bf16)
        for g in range(16):
            parts[g, h] = o[TOK * g : TOK * (g + 1)]
        lses.append(peak + jnp.log2(total))
    if last:
        tile = pack_lse(lses, (ROWS, 128))
        for g in range(16):
            parts[g, HEADS] = tile[TOK * g : TOK * (g + 1)]
        for g in range(8):
            keep[g] = parts[g * 2 + co]
            send[g] = parts[g * 2 + 1 - co]


def merge_heads(blocks):
    tile = blocks[HEADS]
    values, lses = [], []
    for h in range(HEADS):
        column = lse_column(tile, h)
        top = column.max(axis=0)
        w = jnp.exp2(column - top)
        total = w.sum(axis=0)
        values.append((blocks[h].astype(f32) * w).sum(axis=0) / total)
        lses.append(top + jnp.log2(total))
    return values, lses


def pair_kernel(place, a, b, out):
    rows = 8 * TOK
    blocks = [
        jnp.concatenate([r[:, h].reshape(1, rows, 128) for r in (a, b)], axis=0)
        for h in range(HEADS + 1)
    ]
    values, lses = merge_heads(blocks)
    for h in range(HEADS):
        out[:, h] = values[h].astype(bf16).reshape(8, TOK, 128)
    out[:, HEADS] = pack_lse(lses, (rows, 128)).reshape(8, TOK, 128)


def final_kernel(place, x, out):
    values, _ = merge_heads([x[:, h] for h in range(HEADS + 1)])
    for h in range(HEADS):
        out[:, h * VALUE : (h + 1) * VALUE] = values[h].astype(bf16)


def swap(x, d):
    return lax.ppermute(x, CTX, [(i, i ^ d) for i in range(16)])


def gather(x, axes, n):
    copies = jnp.broadcast_to(x[None], (n, *x.shape)).reshape(n * x.shape[0], *x.shape[1:])
    return lax.all_to_all(copies, axes, 0, 0, tiled=True)


def per_device(queries, cache, key_up_weight, value_up_weight, prior_len):
    me, zh = lax.axis_index(CTX), lax.axis_index("zh")
    place = jnp.concatenate([jnp.stack([me, zh]).astype(jnp.int32), prior_len])

    shard, pack = prepare(
        queries,
        cache,
        key_up_weight.transpose(0, 2, 1).reshape(128, 128),
        value_up_weight.transpose(0, 2, 1).reshape(128, 128),
    )

    mirror = lax.ppermute(shard, ("zq", "zr", "zh"), [(i, 15 - i) for i in range(16)])
    here = gather(shard, ("x", "y"), 16)
    pack2 = jnp.concatenate([pack, swap(pack, 8)], axis=0)
    mirror, later = lax.optimization_barrier((mirror, pack2))
    fans = [swap(later, 2), swap(later, 4), swap(later, 6)]
    mirror, here = lax.optimization_barrier((mirror, here))
    there = gather(mirror, ("x", "y"), 16)
    pack8 = jnp.concatenate([pack2] + fans, axis=0)


    q, wv = call(
        query_kernel,
        (shaped((2, HEADS, ROWS, WIDE)), shaped((HEADS, 16, 32, 128))),
        5,
        "query",
        (pltpu.VMEM((6, 16, TOK, 128), bf16), pltpu.VMEM((HEADS, 16, 32, 128), bf16)),
    )(place, pack2, *fans, swap(pack8, 1))

    def attend(last, shape, scratch, *operands):
        def kernel(*refs):
            attention_kernel(last, *refs)

        scratch = (pltpu.VMEM((2, 512, WIDE), bf16), *scratch)
        return call(kernel, shape, len(operands), f"attend{int(last)}", scratch)(place, *operands)

    state = (
        shaped((HEADS, ROWS, LATENT), f32),
        shaped((HEADS, ROWS, 128), f32),
        shaped((HEADS, ROWS, 128), f32),
    )
    run = attend(False, state, (), q, here)
    keep, send = attend(
        True,
        (shaped((8, HEADS + 1, TOK, 128)),) * 2,
        (pltpu.VMEM((16, HEADS + 1, TOK, 128), bf16),),
        q,
        there,
        *run,
        wv,
    )
    merged = call(pair_kernel, shaped((8, HEADS + 1, TOK, 128)), 2, "pair")(place, keep, swap(send, 1))
    spread = lax.all_to_all(merged, ZL, 0, 0, tiled=True)
    return call(final_kernel, shaped((TOK, HEADS * VALUE)), 1, "final")(place, spread)


def solution(mesh):
    fine = Mesh(mesh.devices.reshape(2, 4, 2, 4, 4, 2), ("zq", "zr", "co", "x", "y", "zh"))
    head = ("x", "y", "zh")
    return jax.shard_map(
        per_device,
        mesh=fine,
        in_specs=(P(CTX, head), P(CTX + head, None), P(head, None, CTX), P(head, None, CTX), P()),
        out_specs=P(CTX, head),
        check_vma=False,
    )
```

time: 113 us -> 112 us (level)
  the two profiles are of different devices: /device:TPU:12 before, /device:TPU:2 now
where the time goes in v4:
time: 112 us; the launch traced here: 111 us
  starting transfers between devices  48.3 us (43%)
  blocking collectives  19.3 us (17%)
  Pallas kernels  15.3 us (14%)
  waiting for transfers between devices  13.8 us (12%)
  local copies, waits for them, and re-layouts  13.4 us (12%)
    ppermute x6, starting transfers between devices, swap(): return lax.ppermute(x, CTX, [(i, i ^ d) for i in range(16)])  22.2 us
    all_to_all x1, blocking collectives, per_device(): spread = lax.all_to_all(merged, ZL, 0, 0, tiled=True)  19.3 us
    all_to_all x2, starting transfers between devices, gather(): return lax.all_to_all(copies, axes, 0, 0, tiled=True)  16.6 us
    ppermute x6, waiting for transfers between devices, swap(): return lax.ppermute(x, CTX, [(i, i ^ d) for i in range(16)])  13.8 us
    unnamed x28, local copies, waits for them, and re-layouts  11.1 us
    pallas_call x2, Pallas kernels, attend(): call(kernel, shape, len(operands), f'attend{int(last)}', scratch)  10.8 us
    ppermute x1, starting transfers between devices, per_device(): lax.ppermute(shard, ('zq', 'zr', 'zh'), [(i, 15 - i) for i in range(16)])  9.45 us
    reshape x2, local copies, waits for them, and re-layouts, gather(): jnp.broadcast_to(x[None], (n, *x.shape))  2.29 us
  transfers between devices with their start and end apart: 9, of which 4 were waited for; matrix products, arithmetic and copies ran while one was open for 1% of the time, Pallas kernels for 5%

profile of v4, /device:TPU:2, one launch (start us, length us, event | category | flops | bytes accessed | tf_op | source)
XLA Modules:
  0.0 111.0 jit_solution(16675831741919260226)
XLA Ops:
  0.0 1.0 prepare.1
  1.0 1.1 %reshape.20 = bf16[16,72,512]{2,1,0:T(8,128)(2,1)} broadcast(bf16[72,512]{1,0:T(8,128)(2,1)S(1)} %bitcast.10), dimensions={1,2} | broadcast | bytes 1253376 | tf_op jit(solution)/shard_map/reshape | solution.py:252
  2.1 9.4 %all-to-all-start = ((bf16[16,72,512]{2,1,0:T(8,128)(2,1)}), bf16[16,72,512]{2,1,0:T(8,128)(2,1)S(1)}, u32[]{:S(2)}, u32[]{:S(2)}) async-start(bf16[16,72,512]{2,1,0:T(8,128)(2,1)} %reshape.20), calls=%async_computation | async-start | bytes 2359296 | tf_op jit(solution)/shard_map/all_to_all | solution.py:253
  11.6 9.5 %collective-permute-start.1 = (bf16[1,72,512]{2,1,0:T(8,128)(2,1)S(1)}, bf16[1,72,512]{2,1,0:T(8,128)(2,1)S(1)}, u32[]{:S(2)}, u32[]{:S(2)}) collective-permute-start(bf16[1,72,512]{2,1,0:T(8,128)(2,1)S(1)} %get-tuple-element.19), channel_id=1, source_target_pairs={{0,449},{1,448},{64,385},{65,384},{128,321},{129,320},{192,257},{1... | collective-permute-start | bytes 221192 | tf_op jit(solution)/shard_map/ppermute | solution.py:267
  21.0 8.2 %collective-permute-start = (bf16[1,352,128]{2,1,0:T(8,128)(2,1)S(1)}, bf16[1,352,128]{2,1,0:T(8,128)(2,1)S(1)}, u32[]{:S(2)}, u32[]{:S(2)}) collective-permute-start(bf16[1,352,128]{2,1,0:T(8,128)(2,1)S(1)} %get-tuple-element.18), channel_id=1, source_target_pairs={{0,256},{32,288},{64,320},{96,352},{128,384},{160,416},{192,448},{... | collective-permute-start | bytes 270344 | tf_op jit(solution)/shard_map/ppermute | solution.py:248
  29.2 7.6 %collective-permute-done = bf16[1,352,128]{2,1,0:T(8,128)(2,1)S(1)} collective-permute-done((bf16[1,352,128]{2,1,0:T(8,128)(2,1)S(1)}, bf16[1,352,128]{2,1,0:T(8,128)(2,1)S(1)}, u32[]{:S(2)}, u32[]{:S(2)}) %collective-permute-start) | collective-permute-done | bytes 90144 | tf_op jit(solution)/shard_map/ppermute | solution.py:248
  36.9 0.0 collective-permute-done.1
  36.9 1.9 %collective-permute-start.2 = (bf16[2,352,128]{2,1,0:T(8,128)(2,1)S(1)}, bf16[2,352,128]{2,1,0:T(8,128)(2,1)S(1)}, u32[]{:S(2)}, u32[]{:S(2)}) collective-permute-start(bf16[2,352,128]{2,1,0:T(8,128)(2,1)S(1)} %get-tuple-element.20.p0), channel_id=1, source_target_pairs={{0,64},{32,96},{64,0},{96,32},{128,192},{160,224},{192,128},{224,1... | collective-permute-start | bytes 540680 | tf_op jit(solution)/shard_map/ppermute | solution.py:248
  38.8 1.9 %collective-permute-start.3 = (bf16[2,352,128]{2,1,0:T(8,128)(2,1)S(1)}, bf16[2,352,128]{2,1,0:T(8,128)(2,1)S(1)}, u32[]{:S(2)}, u32[]{:S(2)}) collective-permute-start(bf16[2,352,128]{2,1,0:T(8,128)(2,1)S(1)} %get-tuple-element.20.p0), channel_id=1, source_target_pairs={{0,128},{32,160},{64,192},{96,224},{128,0},{160,32},{192,64},{224,... | collective-permute-start | bytes 540680 | tf_op jit(solution)/shard_map/ppermute | solution.py:248
  40.7 0.0 all-to-all-done.refs_2_
  40.8 0.0 copy-start
  40.8 1.2 %reshape.21 = bf16[16,72,512]{2,1,0:T(8,128)(2,1)} broadcast(bf16[72,512]{1,0:T(8,128)(2,1)S(1)} %bitcast.11), dimensions={1,2} | broadcast | bytes 1253376 | tf_op jit(solution)/shard_map/reshape | solution.py:252
  41.9 0.3 copy-done
  42.2 7.2 %all-to-all-start.1 = ((bf16[16,72,512]{2,1,0:T(8,128)(2,1)}), bf16[16,72,512]{2,1,0:T(8,128)(2,1)}, u32[]{:S(2)}, u32[]{:S(2)}) async-start(bf16[16,72,512]{2,1,0:T(8,128)(2,1)} %reshape.21), calls=%async_computation.1 | async-start | bytes 2359296 | tf_op jit(solution)/shard_map/all_to_all | solution.py:253
  49.4 6.3 %collective-permute-start.4 = (bf16[2,352,128]{2,1,0:T(8,128)(2,1)S(1)}, bf16[2,352,128]{2,1,0:T(8,128)(2,1)S(1)}, u32[]{:S(2)}, u32[]{:S(2)}) collective-permute-start(bf16[2,352,128]{2,1,0:T(8,128)(2,1)S(1)} %get-tuple-element.20.p0), channel_id=1, source_target_pairs={{0,192},{32,224},{64,128},{96,160},{128,64},{160,96},{192,0},{224,... | collective-permute-start | bytes 540680 | tf_op jit(solution)/shard_map/ppermute | solution.py:248
  55.7 0.0 collective-permute-done.2.p1
  55.7 0.0 collective-permute-done.3.p2
  55.8 3.5 %collective-permute-done.4.p3 = bf16[2,352,128]{2,1,0:T(8,128)(2,1)S(1)} collective-permute-done((bf16[2,352,128]{2,1,0:T(8,128)(2,1)S(1)}, bf16[2,352,128]{2,1,0:T(8,128)(2,1)S(1)}, u32[]{:S(2)}, u32[]{:S(2)}) %collective-permute-start.4) | collective-permute-done | bytes 180256 | tf_op jit(solution)/shard_map/ppermute | solution.py:248
  59.3 1.9 %collective-permute-start.5 = (bf16[8,352,128]{2,1,0:T(8,128)(2,1)S(1)}, bf16[8,352,128]{2,1,0:T(8,128)(2,1)S(1)}, u32[]{:S(2)}, u32[]{:S(2)}) collective-permute-start(bf16[8,352,128]{2,1,0:T(8,128)(2,1)S(1)} %constant_dynamic-update-slice_fusion.2), channel_id=1, source_target_pairs={{0,32},{32,0},{64,96},{96,64},{128,160},{160,128},{192,224},{224,1... | collective-permute-start | bytes 2162696 | tf_op jit(solution)/shard_map/ppermute | solution.py:248
  61.9 0.1 pad_add_fusion.place.refs_0_
  61.9 1.4 %collective-permute-done.5.p4 = bf16[8,352,128]{2,1,0:T(8,128)(2,1)S(1)} collective-permute-done((bf16[8,352,128]{2,1,0:T(8,128)(2,1)S(1)}, bf16[8,352,128]{2,1,0:T(8,128)(2,1)S(1)}, u32[]{:S(2)}, u32[]{:S(2)}) %collective-permute-start.5) | collective-permute-done | bytes 720928 | tf_op jit(solution)/shard_map/ppermute | solution.py:248
  63.4 0.0 copy-start.4
  63.4 0.9 copy-done.4
  64.2 0.0 copy-start.5
  64.3 1.1 copy-done.5
  65.4 1.1 query.1
  66.5 0.0 copy-start.6
  66.5 0.8 copy-done.6
  67.2 0.0 copy-start.1
  67.2 1.3 %copy-done.1 = bf16[16,72,512]{2,1,0:T(8,128)(2,1)S(1)} copy-done((bf16[16,72,512]{2,1,0:T(8,128)(2,1)S(1)}, bf16[16,72,512]{2,1,0:T(8,128)(2,1)}, u32[]{:S(2)}) %copy-start.1) | copy-done | bytes 1179672
  68.5 0.0 copy-start.7
  68.5 4.4 %attend0.1 = (f32[4,256,512]{2,1,0:T(8,128)S(1)}, f32[4,256,128]{2,1,0:T(8,128)S(1)}, f32[4,256,128]{2,1,0:T(8,128)S(1)}) custom-call(s32[3]{0:T(128)S(1)} %pad_add_fusion.place.refs_0_, bf16[2,4,256,640]{3,2,1,0:T(8,128)(2,1)S(1)} %get-tuple-element.21.refs_1_, bf16[16,72,512]{2,1,0:T(8,128)(2,1)S(1)} %copy-done.1), custom_call_target="tpu_custom_call" | custom-call | flops 1 | bytes 1 | tf_op jit(solution)/shard_map/attend0/pallas_call | solution.py:290
  72.9 0.0 copy-start.2
  72.9 1.3 %copy-done.2 = f32[4,256,512]{2,1,0:T(8,128)} copy-done((f32[4,256,512]{2,1,0:T(8,128)}, f32[4,256,512]{2,1,0:T(8,128)S(1)}, u32[]{:S(2)}) %copy-start.2) | copy-done | bytes 2097176
  74.3 0.0 copy-start.8
  74.3 0.8 copy-done.8
  75.1 0.0 copy-start.10
  75.1 0.8 copy-done.10
  75.9 0.0 all-to-all-done.1.refs_2_
  75.9 0.0 copy-done.7
  75.9 0.0 copy-start.3
  75.9 1.6 %copy-done.3 = f32[4,256,512]{2,1,0:T(8,128)S(1)} copy-done((f32[4,256,512]{2,1,0:T(8,128)S(1)}, f32[4,256,512]{2,1,0:T(8,128)}, u32[]{:S(2)}) %copy-start.3) | copy-done | bytes 2097176
  77.5 0.0 copy-start.9
  77.5 1.0 copy-done.9
  78.6 0.0 copy-start.11
  78.6 1.0 copy-done.11
  79.6 6.4 %attend1.1 = (bf16[8,5,16,128]{3,2,1,0:T(8,128)(2,1)S(1)}, bf16[8,5,16,128]{3,2,1,0:T(8,128)(2,1)S(1)}) custom-call(s32[3]{0:T(128)S(1)} %pad_add_fusion.place.refs_0_, bf16[2,4,256,640]{3,2,1,0:T(8,128)(2,1)S(1)} %get-tuple-element.21.refs_1_, bf16[16,72,512]{2,1,0:T(8,128)(2,1)} %all-to-all-done.1.refs_2_, f32[4,256,512]{2,1,0:T(8,128)S(1)} %copy-done.3, ...), custom_call_target="tpu_custom_call" | custom-call | flops 1 | bytes 1 | tf_op jit(solution)/shard_map/attend1/pallas_call | solution.py:290
  86.0 2.0 %collective-permute-start.6 = (bf16[8,5,16,128]{3,2,1,0:T(8,128)(2,1)S(1)}, bf16[8,5,16,128]{3,2,1,0:T(8,128)(2,1)S(1)}, u32[]{:S(2)}, u32[]{:S(2)}) collective-permute-start(bf16[8,5,16,128]{3,2,1,0:T(8,128)(2,1)S(1)} %get-tuple-element.30), channel_id=1, source_target_pairs={{0,32},{32,0},{64,96},{96,64},{128,160},{160,128},{192,224},{224,1... | collective-permute-start | bytes 491528 | tf_op jit(solution)/shard_map/ppermute | solution.py:248
  88.0 1.2 %collective-permute-done.6.b = bf16[8,5,16,128]{3,2,1,0:T(8,128)(2,1)S(1)} collective-permute-done((bf16[8,5,16,128]{3,2,1,0:T(8,128)(2,1)S(1)}, bf16[8,5,16,128]{3,2,1,0:T(8,128)(2,1)S(1)}, u32[]{:S(2)}, u32[]{:S(2)}) %collective-permute-start.6) | collective-permute-done | bytes 163872 | tf_op jit(solution)/shard_map/ppermute | solution.py:248
  89.3 1.0 pair.1
  90.3 19.3 %all_to_all.15.x = bf16[8,5,16,128]{3,2,1,0:T(8,128)(2,1)S(1)} all-to-all(bf16[8,5,16,128]{3,2,1,0:T(8,128)(2,1)S(1)} %pair.1), channel_id=1, replica_groups=mesh['zq'=2,'zr'=4,'co'=2,'x'=4,'y'=4,'zh'=2] {'zq','zr'}, dimensions={0} | all-to-all | bytes 327680 | tf_op jit(solution)/shard_map/all_to_all | solution.py:308
  109.6 1.4 %final.1 = bf16[16,512]{1,0:T(8,128)(2,1)} custom-call(s32[3]{0:T(128)S(1)} %pad_add_fusion.place.refs_0_, bf16[8,5,16,128]{3,2,1,0:T(8,128)(2,1)S(1)} %all_to_all.15.x), custom_call_target="tpu_custom_call" | custom-call | flops 1 | bytes 1 | tf_op jit(solution)/shard_map/final/pallas_call | solution.py:309
  (5 shorter events, 0.1 us)
Async XLA Ops:
  2.1 38.6 %all-to-all-start = ((bf16[16,72,512]{2,1,0:T(8,128)(2,1)}), bf16[16,72,512]{2,1,0:T(8,128)(2,1)S(1)}, u32[]{:S(2)}, u32[]{:S(2)}) async-start(bf16[16,72,512]{2,1,0:T(8,128)(2,1)} %reshape.20), calls=%async_computation | async-start | bytes 2359296 | tf_op jit(solution)/shard_map/all_to_all | solution.py:253
  11.6 25.3 %collective-permute-start.1 = (bf16[1,72,512]{2,1,0:T(8,128)(2,1)S(1)}, bf16[1,72,512]{2,1,0:T(8,128)(2,1)S(1)}, u32[]{:S(2)}, u32[]{:S(2)}) collective-permute-start(bf16[1,72,512]{2,1,0:T(8,128)(2,1)S(1)} %get-tuple-element.19), channel_id=1, source_target_pairs={{0,449},{1,448},{64,385},{65,384},{128,321},{129,320},{192,257},{1... | collective-permute-start | bytes 221192 | tf_op jit(solution)/shard_map/ppermute | solution.py:267
  21.0 15.8 %collective-permute-start = (bf16[1,352,128]{2,1,0:T(8,128)(2,1)S(1)}, bf16[1,352,128]{2,1,0:T(8,128)(2,1)S(1)}, u32[]{:S(2)}, u32[]{:S(2)}) collective-permute-start(bf16[1,352,128]{2,1,0:T(8,128)(2,1)S(1)} %get-tuple-element.18), channel_id=1, source_target_pairs={{0,256},{32,288},{64,320},{96,352},{128,384},{160,416},{192,448},{... | collective-permute-start | bytes 270344 | tf_op jit(solution)/shard_map/ppermute | solution.py:248
  36.9 18.8 %collective-permute-start.2 = (bf16[2,352,128]{2,1,0:T(8,128)(2,1)S(1)}, bf16[2,352,128]{2,1,0:T(8,128)(2,1)S(1)}, u32[]{:S(2)}, u32[]{:S(2)}) collective-permute-start(bf16[2,352,128]{2,1,0:T(8,128)(2,1)S(1)} %get-tuple-element.20.p0), channel_id=1, source_target_pairs={{0,64},{32,96},{64,0},{96,32},{128,192},{160,224},{192,128},{224,1... | collective-permute-start | bytes 540680 | tf_op jit(solution)/shard_map/ppermute | solution.py:248
  38.8 16.9 %collective-permute-start.3 = (bf16[2,352,128]{2,1,0:T(8,128)(2,1)S(1)}, bf16[2,352,128]{2,1,0:T(8,128)(2,1)S(1)}, u32[]{:S(2)}, u32[]{:S(2)}) collective-permute-start(bf16[2,352,128]{2,1,0:T(8,128)(2,1)S(1)} %get-tuple-element.20.p0), channel_id=1, source_target_pairs={{0,128},{32,160},{64,192},{96,224},{128,0},{160,32},{192,64},{224,... | collective-permute-start | bytes 540680 | tf_op jit(solution)/shard_map/ppermute | solution.py:248
  40.8 1.4 %copy-start = (bf16[16,72,512]{2,1,0:T(8,128)(2,1)}, bf16[16,72,512]{2,1,0:T(8,128)(2,1)S(1)}, u32[]{:S(2)}) copy-start(bf16[16,72,512]{2,1,0:T(8,128)(2,1)S(1)} %all-to-all-done.refs_2_) | copy-start | bytes 3538948
  42.2 33.7 %all-to-all-start.1 = ((bf16[16,72,512]{2,1,0:T(8,128)(2,1)}), bf16[16,72,512]{2,1,0:T(8,128)(2,1)}, u32[]{:S(2)}, u32[]{:S(2)}) async-start(bf16[16,72,512]{2,1,0:T(8,128)(2,1)} %reshape.21), calls=%async_computation.1 | async-start | bytes 2359296 | tf_op jit(solution)/shard_map/all_to_all | solution.py:253
  49.4 9.8 %collective-permute-start.4 = (bf16[2,352,128]{2,1,0:T(8,128)(2,1)S(1)}, bf16[2,352,128]{2,1,0:T(8,128)(2,1)S(1)}, u32[]{:S(2)}, u32[]{:S(2)}) collective-permute-start(bf16[2,352,128]{2,1,0:T(8,128)(2,1)S(1)} %get-tuple-element.20.p0), channel_id=1, source_target_pairs={{0,192},{32,224},{64,128},{96,160},{128,64},{160,96},{192,0},{224,... | collective-permute-start | bytes 540680 | tf_op jit(solution)/shard_map/ppermute | solution.py:248
  59.3 4.1 %collective-permute-start.5 = (bf16[8,352,128]{2,1,0:T(8,128)(2,1)S(1)}, bf16[8,352,128]{2,1,0:T(8,128)(2,1)S(1)}, u32[]{:S(2)}, u32[]{:S(2)}) collective-permute-start(bf16[8,352,128]{2,1,0:T(8,128)(2,1)S(1)} %constant_dynamic-update-slice_fusion.2), channel_id=1, source_target_pairs={{0,32},{32,0},{64,96},{96,64},{128,160},{160,128},{192,224},{224,1... | collective-permute-start | bytes 2162696 | tf_op jit(solution)/shard_map/ppermute | solution.py:248
  63.4 0.9 copy-start.4
  64.2 1.1 copy-start.5
  66.5 0.8 copy-start.6
  67.2 1.3 %copy-start.1 = (bf16[16,72,512]{2,1,0:T(8,128)(2,1)S(1)}, bf16[16,72,512]{2,1,0:T(8,128)(2,1)}, u32[]{:S(2)}) copy-start(bf16[16,72,512]{2,1,0:T(8,128)(2,1)} %copy-done) | copy-start | bytes 3538948
  68.5 7.4 %copy-start.7 = (bf16[4,16,32,128]{3,2,1,0:T(8,128)(2,1)S(1)}, bf16[4,16,32,128]{3,2,1,0:T(8,128)(2,1)}, u32[]{:S(2)}) copy-start(bf16[4,16,32,128]{3,2,1,0:T(8,128)(2,1)} %copy-done.6) | copy-start | bytes 1572868
  72.9 1.3 %copy-start.2 = (f32[4,256,512]{2,1,0:T(8,128)}, f32[4,256,512]{2,1,0:T(8,128)S(1)}, u32[]{:S(2)}) copy-start(f32[4,256,512]{2,1,0:T(8,128)S(1)} %get-tuple-element.25.refs_3_) | copy-start | bytes 6291460
  74.3 0.8 copy-start.8
  75.1 0.8 copy-start.10
  75.9 1.6 %copy-start.3 = (f32[4,256,512]{2,1,0:T(8,128)S(1)}, f32[4,256,512]{2,1,0:T(8,128)}, u32[]{:S(2)}) copy-start(f32[4,256,512]{2,1,0:T(8,128)} %copy-done.2) | copy-start | bytes 6291460
  77.5 1.0 copy-start.9
  78.6 1.0 copy-start.11
  86.0 3.3 %collective-permute-start.6 = (bf16[8,5,16,128]{3,2,1,0:T(8,128)(2,1)S(1)}, bf16[8,5,16,128]{3,2,1,0:T(8,128)(2,1)S(1)}, u32[]{:S(2)}, u32[]{:S(2)}) collective-permute-start(bf16[8,5,16,128]{3,2,1,0:T(8,128)(2,1)S(1)} %get-tuple-element.30), channel_id=1, source_target_pairs={{0,32},{32,0},{64,96},{96,64},{128,160},{160,128},{192,224},{224,1... | collective-permute-start | bytes 491528 | tf_op jit(solution)/shard_map/ppermute | solution.py:248

commit v5 on v4

--- a/solution.py
+++ b/solution.py
@@ -18,7 +18,8 @@
 ROWS = 256
 NEG = -1e30
 LOG2_SCALE = (PLAIN + ROT) ** (-0.5) * math.log2(math.e)
-VMEM_LIMIT = 40 * 1024 * 1024
+SLOTS = 1024
+MIB = 1024 * 1024
 
 ZL = ("zq", "zr")
 CTX = ("zq", "zr", "co")
@@ -30,14 +31,14 @@
     return pl.BlockSpec(memory_space=pltpu.VMEM)
 
 
-def call(kernel, shape, n_in, name, scratch=()):
+def call(kernel, shape, n_in, name, scratch=(), room=8):
     return pl.pallas_call(
         kernel,
         out_shape=shape,
         in_specs=[pl.BlockSpec(memory_space=pltpu.SMEM)] + [vmem()] * n_in,
         out_specs=jax.tree.map(lambda _: vmem(), shape),
         scratch_shapes=list(scratch),
-        compiler_params=pltpu.CompilerParams(vmem_limit_bytes=VMEM_LIMIT),
+        compiler_params=pltpu.CompilerParams(vmem_limit_bytes=room * MIB),
         cost_estimate=pl.CostEstimate(flops=1, transcendentals=0, bytes_accessed=1),
         name=name,
     )
@@ -85,30 +86,36 @@
             pltpu.VMEM(cache.shape, bf16),
             pltpu.SemaphoreType.DMA((4,)),
         ],
-        compiler_params=pltpu.CompilerParams(vmem_limit_bytes=VMEM_LIMIT),
+        compiler_params=pltpu.CompilerParams(vmem_limit_bytes=4 * MIB),
         name="prepare",
     )(*(pltpu.with_memory_space_constraint(v, pltpu.HBM) for v in (queries, cache, wk, wv)))
 
 
-def query_kernel(place, p0, p1, p2, p3, p4, q_out, wv_out, pieces, panel):
-    me = place[0]
-    sources = [
-        (ref, i, lax.bitwise_xor(me, flip))
-        for ref, flips in (
-            (p0, (0, 8)),
-            (p1, (2, 10)),
-            (p2, (4, 12)),
-            (p3, (6, 14)),
-            (p4, (1, 9, 3, 11, 5, 13, 7, 15)),
-        )
-        for i, flip in enumerate(flips)
+def query_kernel(place, *refs):
+    inputs, (lat_out, rot_out, wv_out), (tiles, pieces, panel, lats, rots, values, sems) = (
+        refs[:5],
+        refs[5:8],
+        refs[8:],
+    )
+    flips = ((0, 8), (2, 10), (4, 12), (6, 14), (1, 9, 3, 11, 5, 13, 7, 15))
+    starts = (0, 2, 4, 6, 8)
+    loads = [
+        pltpu.make_async_copy(ref, tiles.at[at : at + len(f)], sems.at[n])
+        for n, (ref, at, f) in enumerate(zip(inputs, starts, flips))
     ]
-    for ref, i, src in sources:
-        for k in range(6):
-            pieces[k, src] = ref[i, TOK * k : TOK * (k + 1), :]
-        for h in range(HEADS):
-            panel[h, src] = ref[i, 96 + 32 * h : 128 + 32 * h, :]
-            wv_out[h, src] = ref[i, 224 + 32 * h : 256 + 32 * h, :]
+    for c in loads:
+        c.start()
+    for c, at, flip in zip(loads, starts, flips):
+        c.wait()
+        for i, d in enumerate(flip):
+            src = lax.bitwise_xor(place[0], d)
+            for k in range(6):
+                pieces[k, src] = tiles[at + i, TOK * k : TOK * (k + 1), :]
+            for h in range(HEADS):
+                panel[h, src] = tiles[at + i, 96 + 32 * h : 128 + 32 * h, :]
+                values[h, src] = tiles[at + i, 224 + 32 * h : 256 + 32 * h, :]
+    stores = [pltpu.make_async_copy(values, wv_out, sems.at[5])]
+    stores[0].start()
     zero = jnp.zeros((ROWS, ROT), bf16)
     for h in range(HEADS):
         k = (h // 2) * 3
@@ -118,16 +125,45 @@
         else:
             plain = jnp.concatenate([tile[1][:, ROT:], tile[2][:, :ROT]], axis=1)
             rot = tile[2][:, ROT:]
-        lat = lax.dot_general(
+        rots[0, h] = jnp.concatenate([rot, zero], axis=1)
+        rots[1, h] = jnp.concatenate([zero, rot], axis=1)
+        lats[h] = lax.dot_general(
             plain,
             panel[h].reshape(LATENT, PLAIN),
             (((1,), (1,)), ((), ())),
             preferred_element_type=f32,
         ).astype(bf16)
-        for half in range(2):
-            q_out[half, h, :, :LATENT] = lat
-        q_out[0, h, :, LATENT:] = jnp.concatenate([rot, zero], axis=1)
-        q_out[1, h, :, LATENT:] = jnp.concatenate([zero, rot], axis=1)
+        stores.append(pltpu.make_async_copy(lats.at[h], lat_out.at[h], sems.at[6 + h]))
+        stores[-1].start()
+    stores.append(pltpu.make_async_copy(rots, rot_out, sems.at[10]))
+    stores[-1].start()
+    for c in stores:
+        c.wait()
+
+
+def project_queries(place, *pieces):
+    hbm = pl.BlockSpec(memory_space=pltpu.HBM)
+    return pl.pallas_call(
+        query_kernel,
+        out_shape=(
+            pltpu.HBM((HEADS, ROWS, LATENT), bf16),
+            pltpu.HBM((2, HEADS, ROWS, 2 * ROT), bf16),
+            pltpu.HBM((HEADS, 16, 32, 128), bf16),
+        ),
+        in_specs=[pl.BlockSpec(memory_space=pltpu.SMEM)] + [hbm] * 5,
+        out_specs=(hbm,) * 3,
+        scratch_shapes=[
+            pltpu.VMEM((16, 352, 128), bf16),
+            pltpu.VMEM((6, 16, TOK, 128), bf16),
+            pltpu.VMEM((HEADS, 16, 32, 128), bf16),
+            pltpu.VMEM((HEADS, ROWS, LATENT), bf16),
+            pltpu.VMEM((2, HEADS, ROWS, 2 * ROT), bf16),
+            pltpu.VMEM((HEADS, 16, 32, 128), bf16),
+            pltpu.SemaphoreType.DMA((11,)),
+        ],
+        compiler_params=pltpu.CompilerParams(vmem_limit_bytes=16 * MIB),
+        name="query",
+    )(place, *(pltpu.with_memory_space_constraint(p, pltpu.HBM) for p in pieces))
 
 
 def split3(x):
@@ -153,64 +189,80 @@
     return t[..., k : k + 1] + t[..., k + 1 : k + 2] + t[..., k + 2 : k + 3]
 
 
-def attention_kernel(last, place, q, chunk, *refs):
+def attention_kernel(place, lat_hbm, rot_hbm, wv_hbm, chunk, keep, send, keys, parts, lats, rots, values, sems):
     me, zh, prior = place[0], place[1], place[2]
     zl, co = lax.shift_right_logical(me, 1), lax.bitwise_and(me, 1)
-    if last:
-        acc_in, peak_in, total_in, values, keep, send, keys, parts = refs
-        zl, zh = 7 - zl, 1 - zh
-    else:
-        acc_out, peak_out, total_out, keys = refs
-
+    loads = [
+        pltpu.make_async_copy(rot_hbm, rots, sems.at[0]),
+        *(pltpu.make_async_copy(lat_hbm.at[h], lats.at[h], sems.at[1 + h]) for h in range(HEADS)),
+        pltpu.make_async_copy(wv_hbm, values, sems.at[1 + HEADS]),
+    ]
+    for c in loads:
+        c.start()
     for half in range(2):
-        keys[half, :, :LATENT] = chunk[:, 32 * half : 32 * half + 32, :].reshape(512, LATENT)
-        for g in range(16):
+        keys[half, :, :LATENT] = chunk[:, 32 * half : 32 * half + 32, :].reshape(SLOTS, LATENT)
+        for g in range(32):
             for k in range(4):
                 at = 32 * g + 8 * k
                 keys[half, at : at + 8, LATENT:] = chunk[g, 64:72, 128 * k : 128 * (k + 1)]
 
     limit = prior + lax.broadcasted_iota(jnp.int32, (ROWS, 1), 0)
-    n = lax.broadcasted_iota(jnp.int32, (1, 512), 1)
-    slot = ((zl * 2 + co) * 32 + zh) * 64 + lax.shift_right_logical(n, 5) * 128 + lax.bitwise_and(n, 31)
+    n = lax.broadcasted_iota(jnp.int32, (1, SLOTS), 1)
+    near = ((zl * 2 + co) * 32 + zh) * 64
+    far = (((7 - zl) * 2 + co) * 32 + 1 - zh) * 64
+    slot = lax.shift_right_logical(n, 6) * 128 + lax.bitwise_and(n, 31)
+    slot = slot + jnp.where(lax.bitwise_and(n, 32) == 0, near, far)
     lses = []
-    for h in range(HEADS):
+    loads[0].wait()
+    for h in range(HEADS):
+        loads[1 + h].wait()
         scores = []
         for half in range(2):
+            q = jnp.concatenate([lats[h], rots[half, h]], axis=1)
             s = lax.dot_general(
-                q[half, h], keys[half], (((1,), (1,)), ((), ())), preferred_element_type=f32
+                q, keys[half], (((1,), (1,)), ((), ())), preferred_element_type=f32
             )
             scores.append(jnp.where(slot + 32 * half <= limit, s * LOG2_SCALE, NEG))
         peak = jnp.maximum(scores[0], scores[1]).max(axis=1, keepdims=True)
-        if last:
-            old = peak_in[h][:, :1]
-            peak = jnp.maximum(peak, old)
-            fade = jnp.exp2(old - peak)
-            total = total_in[h][:, :1] * fade
-            acc = acc_in[h] * fade
-        else:
-            total = jnp.zeros((ROWS, 1), f32)
-            acc = jnp.zeros((ROWS, LATENT), f32)
+        total = jnp.zeros((ROWS, 1), f32)
+        acc = jnp.zeros((ROWS, LATENT), f32)
         for half in range(2):
             p = jnp.exp2(scores[half] - peak)
             total = total + p.sum(axis=1, keepdims=True)
             acc = acc + jnp.dot(p.astype(bf16), keys[half, :, :LATENT], preferred_element_type=f32)
-        if not last:
-            acc_out[h] = acc
-            peak_out[h] = jnp.broadcast_to(peak, (ROWS, 128))
-            total_out[h] = jnp.broadcast_to(total, (ROWS, 128))
-            continue
+        if h == 0:
+            loads[1 + HEADS].wait()
         latent = (acc / total).astype(bf16)
         o = jnp.dot(latent, values[h].reshape(LATENT, VALUE), preferred_element_type=f32).astype(bf16)
         for g in range(16):
             parts[g, h] = o[TOK * g : TOK * (g + 1)]
         lses.append(peak + jnp.log2(total))
-    if last:
-        tile = pack_lse(lses, (ROWS, 128))
-        for g in range(16):
-            parts[g, HEADS] = tile[TOK * g : TOK * (g + 1)]
-        for g in range(8):
-            keep[g] = parts[g * 2 + co]
-            send[g] = parts[g * 2 + 1 - co]
+    tile = pack_lse(lses, (ROWS, 128))
+    for g in range(16):
+        parts[g, HEADS] = tile[TOK * g : TOK * (g + 1)]
+    for g in range(8):
+        keep[g] = parts[g * 2 + co]
+        send[g] = parts[g * 2 + 1 - co]
+
+
+def attend(place, lat, rot, wv, slots):
+    hbm = pl.BlockSpec(memory_space=pltpu.HBM)
+    return pl.pallas_call(
+        attention_kernel,
+        out_shape=(shaped((8, HEADS + 1, TOK, 128)),) * 2,
+        in_specs=[pl.BlockSpec(memory_space=pltpu.SMEM)] + [hbm] * 3 + [vmem()],
+        out_specs=(vmem(), vmem()),
+        scratch_shapes=[
+            pltpu.VMEM((2, SLOTS, WIDE), bf16),
+            pltpu.VMEM((16, HEADS + 1, TOK, 128), bf16),
+            pltpu.VMEM(lat.shape, bf16),
+            pltpu.VMEM(rot.shape, bf16),
+            pltpu.VMEM(wv.shape, bf16),
+            pltpu.SemaphoreType.DMA((2 + HEADS,)),
+        ],
+        compiler_params=pltpu.CompilerParams(vmem_limit_bytes=24 * MIB),
+        name="attention",
+    )(place, *(pltpu.with_memory_space_constraint(v, pltpu.HBM) for v in (lat, rot, wv)), slots)
 
 
 def merge_heads(blocks):
@@ -265,45 +317,16 @@
     )
 
     mirror = lax.ppermute(shard, ("zq", "zr", "zh"), [(i, 15 - i) for i in range(16)])
-    here = gather(shard, ("x", "y"), 16)
     pack2 = jnp.concatenate([pack, swap(pack, 8)], axis=0)
-    mirror, later = lax.optimization_barrier((mirror, pack2))
-    fans = [swap(later, 2), swap(later, 4), swap(later, 6)]
-    mirror, here = lax.optimization_barrier((mirror, here))
-    there = gather(mirror, ("x", "y"), 16)
+    mirror, pack2 = lax.optimization_barrier((mirror, pack2))
+    pair = jnp.concatenate([shard, mirror], axis=0)
+    slots = gather(pair, ("x", "y"), 16)
+    fans = [swap(pack2, d) for d in (2, 4, 6)]
     pack8 = jnp.concatenate([pack2] + fans, axis=0)
 
 
-    q, wv = call(
-        query_kernel,
-        (shaped((2, HEADS, ROWS, WIDE)), shaped((HEADS, 16, 32, 128))),
-        5,
-        "query",
-        (pltpu.VMEM((6, 16, TOK, 128), bf16), pltpu.VMEM((HEADS, 16, 32, 128), bf16)),
-    )(place, pack2, *fans, swap(pack8, 1))
-
-    def attend(last, shape, scratch, *operands):
-        def kernel(*refs):
-            attention_kernel(last, *refs)
-
-        scratch = (pltpu.VMEM((2, 512, WIDE), bf16), *scratch)
-        return call(kernel, shape, len(operands), f"attend{int(last)}", scratch)(place, *operands)
-
-    state = (
-        shaped((HEADS, ROWS, LATENT), f32),
-        shaped((HEADS, ROWS, 128), f32),
-        shaped((HEADS, ROWS, 128), f32),
-    )
-    run = attend(False, state, (), q, here)
-    keep, send = attend(
-        True,
-        (shaped((8, HEADS + 1, TOK, 128)),) * 2,
-        (pltpu.VMEM((16, HEADS + 1, TOK, 128), bf16),),
-        q,
-        there,
-        *run,
-        wv,
-    )
+    queries = project_queries(place, pack2, *fans, swap(pack8, 1))
+    keep, send = attend(place, *queries, slots)
     merged = call(pair_kernel, shaped((8, HEADS + 1, TOK, 128)), 2, "pair")(place, keep, swap(send, 1))
     spread = lax.all_to_all(merged, ZL, 0, 0, tiled=True)
     return call(final_kernel, shaped((TOK, HEADS * VALUE)), 1, "final")(place, spread)

time: 112 us -> 104 us (0.929)
  the two profiles are of different devices: /device:TPU:2 before, /device:TPU:1 now
where the time goes in v5:
time: 104 us; the launch traced here: 103 us
  starting transfers between devices  45.1 us (43%)
  blocking collectives  20.9 us (20%)
  Pallas kernels  17.8 us (17%)
  waiting for transfers between devices  16.2 us (16%)
  local copies, waits for them, and re-layouts  1.7 us (2%)
    ppermute x6, starting transfers between devices, swap(): return lax.ppermute(x, CTX, [(i, i ^ d) for i in range(16)])  30.9 us
    all_to_all x1, blocking collectives, per_device(): spread = lax.all_to_all(merged, ZL, 0, 0, tiled=True)  20.9 us
    ppermute x6, waiting for transfers between devices, swap(): return lax.ppermute(x, CTX, [(i, i ^ d) for i in range(16)])  10.8 us
    pallas_call x1, Pallas kernels, attend(): pl.pallas_call(attention_kernel, out_shape=(shaped((8, HEADS + 1, TOK, 12...  10.7 us
    ppermute x1, starting transfers between devices, per_device(): lax.ppermute(shard, ('zq', 'zr', 'zh'), [(i, 15 - i) for i in range(16)])  7.48 us
    all_to_all x1, starting transfers between devices, gather(): return lax.all_to_all(copies, axes, 0, 0, tiled=True)  6.75 us
    ppermute x1, waiting for transfers between devices, per_device(): lax.ppermute(shard, ('zq', 'zr', 'zh'), [(i, 15 - i) for i in range(16)])  5.39 us
    pallas_call x1, Pallas kernels, project_queries(): pl.pallas_call(query_kernel, out_shape=(pltpu.HBM((HEADS, ROWS, LATENT),...  3.63 us
  transfers between devices with their start and end apart: 8, of which 4 were waited for; matrix products, arithmetic and copies ran while one was open for 0% of the time, Pallas kernels for 4%

profile of v5, /device:TPU:1, one launch (start us, length us, event | category | flops | bytes accessed | tf_op | source)
XLA Modules:
  0.0 102.8 jit_solution(6268587256503090653)
XLA Ops:
  0.0 1.0 prepare.1
  1.0 9.6 %collective-permute-start.1 = (bf16[1,352,128]{2,1,0:T(8,128)(2,1)S(1)}, bf16[1,352,128]{2,1,0:T(8,128)(2,1)S(1)}, u32[]{:S(2)}, u32[]{:S(2)}) collective-permute-start(bf16[1,352,128]{2,1,0:T(8,128)(2,1)S(1)} %get-tuple-element.15), channel_id=1, source_target_pairs={{0,256},{32,288},{64,320},{96,352},{128,384},{160,416},{192,448},{... | collective-permute-start | bytes 270344 | tf_op jit(solution)/shard_map/ppermute | solution.py:300
  10.7 7.5 %collective-permute-start = (bf16[1,72,512]{2,1,0:T(8,128)(2,1)S(1)}, bf16[1,72,512]{2,1,0:T(8,128)(2,1)S(1)}, u32[]{:S(2)}, u32[]{:S(2)}) collective-permute-start(bf16[1,72,512]{2,1,0:T(8,128)(2,1)S(1)} %get-tuple-element.14), channel_id=1, source_target_pairs={{0,449},{1,448},{64,385},{65,384},{128,321},{129,320},{192,257},{1... | collective-permute-start | bytes 221192 | tf_op jit(solution)/shard_map/ppermute | solution.py:319
  18.2 0.0 collective-permute-done.1
  18.2 0.0 copy-start
  18.2 5.4 %collective-permute-done = bf16[1,72,512]{2,1,0:T(8,128)(2,1)S(1)} collective-permute-done((bf16[1,72,512]{2,1,0:T(8,128)(2,1)S(1)}, bf16[1,72,512]{2,1,0:T(8,128)(2,1)S(1)}, u32[]{:S(2)}, u32[]{:S(2)}) %collective-permute-start) | collective-permute-done | bytes 73760 | tf_op jit(solution)/shard_map/ppermute | solution.py:319
  23.6 1.7 %broadcast_in_dim.2 = bf16[16,2,72,512]{3,2,1,0:T(8,128)(2,1)} broadcast(bf16[2,72,512]{2,1,0:T(8,128)(2,1)S(1)} %pad_maximum_fusion.2), dimensions={1,2,3} | broadcast | bytes 2506752 | tf_op jit(solution)/shard_map/broadcast_in_dim | solution.py:304
  25.3 6.8 %all-to-all-start = ((bf16[32,72,512]{2,1,0:T(8,128)(2,1)}), bf16[32,72,512]{2,1,0:T(8,128)(2,1)S(1)}, u32[]{:S(2)}, u32[]{:S(2)}) async-start(bf16[32,72,512]{2,1,0:T(8,128)(2,1)} %bitcast.9), calls=%async_computation | async-start | bytes 4718592 | tf_op jit(solution)/shard_map/all_to_all | solution.py:305
  32.1 9.8 %collective-permute-start.4 = (bf16[2,352,128]{2,1,0:T(8,128)(2,1)S(1)}, bf16[2,352,128]{2,1,0:T(8,128)(2,1)S(1)}, u32[]{:S(2)}, u32[]{:S(2)}) collective-permute-start(bf16[2,352,128]{2,1,0:T(8,128)(2,1)S(1)} %pad_maximum_fusion.1.refs_0_), channel_id=1, source_target_pairs={{0,192},{32,224},{64,128},{96,160},{128,64},{160,96},{192,0},{224,... | collective-permute-start | bytes 540680 | tf_op jit(solution)/shard_map/ppermute | solution.py:300
  41.9 1.9 %collective-permute-start.3 = (bf16[2,352,128]{2,1,0:T(8,128)(2,1)S(1)}, bf16[2,352,128]{2,1,0:T(8,128)(2,1)S(1)}, u32[]{:S(2)}, u32[]{:S(2)}) collective-permute-start(bf16[2,352,128]{2,1,0:T(8,128)(2,1)S(1)} %pad_maximum_fusion.1.refs_0_), channel_id=1, source_target_pairs={{0,128},{32,160},{64,192},{96,224},{128,0},{160,32},{192,64},{224,... | collective-permute-start | bytes 540680 | tf_op jit(solution)/shard_map/ppermute | solution.py:300
  43.8 2.2 %collective-permute-start.2 = (bf16[2,352,128]{2,1,0:T(8,128)(2,1)S(1)}, bf16[2,352,128]{2,1,0:T(8,128)(2,1)S(1)}, u32[]{:S(2)}, u32[]{:S(2)}) collective-permute-start(bf16[2,352,128]{2,1,0:T(8,128)(2,1)S(1)} %pad_maximum_fusion.1.refs_0_), channel_id=1, source_target_pairs={{0,64},{32,96},{64,0},{96,32},{128,192},{160,224},{192,128},{224,1... | collective-permute-start | bytes 540680 | tf_op jit(solution)/shard_map/ppermute | solution.py:300
  46.0 0.0 collective-permute-done.4.refs_3_
  46.0 0.0 copy-start.1
  46.0 8.6 %collective-permute-done.3.refs_2_ = bf16[2,352,128]{2,1,0:T(8,128)(2,1)S(1)} collective-permute-done((bf16[2,352,128]{2,1,0:T(8,128)(2,1)S(1)}, bf16[2,352,128]{2,1,0:T(8,128)(2,1)S(1)}, u32[]{:S(2)}, u32[]{:S(2)}) %collective-permute-start.3) | collective-permute-done | bytes 180256 | tf_op jit(solution)/shard_map/ppermute | solution.py:300
  54.6 0.0 copy-start.2
  54.6 0.0 collective-permute-done.2.refs_1_
  54.6 0.0 copy-done
  54.6 0.0 copy-start.3
  54.6 0.1 pad_maximum_fusion
  54.7 3.7 %collective-permute-start.5 = (bf16[8,352,128]{2,1,0:T(8,128)(2,1)S(1)}, bf16[8,352,128]{2,1,0:T(8,128)(2,1)}, u32[]{:S(2)}, u32[]{:S(2)}) collective-permute-start(bf16[8,352,128]{2,1,0:T(8,128)(2,1)S(1)} %pad_maximum_fusion), channel_id=1, source_target_pairs={{0,32},{32,0},{64,96},{96,64},{128,160},{160,128},{192,224},{224,1... | collective-permute-start | bytes 2162696 | tf_op jit(solution)/shard_map/ppermute | solution.py:300
  58.4 0.0 copy-done.2
  58.4 0.0 copy-done.3
  59.1 0.1 pad_add_fusion.place
  59.2 1.2 %collective-permute-done.5.refs_4_ = bf16[8,352,128]{2,1,0:T(8,128)(2,1)} collective-permute-done((bf16[8,352,128]{2,1,0:T(8,128)(2,1)S(1)}, bf16[8,352,128]{2,1,0:T(8,128)(2,1)}, u32[]{:S(2)}, u32[]{:S(2)}) %collective-permute-start.5) | collective-permute-done | bytes 720928 | tf_op jit(solution)/shard_map/ppermute | solution.py:300
  60.4 0.0 copy-done.1
  60.4 3.6 %query.1 = (bf16[4,256,512]{2,1,0:T(8,128)(2,1)}, bf16[2,4,256,128]{3,2,1,0:T(8,128)(2,1)}, bf16[4,16,32,128]{3,2,1,0:T(8,128)(2,1)}) custom-call(s32[3]{0:T(128)S(1)} %pad_add_fusion.place, bf16[2,352,128]{2,1,0:T(8,128)(2,1)} %copy-done, bf16[2,352,128]{2,1,0:T(8,128)(2,1)} %copy-done.3, bf16[2,352,128]{2,1,0:T(8,128)(2,1)} %copy-done.2, ...), custom_call_target="tpu_custom_call" | custom-call | tf_op jit(solution)/shard_map/query/pallas_call | solution.py:146
  64.0 0.0 all-to-all-done.chunk
  64.0 10.7 %attention.1 = (bf16[8,5,16,128]{3,2,1,0:T(8,128)(2,1)S(1)}, bf16[8,5,16,128]{3,2,1,0:T(8,128)(2,1)S(1)}) custom-call(s32[3]{0:T(128)S(1)} %pad_add_fusion.place, bf16[4,256,512]{2,1,0:T(8,128)(2,1)} %get-tuple-element.17.lat_hbm, bf16[2,4,256,128]{3,2,1,0:T(8,128)(2,1)} %get-tuple-element.18.rot_hbm, bf16[4,16,32,128]{3,2,1,0:T(8,128)(2,1)} %get-tuple-element.19.wv_hbm, ...), custom_call_target="tpu_custom_call" | custom-call | tf_op jit(solution)/shard_map/attention/pallas_call | solution.py:250
  74.7 3.7 %collective-permute-start.6 = (bf16[8,5,16,128]{3,2,1,0:T(8,128)(2,1)S(1)}, bf16[8,5,16,128]{3,2,1,0:T(8,128)(2,1)S(1)}, u32[]{:S(2)}, u32[]{:S(2)}) collective-permute-start(bf16[8,5,16,128]{3,2,1,0:T(8,128)(2,1)S(1)} %get-tuple-element.22), channel_id=1, source_target_pairs={{0,32},{32,0},{64,96},{96,64},{128,160},{160,128},{192,224},{224,1... | collective-permute-start | bytes 491528 | tf_op jit(solution)/shard_map/ppermute | solution.py:300
  78.4 1.0 collective-permute-done.6.b
  79.4 1.0 pair.1
  80.4 20.9 %all_to_all.10.x = bf16[8,5,16,128]{3,2,1,0:T(8,128)(2,1)S(1)} all-to-all(bf16[8,5,16,128]{3,2,1,0:T(8,128)(2,1)S(1)} %pair.1), channel_id=1, replica_groups=mesh['zq'=2,'zr'=4,'co'=2,'x'=4,'y'=4,'zh'=2] {'zq','zr'}, dimensions={0} | all-to-all | bytes 327680 | tf_op jit(solution)/shard_map/all_to_all | solution.py:331
  101.4 1.4 %final.1 = bf16[16,512]{1,0:T(8,128)(2,1)} custom-call(s32[3]{0:T(128)S(1)} %pad_add_fusion.place, bf16[8,5,16,128]{3,2,1,0:T(8,128)(2,1)S(1)} %all_to_all.10.x), custom_call_target="tpu_custom_call" | custom-call | flops 1 | bytes 1 | tf_op jit(solution)/shard_map/final/pallas_call | solution.py:332
  (2 shorter events, 0.0 us)
Async XLA Ops:
  1.0 17.1 %collective-permute-start.1 = (bf16[1,352,128]{2,1,0:T(8,128)(2,1)S(1)}, bf16[1,352,128]{2,1,0:T(8,128)(2,1)S(1)}, u32[]{:S(2)}, u32[]{:S(2)}) collective-permute-start(bf16[1,352,128]{2,1,0:T(8,128)(2,1)S(1)} %get-tuple-element.15), channel_id=1, source_target_pairs={{0,256},{32,288},{64,320},{96,352},{128,384},{160,416},{192,448},{... | collective-permute-start | bytes 270344 | tf_op jit(solution)/shard_map/ppermute | solution.py:300
  10.7 12.9 %collective-permute-start = (bf16[1,72,512]{2,1,0:T(8,128)(2,1)S(1)}, bf16[1,72,512]{2,1,0:T(8,128)(2,1)S(1)}, u32[]{:S(2)}, u32[]{:S(2)}) collective-permute-start(bf16[1,72,512]{2,1,0:T(8,128)(2,1)S(1)} %get-tuple-element.14), channel_id=1, source_target_pairs={{0,449},{1,448},{64,385},{65,384},{128,321},{129,320},{192,257},{1... | collective-permute-start | bytes 221192 | tf_op jit(solution)/shard_map/ppermute | solution.py:319
  18.2 36.4 %copy-start = (bf16[2,352,128]{2,1,0:T(8,128)(2,1)}, bf16[2,352,128]{2,1,0:T(8,128)(2,1)S(1)}, u32[]{:S(2)}) copy-start(bf16[2,352,128]{2,1,0:T(8,128)(2,1)S(1)} %pad_maximum_fusion.1.refs_0_) | copy-start | bytes 540676
  25.3 38.7 %all-to-all-start = ((bf16[32,72,512]{2,1,0:T(8,128)(2,1)}), bf16[32,72,512]{2,1,0:T(8,128)(2,1)S(1)}, u32[]{:S(2)}, u32[]{:S(2)}) async-start(bf16[32,72,512]{2,1,0:T(8,128)(2,1)} %bitcast.9), calls=%async_computation | async-start | bytes 4718592 | tf_op jit(solution)/shard_map/all_to_all | solution.py:305
  32.1 13.9 %collective-permute-start.4 = (bf16[2,352,128]{2,1,0:T(8,128)(2,1)S(1)}, bf16[2,352,128]{2,1,0:T(8,128)(2,1)S(1)}, u32[]{:S(2)}, u32[]{:S(2)}) collective-permute-start(bf16[2,352,128]{2,1,0:T(8,128)(2,1)S(1)} %pad_maximum_fusion.1.refs_0_), channel_id=1, source_target_pairs={{0,192},{32,224},{64,128},{96,160},{128,64},{160,96},{192,0},{224,... | collective-permute-start | bytes 540680 | tf_op jit(solution)/shard_map/ppermute | solution.py:300
  41.9 12.8 %collective-permute-start.3 = (bf16[2,352,128]{2,1,0:T(8,128)(2,1)S(1)}, bf16[2,352,128]{2,1,0:T(8,128)(2,1)S(1)}, u32[]{:S(2)}, u32[]{:S(2)}) collective-permute-start(bf16[2,352,128]{2,1,0:T(8,128)(2,1)S(1)} %pad_maximum_fusion.1.refs_0_), channel_id=1, source_target_pairs={{0,128},{32,160},{64,192},{96,224},{128,0},{160,32},{192,64},{224,... | collective-permute-start | bytes 540680 | tf_op jit(solution)/shard_map/ppermute | solution.py:300
  43.8 10.8 %collective-permute-start.2 = (bf16[2,352,128]{2,1,0:T(8,128)(2,1)S(1)}, bf16[2,352,128]{2,1,0:T(8,128)(2,1)S(1)}, u32[]{:S(2)}, u32[]{:S(2)}) collective-permute-start(bf16[2,352,128]{2,1,0:T(8,128)(2,1)S(1)} %pad_maximum_fusion.1.refs_0_), channel_id=1, source_target_pairs={{0,64},{32,96},{64,0},{96,32},{128,192},{160,224},{192,128},{224,1... | collective-permute-start | bytes 540680 | tf_op jit(solution)/shard_map/ppermute | solution.py:300
  46.0 14.3 %copy-start.1 = (bf16[2,352,128]{2,1,0:T(8,128)(2,1)}, bf16[2,352,128]{2,1,0:T(8,128)(2,1)S(1)}, u32[]{:S(2)}) copy-start(bf16[2,352,128]{2,1,0:T(8,128)(2,1)S(1)} %collective-permute-done.4.refs_3_) | copy-start | bytes 540676
  54.6 3.8 %copy-start.2 = (bf16[2,352,128]{2,1,0:T(8,128)(2,1)}, bf16[2,352,128]{2,1,0:T(8,128)(2,1)S(1)}, u32[]{:S(2)}) copy-start(bf16[2,352,128]{2,1,0:T(8,128)(2,1)S(1)} %collective-permute-done.3.refs_2_) | copy-start | bytes 540676
  54.6 3.8 %copy-start.3 = (bf16[2,352,128]{2,1,0:T(8,128)(2,1)}, bf16[2,352,128]{2,1,0:T(8,128)(2,1)S(1)}, u32[]{:S(2)}) copy-start(bf16[2,352,128]{2,1,0:T(8,128)(2,1)S(1)} %collective-permute-done.2.refs_1_) | copy-start | bytes 540676
  54.7 5.6 %collective-permute-start.5 = (bf16[8,352,128]{2,1,0:T(8,128)(2,1)S(1)}, bf16[8,352,128]{2,1,0:T(8,128)(2,1)}, u32[]{:S(2)}, u32[]{:S(2)}) collective-permute-start(bf16[8,352,128]{2,1,0:T(8,128)(2,1)S(1)} %pad_maximum_fusion), channel_id=1, source_target_pairs={{0,32},{32,0},{64,96},{96,64},{128,160},{160,128},{192,224},{224,1... | collective-permute-start | bytes 2162696 | tf_op jit(solution)/shard_map/ppermute | solution.py:300
  74.7 4.7 %collective-permute-start.6 = (bf16[8,5,16,128]{3,2,1,0:T(8,128)(2,1)S(1)}, bf16[8,5,16,128]{3,2,1,0:T(8,128)(2,1)S(1)}, u32[]{:S(2)}, u32[]{:S(2)}) collective-permute-start(bf16[8,5,16,128]{3,2,1,0:T(8,128)(2,1)S(1)} %get-tuple-element.22), channel_id=1, source_target_pairs={{0,32},{32,0},{64,96},{96,64},{128,160},{160,128},{192,224},{224,1... | collective-permute-start | bytes 491528 | tf_op jit(solution)/shard_map/ppermute | solution.py:300

commit v6 on v5

--- a/solution.py
+++ b/solution.py
@@ -91,31 +91,27 @@
     )(*(pltpu.with_memory_space_constraint(v, pltpu.HBM) for v in (queries, cache, wk, wv)))
 
 
-def query_kernel(place, *refs):
-    inputs, (lat_out, rot_out, wv_out), (tiles, pieces, panel, lats, rots, values, sems) = (
-        refs[:5],
-        refs[5:8],
-        refs[8:],
-    )
-    flips = ((0, 8), (2, 10), (4, 12), (6, 14), (1, 9, 3, 11, 5, 13, 7, 15))
-    starts = (0, 2, 4, 6, 8)
-    loads = [
+FLIPS = ((0, 8), (2, 10), (4, 12), (6, 14), (1, 9, 3, 11, 5, 13, 7, 15))
+STARTS = (0, 2, 4, 6, 8)
+
+
+def query_loads(inputs, tiles, sems):
+    return [
         pltpu.make_async_copy(ref, tiles.at[at : at + len(f)], sems.at[n])
-        for n, (ref, at, f) in enumerate(zip(inputs, starts, flips))
+        for n, (ref, at, f) in enumerate(zip(inputs, STARTS, FLIPS))
     ]
-    for c in loads:
-        c.start()
-    for c, at, flip in zip(loads, starts, flips):
+
+
+def project_queries(me, loads, tiles, pieces, panel, lats, rots, values):
+    for c, at, flip in zip(loads, STARTS, FLIPS):
         c.wait()
         for i, d in enumerate(flip):
-            src = lax.bitwise_xor(place[0], d)
+            src = lax.bitwise_xor(me, d)
             for k in range(6):
                 pieces[k, src] = tiles[at + i, TOK * k : TOK * (k + 1), :]
             for h in range(HEADS):
                 panel[h, src] = tiles[at + i, 96 + 32 * h : 128 + 32 * h, :]
                 values[h, src] = tiles[at + i, 224 + 32 * h : 256 + 32 * h, :]
-    stores = [pltpu.make_async_copy(values, wv_out, sems.at[5])]
-    stores[0].start()
     zero = jnp.zeros((ROWS, ROT), bf16)
     for h in range(HEADS):
         k = (h // 2) * 3
@@ -133,37 +129,6 @@
             (((1,), (1,)), ((), ())),
             preferred_element_type=f32,
         ).astype(bf16)
-        stores.append(pltpu.make_async_copy(lats.at[h], lat_out.at[h], sems.at[6 + h]))
-        stores[-1].start()
-    stores.append(pltpu.make_async_copy(rots, rot_out, sems.at[10]))
-    stores[-1].start()
-    for c in stores:
-        c.wait()
-
-
-def project_queries(place, *pieces):
-    hbm = pl.BlockSpec(memory_space=pltpu.HBM)
-    return pl.pallas_call(
-        query_kernel,
-        out_shape=(
-            pltpu.HBM((HEADS, ROWS, LATENT), bf16),
-            pltpu.HBM((2, HEADS, ROWS, 2 * ROT), bf16),
-            pltpu.HBM((HEADS, 16, 32, 128), bf16),
-        ),
-        in_specs=[pl.BlockSpec(memory_space=pltpu.SMEM)] + [hbm] * 5,
-        out_specs=(hbm,) * 3,
-        scratch_shapes=[
-            pltpu.VMEM((16, 352, 128), bf16),
-            pltpu.VMEM((6, 16, TOK, 128), bf16),
-            pltpu.VMEM((HEADS, 16, 32, 128), bf16),
-            pltpu.VMEM((HEADS, ROWS, LATENT), bf16),
-            pltpu.VMEM((2, HEADS, ROWS, 2 * ROT), bf16),
-            pltpu.VMEM((HEADS, 16, 32, 128), bf16),
-            pltpu.SemaphoreType.DMA((11,)),
-        ],
-        compiler_params=pltpu.CompilerParams(vmem_limit_bytes=16 * MIB),
-        name="query",
-    )(place, *(pltpu.with_memory_space_constraint(p, pltpu.HBM) for p in pieces))
 
 
 def split3(x):
@@ -189,54 +154,66 @@
     return t[..., k : k + 1] + t[..., k + 1 : k + 2] + t[..., k + 2 : k + 3]
 
 
-def attention_kernel(place, lat_hbm, rot_hbm, wv_hbm, chunk, keep, send, keys, parts, lats, rots, values, sems):
+def attention_kernel(place, p0, p1, p2, p3, p4, chunk, keep, send, keys, turns, parts, *scratch):
     me, zh, prior = place[0], place[1], place[2]
     zl, co = lax.shift_right_logical(me, 1), lax.bitwise_and(me, 1)
-    loads = [
-        pltpu.make_async_copy(rot_hbm, rots, sems.at[0]),
-        *(pltpu.make_async_copy(lat_hbm.at[h], lats.at[h], sems.at[1 + h]) for h in range(HEADS)),
-        pltpu.make_async_copy(wv_hbm, values, sems.at[1 + HEADS]),
-    ]
+    tiles, pieces, panel, lats, rots, values, sems = scratch
+    loads = query_loads((p0, p1, p2, p3, p4), tiles, sems)
     for c in loads:
         c.start()
     for half in range(2):
-        keys[half, :, :LATENT] = chunk[:, 32 * half : 32 * half + 32, :].reshape(SLOTS, LATENT)
-        for g in range(32):
-            for k in range(4):
-                at = 32 * g + 8 * k
-                keys[half, at : at + 8, LATENT:] = chunk[g, 64:72, 128 * k : 128 * (k + 1)]
-
-    limit = prior + lax.broadcasted_iota(jnp.int32, (ROWS, 1), 0)
+        keys[half] = chunk[:, 32 * half : 32 * half + 32, :].reshape(SLOTS, LATENT)
+    for g in range(32):
+        for k in range(4):
+            at = 32 * g + 8 * k
+            turns[at : at + 8] = chunk[g, 64:72, 128 * k : 128 * (k + 1)]
+
     n = lax.broadcasted_iota(jnp.int32, (1, SLOTS), 1)
     near = ((zl * 2 + co) * 32 + zh) * 64
     far = (((7 - zl) * 2 + co) * 32 + 1 - zh) * 64
     slot = lax.shift_right_logical(n, 6) * 128 + lax.bitwise_and(n, 31)
     slot = slot + jnp.where(lax.bitwise_and(n, 32) == 0, near, far)
+    project_queries(me, loads, tiles, pieces, panel, lats, rots, values)
+    limit = prior + lax.bitwise_and(lax.broadcasted_iota(jnp.int32, (4 * ROWS, 1), 0), ROWS - 1)
+    blocks = [(half, cut) for half in range(2) for cut in range(0, SLOTS, 512)]
     lses = []
-    loads[0].wait()
-    for h in range(HEADS):
-        loads[1 + h].wait()
+    for first in range(0, HEADS, 4):
+        group = range(first, first + 4)
         scores = []
-        for half in range(2):
-            q = jnp.concatenate([lats[h], rots[half, h]], axis=1)
+        for half, cut in blocks:
+            q = jnp.concatenate(
+                [
+                    lats[first : first + 4].reshape(4 * ROWS, LATENT),
+                    rots[half, first : first + 4].reshape(4 * ROWS, 2 * ROT),
+                ],
+                axis=1,
+            )
+            span = slice(cut, cut + 512)
             s = lax.dot_general(
-                q, keys[half], (((1,), (1,)), ((), ())), preferred_element_type=f32
+                q,
+                jnp.concatenate([keys[half, span], turns[span]], axis=1),
+                (((1,), (1,)), ((), ())),
+                preferred_element_type=f32,
             )
-            scores.append(jnp.where(slot + 32 * half <= limit, s * LOG2_SCALE, NEG))
-        peak = jnp.maximum(scores[0], scores[1]).max(axis=1, keepdims=True)
-        total = jnp.zeros((ROWS, 1), f32)
-        acc = jnp.zeros((ROWS, LATENT), f32)
-        for half in range(2):
-            p = jnp.exp2(scores[half] - peak)
+            scores.append(jnp.where(slot[:, span] + 32 * half <= limit, s * LOG2_SCALE, NEG))
+        peak = scores[0]
+        for s in scores[1:]:
+            peak = jnp.maximum(peak, s)
+        peak = peak.max(axis=1, keepdims=True)
+        total = jnp.zeros((4 * ROWS, 1), f32)
+        acc = jnp.zeros((4 * ROWS, LATENT), f32)
+        for s, (half, cut) in zip(scores, blocks):
+            p = jnp.exp2(s - peak)
             total = total + p.sum(axis=1, keepdims=True)
-            acc = acc + jnp.dot(p.astype(bf16), keys[half, :, :LATENT], preferred_element_type=f32)
-        if h == 0:
-            loads[1 + HEADS].wait()
+            acc = acc + jnp.dot(p.astype(bf16), keys[half, cut : cut + 512], preferred_element_type=f32)
         latent = (acc / total).astype(bf16)
-        o = jnp.dot(latent, values[h].reshape(LATENT, VALUE), preferred_element_type=f32).astype(bf16)
-        for g in range(16):
-            parts[g, h] = o[TOK * g : TOK * (g + 1)]
-        lses.append(peak + jnp.log2(total))
+        lse = peak + jnp.log2(total)
+        for i, h in enumerate(group):
+            rows = slice(i * ROWS, (i + 1) * ROWS)
+            o = jnp.dot(latent[rows], values[h].reshape(LATENT, VALUE), preferred_element_type=f32).astype(bf16)
+            for g in range(16):
+                parts[g, h] = o[TOK * g : TOK * (g + 1)]
+            lses.append(lse[rows])
     tile = pack_lse(lses, (ROWS, 128))
     for g in range(16):
         parts[g, HEADS] = tile[TOK * g : TOK * (g + 1)]
@@ -245,24 +222,28 @@
         send[g] = parts[g * 2 + 1 - co]
 
 
-def attend(place, lat, rot, wv, slots):
+def attend(place, slots, *pieces):
     hbm = pl.BlockSpec(memory_space=pltpu.HBM)
     return pl.pallas_call(
         attention_kernel,
         out_shape=(shaped((8, HEADS + 1, TOK, 128)),) * 2,
-        in_specs=[pl.BlockSpec(memory_space=pltpu.SMEM)] + [hbm] * 3 + [vmem()],
+        in_specs=[pl.BlockSpec(memory_space=pltpu.SMEM)] + [hbm] * 5 + [vmem()],
         out_specs=(vmem(), vmem()),
         scratch_shapes=[
-            pltpu.VMEM((2, SLOTS, WIDE), bf16),
+            pltpu.VMEM((2, SLOTS, LATENT), bf16),
+            pltpu.VMEM((SLOTS, 2 * ROT), bf16),
             pltpu.VMEM((16, HEADS + 1, TOK, 128), bf16),
-            pltpu.VMEM(lat.shape, bf16),
-            pltpu.VMEM(rot.shape, bf16),
-            pltpu.VMEM(wv.shape, bf16),
-            pltpu.SemaphoreType.DMA((2 + HEADS,)),
+            pltpu.VMEM((16, 352, 128), bf16),
+            pltpu.VMEM((6, 16, TOK, 128), bf16),
+            pltpu.VMEM((HEADS, 16, 32, 128), bf16),
+            pltpu.VMEM((HEADS, ROWS, LATENT), bf16),
+            pltpu.VMEM((2, HEADS, ROWS, 2 * ROT), bf16),
+            pltpu.VMEM((HEADS, 16, 32, 128), bf16),
+            pltpu.SemaphoreType.DMA((5,)),
         ],
-        compiler_params=pltpu.CompilerParams(vmem_limit_bytes=24 * MIB),
+        compiler_params=pltpu.CompilerParams(vmem_limit_bytes=32 * MIB),
         name="attention",
-    )(place, *(pltpu.with_memory_space_constraint(v, pltpu.HBM) for v in (lat, rot, wv)), slots)
+    )(place, *(pltpu.with_memory_space_constraint(p, pltpu.HBM) for p in pieces), slots)
 
 
 def merge_heads(blocks):
@@ -317,16 +298,14 @@
     )
 
     mirror = lax.ppermute(shard, ("zq", "zr", "zh"), [(i, 15 - i) for i in range(16)])
-    pack2 = jnp.concatenate([pack, swap(pack, 8)], axis=0)
-    mirror, pack2 = lax.optimization_barrier((mirror, pack2))
+    mirror, pack = lax.optimization_barrier((mirror, pack))
     pair = jnp.concatenate([shard, mirror], axis=0)
     slots = gather(pair, ("x", "y"), 16)
+    pack2 = jnp.concatenate([pack, swap(pack, 8)], axis=0)
     fans = [swap(pack2, d) for d in (2, 4, 6)]
     pack8 = jnp.concatenate([pack2] + fans, axis=0)
 
-
-    queries = project_queries(place, pack2, *fans, swap(pack8, 1))
-    keep, send = attend(place, *queries, slots)
+    keep, send = attend(place, slots, pack2, *fans, swap(pack8, 1))
     merged = call(pair_kernel, shaped((8, HEADS + 1, TOK, 128)), 2, "pair")(place, keep, swap(send, 1))
     spread = lax.all_to_all(merged, ZL, 0, 0, tiled=True)
     return call(final_kernel, shaped((TOK, HEADS * VALUE)), 1, "final")(place, spread)

time: 104 us -> 105 us (level)
  the two profiles are of different devices: /device:TPU:1 before, /device:TPU:2 now
where the time goes in v6:
time: 105 us
  starting transfers between devices  36.7 us (35%)
  waiting for transfers between devices  29 us (28%)
  blocking collectives  20.3 us (19%)
  Pallas kernels  12.8 us (12%)
  local copies, waits for them, and re-layouts  5.19 us (5%)
    ppermute x6, waiting for transfers between devices, swap(): return lax.ppermute(x, CTX, [(i, i ^ d) for i in range(16)])  22 us
    all_to_all x1, blocking collectives, per_device(): spread = lax.all_to_all(merged, ZL, 0, 0, tiled=True)  20.3 us
    ppermute x6, starting transfers between devices, swap(): return lax.ppermute(x, CTX, [(i, i ^ d) for i in range(16)])  17.8 us
    ppermute x1, starting transfers between devices, per_device(): lax.ppermute(shard, ('zq', 'zr', 'zh'), [(i, 15 - i) for i in range(16)])  11.4 us
    pallas_call x1, Pallas kernels, attend(): pl.pallas_call(attention_kernel, out_shape=(shaped((8, HEADS + 1, TOK, 12...  9.39 us
    all_to_all x1, starting transfers between devices, gather(): return lax.all_to_all(copies, axes, 0, 0, tiled=True)  7.48 us
    ppermute x1, waiting for transfers between devices, per_device(): lax.ppermute(shard, ('zq', 'zr', 'zh'), [(i, 15 - i) for i in range(16)])  6.99 us
    unnamed x12, local copies, waits for them, and re-layouts  2.77 us
  transfers between devices with their start and end apart: 8, of which 5 were waited for; matrix products, arithmetic and copies ran while one was open for 3% of the time, Pallas kernels for 0%

profile of v6, /device:TPU:2, one launch (start us, length us, event | category | flops | bytes accessed | tf_op | source)
XLA Modules:
  0.0 104.9 jit_solution(5711386816391988601)
XLA Ops:
  0.0 1.0 prepare.1
  1.0 11.4 %collective-permute-start = (bf16[1,72,512]{2,1,0:T(8,128)(2,1)S(1)}, bf16[1,72,512]{2,1,0:T(8,128)(2,1)S(1)}, u32[]{:S(2)}, u32[]{:S(2)}) collective-permute-start(bf16[1,72,512]{2,1,0:T(8,128)(2,1)S(1)} %get-tuple-element.11), channel_id=1, source_target_pairs={{0,449},{1,448},{64,385},{65,384},{128,321},{129,320},{192,257},{1... | collective-permute-start | bytes 221192 | tf_op jit(solution)/shard_map/ppermute | solution.py:300
  12.4 7.0 %collective-permute-done = bf16[1,72,512]{2,1,0:T(8,128)(2,1)S(1)} collective-permute-done((bf16[1,72,512]{2,1,0:T(8,128)(2,1)S(1)}, bf16[1,72,512]{2,1,0:T(8,128)(2,1)S(1)}, u32[]{:S(2)}, u32[]{:S(2)}) %collective-permute-start) | collective-permute-done | bytes 73760 | tf_op jit(solution)/shard_map/ppermute | solution.py:300
  19.4 1.7 %broadcast_in_dim.2 = bf16[16,2,72,512]{3,2,1,0:T(8,128)(2,1)} broadcast(bf16[2,72,512]{2,1,0:T(8,128)(2,1)S(1)} %pad_maximum_fusion), dimensions={1,2,3} | broadcast | bytes 2506752 | tf_op jit(solution)/shard_map/broadcast_in_dim | solution.py:285
  21.1 7.5 %all-to-all-start = ((bf16[32,72,512]{2,1,0:T(8,128)(2,1)}), bf16[32,72,512]{2,1,0:T(8,128)(2,1)S(1)}, u32[]{:S(2)}, u32[]{:S(2)}) async-start(bf16[32,72,512]{2,1,0:T(8,128)(2,1)} %bitcast.9), calls=%async_computation | async-start | bytes 4718592 | tf_op jit(solution)/shard_map/all_to_all | solution.py:286
  28.6 3.8 %collective-permute-start.1 = (bf16[1,352,128]{2,1,0:T(8,128)(2,1)S(1)}, bf16[1,352,128]{2,1,0:T(8,128)(2,1)S(1)}, u32[]{:S(2)}, u32[]{:S(2)}) collective-permute-start(bf16[1,352,128]{2,1,0:T(8,128)(2,1)S(1)} %get-tuple-element.13), channel_id=1, source_target_pairs={{0,256},{32,288},{64,320},{96,352},{128,384},{160,416},{192,448},{... | collective-permute-start | bytes 270344 | tf_op jit(solution)/shard_map/ppermute | solution.py:281
  32.4 0.6 constant_dynamic-update-slice_fusion.6
  33.0 9.9 %collective-permute-done.1 = bf16[1,352,128]{2,1,0:T(8,128)(2,1)S(1)} collective-permute-done((bf16[1,352,128]{2,1,0:T(8,128)(2,1)S(1)}, bf16[1,352,128]{2,1,0:T(8,128)(2,1)S(1)}, u32[]{:S(2)}, u32[]{:S(2)}) %collective-permute-start.1) | collective-permute-done | bytes 90144 | tf_op jit(solution)/shard_map/ppermute | solution.py:281
  43.0 0.7 constant_dynamic-update-slice_fusion.5
  43.6 0.0 copy-start.3
  43.6 1.9 %collective-permute-start.2 = (bf16[2,352,128]{2,1,0:T(8,128)(2,1)S(1)}, bf16[2,352,128]{2,1,0:T(8,128)(2,1)S(1)}, u32[]{:S(2)}, u32[]{:S(2)}) collective-permute-start(bf16[2,352,128]{2,1,0:T(8,128)(2,1)S(1)} %get-tuple-element.18.p0), channel_id=1, source_target_pairs={{0,64},{32,96},{64,0},{96,32},{128,192},{160,224},{192,128},{224,1... | collective-permute-start | bytes 540680 | tf_op jit(solution)/shard_map/ppermute | solution.py:281
  45.6 1.9 %collective-permute-start.3 = (bf16[2,352,128]{2,1,0:T(8,128)(2,1)S(1)}, bf16[2,352,128]{2,1,0:T(8,128)(2,1)S(1)}, u32[]{:S(2)}, u32[]{:S(2)}) collective-permute-start(bf16[2,352,128]{2,1,0:T(8,128)(2,1)S(1)} %get-tuple-element.18.p0), channel_id=1, source_target_pairs={{0,128},{32,160},{64,192},{96,224},{128,0},{160,32},{192,64},{224,... | collective-permute-start | bytes 540680 | tf_op jit(solution)/shard_map/ppermute | solution.py:281
  47.5 6.3 %collective-permute-start.4 = (bf16[2,352,128]{2,1,0:T(8,128)(2,1)S(1)}, bf16[2,352,128]{2,1,0:T(8,128)(2,1)S(1)}, u32[]{:S(2)}, u32[]{:S(2)}) collective-permute-start(bf16[2,352,128]{2,1,0:T(8,128)(2,1)S(1)} %get-tuple-element.18.p0), channel_id=1, source_target_pairs={{0,192},{32,224},{64,128},{96,160},{128,64},{160,96},{192,0},{224,... | collective-permute-start | bytes 540680 | tf_op jit(solution)/shard_map/ppermute | solution.py:281
  53.8 0.0 collective-permute-done.2.p1
  53.8 0.0 copy-start
  53.8 0.7 constant_dynamic-update-slice_fusion.4
  54.5 9.0 %collective-permute-done.3.p2 = bf16[2,352,128]{2,1,0:T(8,128)(2,1)S(1)} collective-permute-done((bf16[2,352,128]{2,1,0:T(8,128)(2,1)S(1)}, bf16[2,352,128]{2,1,0:T(8,128)(2,1)S(1)}, u32[]{:S(2)}, u32[]{:S(2)}) %collective-permute-start.3) | collective-permute-done | bytes 180256 | tf_op jit(solution)/shard_map/ppermute | solution.py:281
  63.5 0.0 copy-start.1
  63.5 0.7 constant_dynamic-update-slice_fusion.3
  64.3 0.0 collective-permute-done.4.p3
  64.3 0.0 copy-start.2
  64.3 0.7 constant_dynamic-update-slice_fusion.2
  65.0 1.9 %collective-permute-start.5 = (bf16[8,352,128]{2,1,0:T(8,128)(2,1)}, bf16[8,352,128]{2,1,0:T(8,128)(2,1)}, u32[]{:S(2)}, u32[]{:S(2)}) collective-permute-start(bf16[8,352,128]{2,1,0:T(8,128)(2,1)} %constant_dynamic-update-slice_fusion.2), channel_id=1, source_target_pairs={{0,32},{32,0},{64,96},{96,64},{128,160},{160,128},{192,224},{224,1... | collective-permute-start | bytes 2162696 | tf_op jit(solution)/shard_map/ppermute | solution.py:281
  67.6 0.1 pad_add_fusion.place
  67.6 1.8 %collective-permute-done.5.p4 = bf16[8,352,128]{2,1,0:T(8,128)(2,1)} collective-permute-done((bf16[8,352,128]{2,1,0:T(8,128)(2,1)}, bf16[8,352,128]{2,1,0:T(8,128)(2,1)}, u32[]{:S(2)}, u32[]{:S(2)}) %collective-permute-start.5) | collective-permute-done | bytes 720928 | tf_op jit(solution)/shard_map/ppermute | solution.py:281
  69.4 0.0 all-to-all-done.chunk
  69.4 0.0 copy-done.3
  69.4 0.0 copy-done
  69.4 0.0 copy-done.1
  69.4 0.0 copy-done.2
  69.4 9.4 %attention.1 = (bf16[8,5,16,128]{3,2,1,0:T(8,128)(2,1)S(1)}, bf16[8,5,16,128]{3,2,1,0:T(8,128)(2,1)S(1)}) custom-call(s32[3]{0:T(128)S(1)} %pad_add_fusion.place, bf16[2,352,128]{2,1,0:T(8,128)(2,1)} %copy-done.3, bf16[2,352,128]{2,1,0:T(8,128)(2,1)} %copy-done, bf16[2,352,128]{2,1,0:T(8,128)(2,1)} %copy-done.1, bf16[2,352,128]{2,1,0:T(8,128)(2,1)} %copy-done.2, ...), custom_call_target="tpu_custom_call" | custom-call | tf_op jit(solution)/shard_map/attention/pallas_call | solution.py:227
  78.8 2.1 %collective-permute-start.6 = (bf16[8,5,16,128]{3,2,1,0:T(8,128)(2,1)S(1)}, bf16[8,5,16,128]{3,2,1,0:T(8,128)(2,1)S(1)}, u32[]{:S(2)}, u32[]{:S(2)}) collective-permute-start(bf16[8,5,16,128]{3,2,1,0:T(8,128)(2,1)S(1)} %get-tuple-element.16), channel_id=1, source_target_pairs={{0,32},{32,0},{64,96},{96,64},{128,160},{160,128},{192,224},{224,1... | collective-permute-start | bytes 491528 | tf_op jit(solution)/shard_map/ppermute | solution.py:281
  80.9 1.2 %collective-permute-done.6.b = bf16[8,5,16,128]{3,2,1,0:T(8,128)(2,1)S(1)} collective-permute-done((bf16[8,5,16,128]{3,2,1,0:T(8,128)(2,1)S(1)}, bf16[8,5,16,128]{3,2,1,0:T(8,128)(2,1)S(1)}, u32[]{:S(2)}, u32[]{:S(2)}) %collective-permute-start.6) | collective-permute-done | bytes 163872 | tf_op jit(solution)/shard_map/ppermute | solution.py:281
  82.1 1.0 pair.1
  83.1 20.3 %all_to_all.10.x = bf16[8,5,16,128]{3,2,1,0:T(8,128)(2,1)S(1)} all-to-all(bf16[8,5,16,128]{3,2,1,0:T(8,128)(2,1)S(1)} %pair.1), channel_id=1, replica_groups=mesh['zq'=2,'zr'=4,'co'=2,'x'=4,'y'=4,'zh'=2] {'zq','zr'}, dimensions={0} | all-to-all | bytes 327680 | tf_op jit(solution)/shard_map/all_to_all | solution.py:310
  103.5 1.4 %final.1 = bf16[16,512]{1,0:T(8,128)(2,1)} custom-call(s32[3]{0:T(128)S(1)} %pad_add_fusion.place, bf16[8,5,16,128]{3,2,1,0:T(8,128)(2,1)S(1)} %all_to_all.10.x), custom_call_target="tpu_custom_call" | custom-call | flops 1 | bytes 1 | tf_op jit(solution)/shard_map/final/pallas_call | solution.py:311
  (1 shorter events, 0.0 us)
Async XLA Ops:
  1.0 18.4 %collective-permute-start = (bf16[1,72,512]{2,1,0:T(8,128)(2,1)S(1)}, bf16[1,72,512]{2,1,0:T(8,128)(2,1)S(1)}, u32[]{:S(2)}, u32[]{:S(2)}) collective-permute-start(bf16[1,72,512]{2,1,0:T(8,128)(2,1)S(1)} %get-tuple-element.11), channel_id=1, source_target_pairs={{0,449},{1,448},{64,385},{65,384},{128,321},{129,320},{192,257},{1... | collective-permute-start | bytes 221192 | tf_op jit(solution)/shard_map/ppermute | solution.py:300
  21.1 48.3 %all-to-all-start = ((bf16[32,72,512]{2,1,0:T(8,128)(2,1)}), bf16[32,72,512]{2,1,0:T(8,128)(2,1)S(1)}, u32[]{:S(2)}, u32[]{:S(2)}) async-start(bf16[32,72,512]{2,1,0:T(8,128)(2,1)} %bitcast.9), calls=%async_computation | async-start | bytes 4718592 | tf_op jit(solution)/shard_map/all_to_all | solution.py:286
  28.6 14.4 %collective-permute-start.1 = (bf16[1,352,128]{2,1,0:T(8,128)(2,1)S(1)}, bf16[1,352,128]{2,1,0:T(8,128)(2,1)S(1)}, u32[]{:S(2)}, u32[]{:S(2)}) collective-permute-start(bf16[1,352,128]{2,1,0:T(8,128)(2,1)S(1)} %get-tuple-element.13), channel_id=1, source_target_pairs={{0,256},{32,288},{64,320},{96,352},{128,384},{160,416},{192,448},{... | collective-permute-start | bytes 270344 | tf_op jit(solution)/shard_map/ppermute | solution.py:281
  43.6 25.8 %copy-start.3 = (bf16[2,352,128]{2,1,0:T(8,128)(2,1)}, bf16[2,352,128]{2,1,0:T(8,128)(2,1)S(1)}, u32[]{:S(2)}) copy-start(bf16[2,352,128]{2,1,0:T(8,128)(2,1)S(1)} %get-tuple-element.18.p0) | copy-start | bytes 540676
  43.6 10.1 %collective-permute-start.2 = (bf16[2,352,128]{2,1,0:T(8,128)(2,1)S(1)}, bf16[2,352,128]{2,1,0:T(8,128)(2,1)S(1)}, u32[]{:S(2)}, u32[]{:S(2)}) collective-permute-start(bf16[2,352,128]{2,1,0:T(8,128)(2,1)S(1)} %get-tuple-element.18.p0), channel_id=1, source_target_pairs={{0,64},{32,96},{64,0},{96,32},{128,192},{160,224},{192,128},{224,1... | collective-permute-start | bytes 540680 | tf_op jit(solution)/shard_map/ppermute | solution.py:281
  45.6 18.0 %collective-permute-start.3 = (bf16[2,352,128]{2,1,0:T(8,128)(2,1)S(1)}, bf16[2,352,128]{2,1,0:T(8,128)(2,1)S(1)}, u32[]{:S(2)}, u32[]{:S(2)}) collective-permute-start(bf16[2,352,128]{2,1,0:T(8,128)(2,1)S(1)} %get-tuple-element.18.p0), channel_id=1, source_target_pairs={{0,128},{32,160},{64,192},{96,224},{128,0},{160,32},{192,64},{224,... | collective-permute-start | bytes 540680 | tf_op jit(solution)/shard_map/ppermute | solution.py:281
  47.5 16.8 %collective-permute-start.4 = (bf16[2,352,128]{2,1,0:T(8,128)(2,1)S(1)}, bf16[2,352,128]{2,1,0:T(8,128)(2,1)S(1)}, u32[]{:S(2)}, u32[]{:S(2)}) collective-permute-start(bf16[2,352,128]{2,1,0:T(8,128)(2,1)S(1)} %get-tuple-element.18.p0), channel_id=1, source_target_pairs={{0,192},{32,224},{64,128},{96,160},{128,64},{160,96},{192,0},{224,... | collective-permute-start | bytes 540680 | tf_op jit(solution)/shard_map/ppermute | solution.py:281
  53.8 15.6 %copy-start = (bf16[2,352,128]{2,1,0:T(8,128)(2,1)}, bf16[2,352,128]{2,1,0:T(8,128)(2,1)S(1)}, u32[]{:S(2)}) copy-start(bf16[2,352,128]{2,1,0:T(8,128)(2,1)S(1)} %collective-permute-done.2.p1) | copy-start | bytes 540676
  63.5 5.9 %copy-start.1 = (bf16[2,352,128]{2,1,0:T(8,128)(2,1)}, bf16[2,352,128]{2,1,0:T(8,128)(2,1)S(1)}, u32[]{:S(2)}) copy-start(bf16[2,352,128]{2,1,0:T(8,128)(2,1)S(1)} %collective-permute-done.3.p2) | copy-start | bytes 540676
  64.3 5.2 %copy-start.2 = (bf16[2,352,128]{2,1,0:T(8,128)(2,1)}, bf16[2,352,128]{2,1,0:T(8,128)(2,1)S(1)}, u32[]{:S(2)}) copy-start(bf16[2,352,128]{2,1,0:T(8,128)(2,1)S(1)} %collective-permute-done.4.p3) | copy-start | bytes 540676
  65.0 4.4 %collective-permute-start.5 = (bf16[8,352,128]{2,1,0:T(8,128)(2,1)}, bf16[8,352,128]{2,1,0:T(8,128)(2,1)}, u32[]{:S(2)}, u32[]{:S(2)}) collective-permute-start(bf16[8,352,128]{2,1,0:T(8,128)(2,1)} %constant_dynamic-update-slice_fusion.2), channel_id=1, source_target_pairs={{0,32},{32,0},{64,96},{96,64},{128,160},{160,128},{192,224},{224,1... | collective-permute-start | bytes 2162696 | tf_op jit(solution)/shard_map/ppermute | solution.py:281
  78.8 3.3 %collective-permute-start.6 = (bf16[8,5,16,128]{3,2,1,0:T(8,128)(2,1)S(1)}, bf16[8,5,16,128]{3,2,1,0:T(8,128)(2,1)S(1)}, u32[]{:S(2)}, u32[]{:S(2)}) collective-permute-start(bf16[8,5,16,128]{3,2,1,0:T(8,128)(2,1)S(1)} %get-tuple-element.16), channel_id=1, source_target_pairs={{0,32},{32,0},{64,96},{96,64},{128,160},{160,128},{192,224},{224,1... | collective-permute-start | bytes 491528 | tf_op jit(solution)/shard_map/ppermute | solution.py:281

commit v7 on v6

--- a/solution.py
+++ b/solution.py
@@ -298,10 +298,12 @@
     )
 
     mirror = lax.ppermute(shard, ("zq", "zr", "zh"), [(i, 15 - i) for i in range(16)])
-    mirror, pack = lax.optimization_barrier((mirror, pack))
+    got = swap(pack, 8)
     pair = jnp.concatenate([shard, mirror], axis=0)
-    slots = gather(pair, ("x", "y"), 16)
-    pack2 = jnp.concatenate([pack, swap(pack, 8)], axis=0)
+    copies = jnp.broadcast_to(pair[None], (16, 2, 72, LATENT)).reshape(32, 72, LATENT)
+    pack2 = jnp.concatenate([pack, got], axis=0)
+    copies, pack2 = lax.optimization_barrier((copies, pack2))
+    slots = lax.all_to_all(copies, ("x", "y"), 0, 0, tiled=True)
     fans = [swap(pack2, d) for d in (2, 4, 6)]
     pack8 = jnp.concatenate([pack2] + fans, axis=0)
 

time: 105 us -> 98.7 us (0.940)
  the two profiles are of different devices: /device:TPU:2 before, /device:TPU:1 now
where the time goes in v7:
time: 98.7 us; the launch traced here: 97.1 us
  starting transfers between devices  50.2 us (51%)
  blocking collectives  17.1 us (17%)
  waiting for transfers between devices  13.4 us (14%)
  Pallas kernels  12.8 us (13%)
  local copies, waits for them, and re-layouts  1.71 us (2%)
  other arithmetic  1.07 us (1%)
    ppermute x6, starting transfers between devices, swap(): return lax.ppermute(x, CTX, [(i, i ^ d) for i in range(16)])  31.5 us
    all_to_all x1, blocking collectives, per_device(): spread = lax.all_to_all(merged, ZL, 0, 0, tiled=True)  17.1 us
    ppermute x6, waiting for transfers between devices, swap(): return lax.ppermute(x, CTX, [(i, i ^ d) for i in range(16)])  13.4 us
    ppermute x1, starting transfers between devices, per_device(): lax.ppermute(shard, ('zq', 'zr', 'zh'), [(i, 15 - i) for i in range(16)])  12 us
    pallas_call x1, Pallas kernels, attend(): pl.pallas_call(attention_kernel, out_shape=(shaped((8, HEADS + 1, TOK, 12...  9.4 us
    all_to_all x1, starting transfers between devices, per_device(): slots = lax.all_to_all(copies, ('x', 'y'), 0, 0, tiled=True)  6.75 us
  transfers between devices with their start and end apart: 8, of which 5 were waited for; matrix products, arithmetic and copies ran while one was open for 1% of the time, Pallas kernels for 0%

profile of v7, /device:TPU:1, one launch (start us, length us, event | category | flops | bytes accessed | tf_op | source)
XLA Modules:
  0.0 97.1 jit_solution(3487343948837617032)
XLA Ops:
  0.0 1.0 %prepare.1 = (bf16[1,72,512]{2,1,0:T(8,128)(2,1)S(1)}, bf16[1,352,128]{2,1,0:T(8,128)(2,1)S(1)}) custom-call(bf16[16,768]{1,0:T(8,128)(2,1)} %queries_hbm.1, bf16[64,576]{1,0:T(8,128)(2,1)} %cache_hbm.1, bf16[128,128]{1,0:T(8,128)(2,1)} %bitcast.10, bf16[128,128]{1,0:T(8,128)(2,1)} %bitcast.11), custom_call_target="tpu_custom_call" | custom-call | tf_op jit(solution)/shard_map/prepare/pallas_call | solution.py:79
  1.0 12.0 %collective-permute-start = (bf16[1,72,512]{2,1,0:T(8,128)(2,1)S(1)}, bf16[1,72,512]{2,1,0:T(8,128)(2,1)S(1)}, u32[]{:S(2)}, u32[]{:S(2)}) collective-permute-start(bf16[1,72,512]{2,1,0:T(8,128)(2,1)S(1)} %get-tuple-element.11), channel_id=1, source_target_pairs={{0,449},{1,448},{64,385},{65,384},{128,321},{129,320},{192,257},{1... | collective-permute-start | bytes 221192 | tf_op jit(solution)/shard_map/ppermute | solution.py:300
  13.0 7.9 %collective-permute-start.1 = (bf16[1,352,128]{2,1,0:T(8,128)(2,1)S(1)}, bf16[1,352,128]{2,1,0:T(8,128)(2,1)S(1)}, u32[]{:S(2)}, u32[]{:S(2)}) collective-permute-start(bf16[1,352,128]{2,1,0:T(8,128)(2,1)S(1)} %get-tuple-element.12), channel_id=1, source_target_pairs={{0,256},{32,288},{64,320},{96,352},{128,384},{160,416},{192,448},{... | collective-permute-start | bytes 270344 | tf_op jit(solution)/shard_map/ppermute | solution.py:281
  20.9 0.0 collective-permute-done
  20.9 3.2 %collective-permute-done.1 = bf16[1,352,128]{2,1,0:T(8,128)(2,1)S(1)} collective-permute-done((bf16[1,352,128]{2,1,0:T(8,128)(2,1)S(1)}, bf16[1,352,128]{2,1,0:T(8,128)(2,1)S(1)}, u32[]{:S(2)}, u32[]{:S(2)}) %collective-permute-start.1) | collective-permute-done | bytes 90144 | tf_op jit(solution)/shard_map/ppermute | solution.py:281
  24.2 0.0 copy-start
  24.2 1.7 %broadcast_in_dim.2 = bf16[16,2,72,512]{3,2,1,0:T(8,128)(2,1)} broadcast(bf16[2,72,512]{2,1,0:T(8,128)(2,1)S(1)} %pad_maximum_fusion.2), dimensions={1,2,3} | broadcast | bytes 2506752 | tf_op jit(solution)/shard_map/broadcast_in_dim | solution.py:303
  25.9 6.8 %all-to-all-start = ((bf16[32,72,512]{2,1,0:T(8,128)(2,1)}), bf16[32,72,512]{2,1,0:T(8,128)(2,1)S(1)}, u32[]{:S(2)}, u32[]{:S(2)}) async-start(bf16[32,72,512]{2,1,0:T(8,128)(2,1)} %bitcast.9), calls=%async_computation | async-start | bytes 4718592 | tf_op jit(solution)/shard_map/all_to_all | solution.py:306
  32.6 4.3 %collective-permute-start.4 = (bf16[2,352,128]{2,1,0:T(8,128)(2,1)S(1)}, bf16[2,352,128]{2,1,0:T(8,128)(2,1)S(1)}, u32[]{:S(2)}, u32[]{:S(2)}) collective-permute-start(bf16[2,352,128]{2,1,0:T(8,128)(2,1)S(1)} %pad_maximum_fusion.1.p0), channel_id=1, source_target_pairs={{0,192},{32,224},{64,128},{96,160},{128,64},{160,96},{192,0},{224,... | collective-permute-start | bytes 540680 | tf_op jit(solution)/shard_map/ppermute | solution.py:281
  37.0 1.9 %collective-permute-start.3 = (bf16[2,352,128]{2,1,0:T(8,128)(2,1)S(1)}, bf16[2,352,128]{2,1,0:T(8,128)(2,1)S(1)}, u32[]{:S(2)}, u32[]{:S(2)}) collective-permute-start(bf16[2,352,128]{2,1,0:T(8,128)(2,1)S(1)} %pad_maximum_fusion.1.p0), channel_id=1, source_target_pairs={{0,128},{32,160},{64,192},{96,224},{128,0},{160,32},{192,64},{224,... | collective-permute-start | bytes 540680 | tf_op jit(solution)/shard_map/ppermute | solution.py:281
  38.9 3.0 %collective-permute-start.2 = (bf16[2,352,128]{2,1,0:T(8,128)(2,1)S(1)}, bf16[2,352,128]{2,1,0:T(8,128)(2,1)S(1)}, u32[]{:S(2)}, u32[]{:S(2)}) collective-permute-start(bf16[2,352,128]{2,1,0:T(8,128)(2,1)S(1)} %pad_maximum_fusion.1.p0), channel_id=1, source_target_pairs={{0,64},{32,96},{64,0},{96,32},{128,192},{160,224},{192,128},{224,1... | collective-permute-start | bytes 540680 | tf_op jit(solution)/shard_map/ppermute | solution.py:281
  41.9 0.0 collective-permute-done.4.p3
  41.9 0.0 copy-start.1
  41.9 5.7 %collective-permute-done.3.p2 = bf16[2,352,128]{2,1,0:T(8,128)(2,1)S(1)} collective-permute-done((bf16[2,352,128]{2,1,0:T(8,128)(2,1)S(1)}, bf16[2,352,128]{2,1,0:T(8,128)(2,1)S(1)}, u32[]{:S(2)}, u32[]{:S(2)}) %collective-permute-start.3) | collective-permute-done | bytes 180256 | tf_op jit(solution)/shard_map/ppermute | solution.py:281
  47.7 0.0 copy-start.2
  47.7 2.0 %collective-permute-done.2.p1 = bf16[2,352,128]{2,1,0:T(8,128)(2,1)S(1)} collective-permute-done((bf16[2,352,128]{2,1,0:T(8,128)(2,1)S(1)}, bf16[2,352,128]{2,1,0:T(8,128)(2,1)S(1)}, u32[]{:S(2)}, u32[]{:S(2)}) %collective-permute-start.2) | collective-permute-done | bytes 180256 | tf_op jit(solution)/shard_map/ppermute | solution.py:281
  49.7 0.0 copy-done
  49.7 0.0 copy-start.3
  49.7 1.0 pad_maximum_fusion
  50.6 6.0 %collective-permute-start.5 = (bf16[8,352,128]{2,1,0:T(8,128)(2,1)}, bf16[8,352,128]{2,1,0:T(8,128)(2,1)}, u32[]{:S(2)}, u32[]{:S(2)}) collective-permute-start(bf16[8,352,128]{2,1,0:T(8,128)(2,1)} %pad_maximum_fusion), channel_id=1, source_target_pairs={{0,32},{32,0},{64,96},{96,64},{128,160},{160,128},{192,224},{224,1... | collective-permute-start | bytes 2162696 | tf_op jit(solution)/shard_map/ppermute | solution.py:281
  57.3 0.1 pad_add_fusion.place
  57.4 1.4 %collective-permute-done.5.p4 = bf16[8,352,128]{2,1,0:T(8,128)(2,1)} collective-permute-done((bf16[8,352,128]{2,1,0:T(8,128)(2,1)}, bf16[8,352,128]{2,1,0:T(8,128)(2,1)}, u32[]{:S(2)}, u32[]{:S(2)}) %collective-permute-start.5) | collective-permute-done | bytes 720928 | tf_op jit(solution)/shard_map/ppermute | solution.py:281
  58.8 0.0 all-to-all-done.chunk
  58.8 0.0 copy-done.1
  58.8 0.0 copy-done.2
  58.8 0.0 copy-done.3
  58.8 9.4 %attention.1 = (bf16[8,5,16,128]{3,2,1,0:T(8,128)(2,1)S(1)}, bf16[8,5,16,128]{3,2,1,0:T(8,128)(2,1)S(1)}) custom-call(s32[3]{0:T(128)S(1)} %pad_add_fusion.place, bf16[2,352,128]{2,1,0:T(8,128)(2,1)} %copy-done, bf16[2,352,128]{2,1,0:T(8,128)(2,1)} %copy-done.3, bf16[2,352,128]{2,1,0:T(8,128)(2,1)} %copy-done.2, bf16[2,352,128]{2,1,0:T(8,128)(2,1)} %copy-done.1, ...), custom_call_target="tpu_custom_call" | custom-call | tf_op jit(solution)/shard_map/attention/pallas_call | solution.py:227
  68.3 8.3 %collective-permute-start.6 = (bf16[8,5,16,128]{3,2,1,0:T(8,128)(2,1)S(1)}, bf16[8,5,16,128]{3,2,1,0:T(8,128)(2,1)S(1)}, u32[]{:S(2)}, u32[]{:S(2)}) collective-permute-start(bf16[8,5,16,128]{3,2,1,0:T(8,128)(2,1)S(1)} %get-tuple-element.16), channel_id=1, source_target_pairs={{0,32},{32,0},{64,96},{96,64},{128,160},{160,128},{192,224},{224,1... | collective-permute-start | bytes 491528 | tf_op jit(solution)/shard_map/ppermute | solution.py:281
  76.5 1.0 %collective-permute-done.6.b = bf16[8,5,16,128]{3,2,1,0:T(8,128)(2,1)S(1)} collective-permute-done((bf16[8,5,16,128]{3,2,1,0:T(8,128)(2,1)S(1)}, bf16[8,5,16,128]{3,2,1,0:T(8,128)(2,1)S(1)}, u32[]{:S(2)}, u32[]{:S(2)}) %collective-permute-start.6) | collective-permute-done | bytes 163872 | tf_op jit(solution)/shard_map/ppermute | solution.py:281
  77.6 1.0 %pair.1 = bf16[8,5,16,128]{3,2,1,0:T(8,128)(2,1)S(1)} custom-call(s32[3]{0:T(128)S(1)} %pad_add_fusion.place, bf16[8,5,16,128]{3,2,1,0:T(8,128)(2,1)S(1)} %get-tuple-element.15.a, bf16[8,5,16,128]{3,2,1,0:T(8,128)(2,1)S(1)} %collective-permute-done.6.b), custom_call_target="tpu_custom_call" | custom-call | flops 1 | bytes 1 | tf_op jit(solution)/shard_map/pair/pallas_call | solution.py:311
  78.6 17.1 %all_to_all.10.x = bf16[8,5,16,128]{3,2,1,0:T(8,128)(2,1)S(1)} all-to-all(bf16[8,5,16,128]{3,2,1,0:T(8,128)(2,1)S(1)} %pair.1), channel_id=1, replica_groups=mesh['zq'=2,'zr'=4,'co'=2,'x'=4,'y'=4,'zh'=2] {'zq','zr'}, dimensions={0} | all-to-all | bytes 327680 | tf_op jit(solution)/shard_map/all_to_all | solution.py:312
  95.7 1.4 %final.1 = bf16[16,512]{1,0:T(8,128)(2,1)} custom-call(s32[3]{0:T(128)S(1)} %pad_add_fusion.place, bf16[8,5,16,128]{3,2,1,0:T(8,128)(2,1)S(1)} %all_to_all.10.x), custom_call_target="tpu_custom_call" | custom-call | flops 1 | bytes 1 | tf_op jit(solution)/shard_map/final/pallas_call | solution.py:313
  (2 shorter events, 0.0 us)
Async XLA Ops:
  1.0 19.8 %collective-permute-start = (bf16[1,72,512]{2,1,0:T(8,128)(2,1)S(1)}, bf16[1,72,512]{2,1,0:T(8,128)(2,1)S(1)}, u32[]{:S(2)}, u32[]{:S(2)}) collective-permute-start(bf16[1,72,512]{2,1,0:T(8,128)(2,1)S(1)} %get-tuple-element.11), channel_id=1, source_target_pairs={{0,449},{1,448},{64,385},{65,384},{128,321},{129,320},{192,257},{1... | collective-permute-start | bytes 221192 | tf_op jit(solution)/shard_map/ppermute | solution.py:300
  13.0 11.2 %collective-permute-start.1 = (bf16[1,352,128]{2,1,0:T(8,128)(2,1)S(1)}, bf16[1,352,128]{2,1,0:T(8,128)(2,1)S(1)}, u32[]{:S(2)}, u32[]{:S(2)}) collective-permute-start(bf16[1,352,128]{2,1,0:T(8,128)(2,1)S(1)} %get-tuple-element.12), channel_id=1, source_target_pairs={{0,256},{32,288},{64,320},{96,352},{128,384},{160,416},{192,448},{... | collective-permute-start | bytes 270344 | tf_op jit(solution)/shard_map/ppermute | solution.py:281
  24.2 25.5 %copy-start = (bf16[2,352,128]{2,1,0:T(8,128)(2,1)}, bf16[2,352,128]{2,1,0:T(8,128)(2,1)S(1)}, u32[]{:S(2)}) copy-start(bf16[2,352,128]{2,1,0:T(8,128)(2,1)S(1)} %pad_maximum_fusion.1.p0) | copy-start | bytes 540676
  25.9 33.0 %all-to-all-start = ((bf16[32,72,512]{2,1,0:T(8,128)(2,1)}), bf16[32,72,512]{2,1,0:T(8,128)(2,1)S(1)}, u32[]{:S(2)}, u32[]{:S(2)}) async-start(bf16[32,72,512]{2,1,0:T(8,128)(2,1)} %bitcast.9), calls=%async_computation | async-start | bytes 4718592 | tf_op jit(solution)/shard_map/all_to_all | solution.py:306
  32.6 9.3 %collective-permute-start.4 = (bf16[2,352,128]{2,1,0:T(8,128)(2,1)S(1)}, bf16[2,352,128]{2,1,0:T(8,128)(2,1)S(1)}, u32[]{:S(2)}, u32[]{:S(2)}) collective-permute-start(bf16[2,352,128]{2,1,0:T(8,128)(2,1)S(1)} %pad_maximum_fusion.1.p0), channel_id=1, source_target_pairs={{0,192},{32,224},{64,128},{96,160},{128,64},{160,96},{192,0},{224,... | collective-permute-start | bytes 540680 | tf_op jit(solution)/shard_map/ppermute | solution.py:281
  37.0 10.7 %collective-permute-start.3 = (bf16[2,352,128]{2,1,0:T(8,128)(2,1)S(1)}, bf16[2,352,128]{2,1,0:T(8,128)(2,1)S(1)}, u32[]{:S(2)}, u32[]{:S(2)}) collective-permute-start(bf16[2,352,128]{2,1,0:T(8,128)(2,1)S(1)} %pad_maximum_fusion.1.p0), channel_id=1, source_target_pairs={{0,128},{32,160},{64,192},{96,224},{128,0},{160,32},{192,64},{224,... | collective-permute-start | bytes 540680 | tf_op jit(solution)/shard_map/ppermute | solution.py:281
  38.9 10.8 %collective-permute-start.2 = (bf16[2,352,128]{2,1,0:T(8,128)(2,1)S(1)}, bf16[2,352,128]{2,1,0:T(8,128)(2,1)S(1)}, u32[]{:S(2)}, u32[]{:S(2)}) collective-permute-start(bf16[2,352,128]{2,1,0:T(8,128)(2,1)S(1)} %pad_maximum_fusion.1.p0), channel_id=1, source_target_pairs={{0,64},{32,96},{64,0},{96,32},{128,192},{160,224},{192,128},{224,1... | collective-permute-start | bytes 540680 | tf_op jit(solution)/shard_map/ppermute | solution.py:281
  41.9 16.9 %copy-start.1 = (bf16[2,352,128]{2,1,0:T(8,128)(2,1)}, bf16[2,352,128]{2,1,0:T(8,128)(2,1)S(1)}, u32[]{:S(2)}) copy-start(bf16[2,352,128]{2,1,0:T(8,128)(2,1)S(1)} %collective-permute-done.4.p3) | copy-start | bytes 540676
  47.7 11.2 %copy-start.2 = (bf16[2,352,128]{2,1,0:T(8,128)(2,1)}, bf16[2,352,128]{2,1,0:T(8,128)(2,1)S(1)}, u32[]{:S(2)}) copy-start(bf16[2,352,128]{2,1,0:T(8,128)(2,1)S(1)} %collective-permute-done.3.p2) | copy-start | bytes 540676
  49.7 9.2 %copy-start.3 = (bf16[2,352,128]{2,1,0:T(8,128)(2,1)}, bf16[2,352,128]{2,1,0:T(8,128)(2,1)S(1)}, u32[]{:S(2)}) copy-start(bf16[2,352,128]{2,1,0:T(8,128)(2,1)S(1)} %collective-permute-done.2.p1) | copy-start | bytes 540676
  50.6 8.2 %collective-permute-start.5 = (bf16[8,352,128]{2,1,0:T(8,128)(2,1)}, bf16[8,352,128]{2,1,0:T(8,128)(2,1)}, u32[]{:S(2)}, u32[]{:S(2)}) collective-permute-start(bf16[8,352,128]{2,1,0:T(8,128)(2,1)} %pad_maximum_fusion), channel_id=1, source_target_pairs={{0,32},{32,0},{64,96},{96,64},{128,160},{160,128},{192,224},{224,1... | collective-permute-start | bytes 2162696 | tf_op jit(solution)/shard_map/ppermute | solution.py:281
  68.3 9.3 %collective-permute-start.6 = (bf16[8,5,16,128]{3,2,1,0:T(8,128)(2,1)S(1)}, bf16[8,5,16,128]{3,2,1,0:T(8,128)(2,1)S(1)}, u32[]{:S(2)}, u32[]{:S(2)}) collective-permute-start(bf16[8,5,16,128]{3,2,1,0:T(8,128)(2,1)S(1)} %get-tuple-element.16), channel_id=1, source_target_pairs={{0,32},{32,0},{64,96},{96,64},{128,160},{160,128},{192,224},{224,1... | collective-permute-start | bytes 491528 | tf_op jit(solution)/shard_map/ppermute | solution.py:281

commit v8 on v6

--- a/solution.py
+++ b/solution.py
@@ -31,15 +31,13 @@
     return pl.BlockSpec(memory_space=pltpu.VMEM)
 
 
-def call(kernel, shape, n_in, name, scratch=(), room=8):
+def call(kernel, shape, n_in, name):
     return pl.pallas_call(
         kernel,
         out_shape=shape,
-        in_specs=[pl.BlockSpec(memory_space=pltpu.SMEM)] + [vmem()] * n_in,
-        out_specs=jax.tree.map(lambda _: vmem(), shape),
-        scratch_shapes=list(scratch),
-        compiler_params=pltpu.CompilerParams(vmem_limit_bytes=room * MIB),
-        cost_estimate=pl.CostEstimate(flops=1, transcendentals=0, bytes_accessed=1),
+        in_specs=[vmem()] * n_in,
+        out_specs=vmem(),
+        compiler_params=pltpu.CompilerParams(vmem_limit_bytes=8 * MIB),
         name=name,
     )
 
@@ -154,7 +152,7 @@
     return t[..., k : k + 1] + t[..., k + 1 : k + 2] + t[..., k + 2 : k + 3]
 
 
-def attention_kernel(place, p0, p1, p2, p3, p4, chunk, keep, send, keys, turns, parts, *scratch):
+def attention_kernel(place, token, p0, p1, p2, p3, p4, chunk, keep, send, keys, turns, parts, *scratch):
     me, zh, prior = place[0], place[1], place[2]
     zl, co = lax.shift_right_logical(me, 1), lax.bitwise_and(me, 1)
     tiles, pieces, panel, lats, rots, values, sems = scratch
@@ -227,7 +225,7 @@
     return pl.pallas_call(
         attention_kernel,
         out_shape=(shaped((8, HEADS + 1, TOK, 128)),) * 2,
-        in_specs=[pl.BlockSpec(memory_space=pltpu.SMEM)] + [hbm] * 5 + [vmem()],
+        in_specs=[pl.BlockSpec(memory_space=pltpu.SMEM)] + [hbm] * 6 + [vmem()],
         out_specs=(vmem(), vmem()),
         scratch_shapes=[
             pltpu.VMEM((2, SLOTS, LATENT), bf16),
@@ -246,6 +244,27 @@
     )(place, *(pltpu.with_memory_space_constraint(p, pltpu.HBM) for p in pieces), slots)
 
 
+def arrival_kernel(last, out, token, sem):
+    token[...] = jnp.zeros_like(token)
+    copy = pltpu.make_async_copy(token, out, sem)
+    copy.start()
+    copy.wait()
+
+
+def arrival(last):
+    hbm = pl.BlockSpec(memory_space=pltpu.HBM)
+    return pl.pallas_call(
+        arrival_kernel,
+        out_shape=pltpu.HBM((8, 128), f32),
+        in_specs=[hbm],
+        out_specs=hbm,
+        scratch_shapes=[pltpu.VMEM((8, 128), f32), pltpu.SemaphoreType.DMA],
+        cost_estimate=pl.CostEstimate(flops=11500000000, transcendentals=0, bytes_accessed=0),
+        compiler_params=pltpu.CompilerParams(vmem_limit_bytes=MIB),
+        name="arrival",
+    )(pltpu.with_memory_space_constraint(last, pltpu.HBM))
+
+
 def merge_heads(blocks):
     tile = blocks[HEADS]
     values, lses = [], []
@@ -259,7 +278,7 @@
     return values, lses
 
 
-def pair_kernel(place, a, b, out):
+def pair_kernel(a, b, out):
     rows = 8 * TOK
     blocks = [
         jnp.concatenate([r[:, h].reshape(1, rows, 128) for r in (a, b)], axis=0)
@@ -271,7 +290,7 @@
     out[:, HEADS] = pack_lse(lses, (rows, 128)).reshape(8, TOK, 128)
 
 
-def final_kernel(place, x, out):
+def final_kernel(x, out):
     values, _ = merge_heads([x[:, h] for h in range(HEADS + 1)])
     for h in range(HEADS):
         out[:, h * VALUE : (h + 1) * VALUE] = values[h].astype(bf16)
@@ -298,17 +317,18 @@
     )
 
     mirror = lax.ppermute(shard, ("zq", "zr", "zh"), [(i, 15 - i) for i in range(16)])
-    mirror, pack = lax.optimization_barrier((mirror, pack))
+    pack2 = jnp.concatenate([pack, swap(pack, 8)], axis=0)
+    _, pack2 = lax.optimization_barrier((mirror, pack2))
     pair = jnp.concatenate([shard, mirror], axis=0)
     slots = gather(pair, ("x", "y"), 16)
-    pack2 = jnp.concatenate([pack, swap(pack, 8)], axis=0)
     fans = [swap(pack2, d) for d in (2, 4, 6)]
     pack8 = jnp.concatenate([pack2] + fans, axis=0)
 
-    keep, send = attend(place, slots, pack2, *fans, swap(pack8, 1))
-    merged = call(pair_kernel, shaped((8, HEADS + 1, TOK, 128)), 2, "pair")(place, keep, swap(send, 1))
+    last = swap(pack8, 1)
+    keep, send = attend(place, slots, arrival(last), pack2, *fans, last)
+    merged = call(pair_kernel, shaped((8, HEADS + 1, TOK, 128)), 2, "pair")(keep, swap(send, 1))
     spread = lax.all_to_all(merged, ZL, 0, 0, tiled=True)
-    return call(final_kernel, shaped((TOK, HEADS * VALUE)), 1, "final")(place, spread)
+    return call(final_kernel, shaped((TOK, HEADS * VALUE)), 1, "final")(spread)
 
 
 def solution(mesh):

time: 105 us -> 94.5 us (0.900)
  the two profiles are of different devices: /device:TPU:2 before, /device:TPU:1 now
where the time goes in v8:
time: 94.5 us; the launch traced here: 92.9 us
  starting transfers between devices  47.2 us (50%)
  blocking collectives  15.8 us (17%)
  waiting for transfers between devices  13.9 us (15%)
  Pallas kernels  12.3 us (13%)
  local copies, waits for them, and re-layouts  1.71 us (2%)
  other arithmetic  1.09 us (1%)
    ppermute x6, starting transfers between devices, swap(): return lax.ppermute(x, CTX, [(i, i ^ d) for i in range(16)])  28.5 us
    all_to_all x1, blocking collectives, per_device(): spread = lax.all_to_all(merged, ZL, 0, 0, tiled=True)  15.8 us
    ppermute x1, starting transfers between devices, per_device(): lax.ppermute(shard, ('zq', 'zr', 'zh'), [(i, 15 - i) for i in range(16)])  12 us
    ppermute x6, waiting for transfers between devices, swap(): return lax.ppermute(x, CTX, [(i, i ^ d) for i in range(16)])  11.2 us
    pallas_call x1, Pallas kernels, attend(): pl.pallas_call(attention_kernel, out_shape=(shaped((8, HEADS + 1, TOK, 12...  9.39 us
    all_to_all x1, starting transfers between devices, gather(): return lax.all_to_all(copies, axes, 0, 0, tiled=True)  6.75 us
    all_to_all x1, waiting for transfers between devices, gather(): return lax.all_to_all(copies, axes, 0, 0, tiled=True)  2.68 us
  transfers between devices with their start and end apart: 8, of which 4 were waited for; matrix products, arithmetic and copies ran while one was open for 3% of the time, Pallas kernels for 1%

profile of v8, /device:TPU:1, one launch (start us, length us, event | category | flops | bytes accessed | tf_op | source)
XLA Modules:
  0.0 92.9 jit_solution(13994463359640636673)
XLA Ops:
  0.0 1.0 %prepare.1 = (bf16[1,72,512]{2,1,0:T(8,128)(2,1)S(1)}, bf16[1,352,128]{2,1,0:T(8,128)(2,1)S(1)}) custom-call(bf16[16,768]{1,0:T(8,128)(2,1)} %queries_hbm.1, bf16[64,576]{1,0:T(8,128)(2,1)} %cache_hbm.1, bf16[128,128]{1,0:T(8,128)(2,1)} %bitcast.10, bf16[128,128]{1,0:T(8,128)(2,1)} %bitcast.11), custom_call_target="tpu_custom_call" | custom-call | tf_op jit(solution)/shard_map/prepare/pallas_call | solution.py:77
  1.0 12.0 %collective-permute-start = (bf16[1,72,512]{2,1,0:T(8,128)(2,1)S(1)}, bf16[1,72,512]{2,1,0:T(8,128)(2,1)S(1)}, u32[]{:S(2)}, u32[]{:S(2)}) collective-permute-start(bf16[1,72,512]{2,1,0:T(8,128)(2,1)S(1)} %get-tuple-element.10), channel_id=1, source_target_pairs={{0,449},{1,448},{64,385},{65,384},{128,321},{129,320},{192,257},{1... | collective-permute-start | bytes 221192 | tf_op jit(solution)/shard_map/ppermute | solution.py:319
  13.0 7.9 %collective-permute-start.1 = (bf16[1,352,128]{2,1,0:T(8,128)(2,1)S(1)}, bf16[1,352,128]{2,1,0:T(8,128)(2,1)S(1)}, u32[]{:S(2)}, u32[]{:S(2)}) collective-permute-start(bf16[1,352,128]{2,1,0:T(8,128)(2,1)S(1)} %get-tuple-element.11), channel_id=1, source_target_pairs={{0,256},{32,288},{64,320},{96,352},{128,384},{160,416},{192,448},{... | collective-permute-start | bytes 270344 | tf_op jit(solution)/shard_map/ppermute | solution.py:300
  20.9 0.0 collective-permute-done
  20.9 1.7 %broadcast_in_dim.2 = bf16[16,2,72,512]{3,2,1,0:T(8,128)(2,1)} broadcast(bf16[2,72,512]{2,1,0:T(8,128)(2,1)S(1)} %pad_maximum_fusion.2), dimensions={1,2,3} | broadcast | bytes 2506752 | tf_op jit(solution)/shard_map/broadcast_in_dim | solution.py:304
  22.6 6.8 %all-to-all-start = ((bf16[32,72,512]{2,1,0:T(8,128)(2,1)}), bf16[32,72,512]{2,1,0:T(8,128)(2,1)S(1)}, u32[]{:S(2)}, u32[]{:S(2)}) async-start(bf16[32,72,512]{2,1,0:T(8,128)(2,1)} %bitcast.9), calls=%async_computation | async-start | bytes 4718592 | tf_op jit(solution)/shard_map/all_to_all | solution.py:305
  29.4 0.0 collective-permute-done.1
  29.4 0.0 copy-start
  29.4 1.9 %collective-permute-start.4 = (bf16[2,352,128]{2,1,0:T(8,128)(2,1)S(1)}, bf16[2,352,128]{2,1,0:T(8,128)(2,1)S(1)}, u32[]{:S(2)}, u32[]{:S(2)}) collective-permute-start(bf16[2,352,128]{2,1,0:T(8,128)(2,1)S(1)} %pad_maximum_fusion.1.p0), channel_id=1, source_target_pairs={{0,192},{32,224},{64,128},{96,160},{128,64},{160,96},{192,0},{224,... | collective-permute-start | bytes 540680 | tf_op jit(solution)/shard_map/ppermute | solution.py:300
  31.3 2.9 %collective-permute-start.3 = (bf16[2,352,128]{2,1,0:T(8,128)(2,1)S(1)}, bf16[2,352,128]{2,1,0:T(8,128)(2,1)S(1)}, u32[]{:S(2)}, u32[]{:S(2)}) collective-permute-start(bf16[2,352,128]{2,1,0:T(8,128)(2,1)S(1)} %pad_maximum_fusion.1.p0), channel_id=1, source_target_pairs={{0,128},{32,160},{64,192},{96,224},{128,0},{160,32},{192,64},{224,... | collective-permute-start | bytes 540680 | tf_op jit(solution)/shard_map/ppermute | solution.py:300
  34.2 4.4 %collective-permute-start.2 = (bf16[2,352,128]{2,1,0:T(8,128)(2,1)S(1)}, bf16[2,352,128]{2,1,0:T(8,128)(2,1)S(1)}, u32[]{:S(2)}, u32[]{:S(2)}) collective-permute-start(bf16[2,352,128]{2,1,0:T(8,128)(2,1)S(1)} %pad_maximum_fusion.1.p0), channel_id=1, source_target_pairs={{0,64},{32,96},{64,0},{96,32},{128,192},{160,224},{192,128},{224,1... | collective-permute-start | bytes 540680 | tf_op jit(solution)/shard_map/ppermute | solution.py:300
  38.7 0.0 collective-permute-done.4.p3
  38.7 0.0 copy-start.1
  38.7 8.8 %collective-permute-done.3.p2 = bf16[2,352,128]{2,1,0:T(8,128)(2,1)S(1)} collective-permute-done((bf16[2,352,128]{2,1,0:T(8,128)(2,1)S(1)}, bf16[2,352,128]{2,1,0:T(8,128)(2,1)S(1)}, u32[]{:S(2)}, u32[]{:S(2)}) %collective-permute-start.3) | collective-permute-done | bytes 180256 | tf_op jit(solution)/shard_map/ppermute | solution.py:300
  47.5 0.0 copy-start.2
  47.5 0.0 collective-permute-done.2.p1
  47.5 0.0 copy-start.3
  47.5 1.0 %pad_maximum_fusion = bf16[8,352,128]{2,1,0:T(8,128)(2,1)} fusion(bf16[2,352,128]{2,1,0:T(8,128)(2,1)S(1)} %collective-permute-done.4.p3, bf16[2,352,128]{2,1,0:T(8,128)(2,1)S(1)} %collective-permute-done.3.p2, bf16[2,352,128]{2,1,0:T(8,128)(2,1)S(1)} %collective-permute-done.2.p1, bf16[2,352,128]{2,1,0:T(8,128)(2,1)S(1)} %pad_maximum_fusion.1.p0), kind=kLoop, calls=%fused_computation | loop fusion | flops 1081344 | bytes 1441792 | tf_op jit(solution)/shard_map/concatenate | solution.py:325
  48.5 3.8 %collective-permute-start.5 = (bf16[8,352,128]{2,1,0:T(8,128)(2,1)}, bf16[8,352,128]{2,1,0:T(8,128)(2,1)}, u32[]{:S(2)}, u32[]{:S(2)}) collective-permute-start(bf16[8,352,128]{2,1,0:T(8,128)(2,1)} %pad_maximum_fusion), channel_id=1, source_target_pairs={{0,32},{32,0},{64,96},{96,64},{128,160},{160,128},{192,224},{224,1... | collective-permute-start | bytes 2162696 | tf_op jit(solution)/shard_map/ppermute | solution.py:300
  53.0 0.1 pad_add_fusion.place
  53.1 1.4 %collective-permute-done.5.last.p4 = bf16[8,352,128]{2,1,0:T(8,128)(2,1)} collective-permute-done((bf16[8,352,128]{2,1,0:T(8,128)(2,1)}, bf16[8,352,128]{2,1,0:T(8,128)(2,1)}, u32[]{:S(2)}, u32[]{:S(2)}) %collective-permute-start.5) | collective-permute-done | bytes 720928 | tf_op jit(solution)/shard_map/ppermute | solution.py:300
  54.5 0.6 arrival.1.token
  55.1 0.0 copy-done
  55.1 0.0 copy-done.1
  55.1 0.0 copy-done.2
  55.1 0.0 copy-done.3
  55.1 2.7 %all-to-all-done.chunk = bf16[32,72,512]{2,1,0:T(8,128)(2,1)S(1)} async-done(((bf16[32,72,512]{2,1,0:T(8,128)(2,1)}), bf16[32,72,512]{2,1,0:T(8,128)(2,1)S(1)}, u32[]{:S(2)}, u32[]{:S(2)}) %all-to-all-start) | async-done | bytes 2359328 | tf_op jit(solution)/shard_map/all_to_all | solution.py:305
  57.8 9.4 %attention.1 = (bf16[8,5,16,128]{3,2,1,0:T(8,128)(2,1)S(1)}, bf16[8,5,16,128]{3,2,1,0:T(8,128)(2,1)S(1)}) custom-call(s32[3]{0:T(128)S(1)} %pad_add_fusion.place, f32[8,128]{1,0:T(8,128)} %arrival.1.token, bf16[2,352,128]{2,1,0:T(8,128)(2,1)} %copy-done, bf16[2,352,128]{2,1,0:T(8,128)(2,1)} %copy-done.3, bf16[2,352,128]{2,1,0:T(8,128)(2,1)} %copy-done.2, ...), custom_call_target="tpu_custom_call" | custom-call | tf_op jit(solution)/shard_map/attention/pallas_call | solution.py:225
  67.2 7.6 %collective-permute-start.6 = (bf16[8,5,16,128]{3,2,1,0:T(8,128)(2,1)S(1)}, bf16[8,5,16,128]{3,2,1,0:T(8,128)(2,1)S(1)}, u32[]{:S(2)}, u32[]{:S(2)}) collective-permute-start(bf16[8,5,16,128]{3,2,1,0:T(8,128)(2,1)S(1)} %get-tuple-element.14), channel_id=1, source_target_pairs={{0,32},{32,0},{64,96},{96,64},{128,160},{160,128},{192,224},{224,1... | collective-permute-start | bytes 491528 | tf_op jit(solution)/shard_map/ppermute | solution.py:300
  74.8 1.0 %collective-permute-done.6.b = bf16[8,5,16,128]{3,2,1,0:T(8,128)(2,1)S(1)} collective-permute-done((bf16[8,5,16,128]{3,2,1,0:T(8,128)(2,1)S(1)}, bf16[8,5,16,128]{3,2,1,0:T(8,128)(2,1)S(1)}, u32[]{:S(2)}, u32[]{:S(2)}) %collective-permute-start.6) | collective-permute-done | bytes 163872 | tf_op jit(solution)/shard_map/ppermute | solution.py:300
  75.8 0.5 pair.1
  76.3 15.8 %all_to_all.10.x = bf16[8,5,16,128]{3,2,1,0:T(8,128)(2,1)S(1)} all-to-all(bf16[8,5,16,128]{3,2,1,0:T(8,128)(2,1)S(1)} %pair.1), channel_id=1, replica_groups=mesh['zq'=2,'zr'=4,'co'=2,'x'=4,'y'=4,'zh'=2] {'zq','zr'}, dimensions={0} | all-to-all | bytes 327680 | tf_op jit(solution)/shard_map/all_to_all | solution.py:330
  92.1 0.9 final.1
  (2 shorter events, 0.0 us)
Async XLA Ops:
  1.0 19.8 %collective-permute-start = (bf16[1,72,512]{2,1,0:T(8,128)(2,1)S(1)}, bf16[1,72,512]{2,1,0:T(8,128)(2,1)S(1)}, u32[]{:S(2)}, u32[]{:S(2)}) collective-permute-start(bf16[1,72,512]{2,1,0:T(8,128)(2,1)S(1)} %get-tuple-element.10), channel_id=1, source_target_pairs={{0,449},{1,448},{64,385},{65,384},{128,321},{129,320},{192,257},{1... | collective-permute-start | bytes 221192 | tf_op jit(solution)/shard_map/ppermute | solution.py:319
  13.0 16.4 %collective-permute-start.1 = (bf16[1,352,128]{2,1,0:T(8,128)(2,1)S(1)}, bf16[1,352,128]{2,1,0:T(8,128)(2,1)S(1)}, u32[]{:S(2)}, u32[]{:S(2)}) collective-permute-start(bf16[1,352,128]{2,1,0:T(8,128)(2,1)S(1)} %get-tuple-element.11), channel_id=1, source_target_pairs={{0,256},{32,288},{64,320},{96,352},{128,384},{160,416},{192,448},{... | collective-permute-start | bytes 270344 | tf_op jit(solution)/shard_map/ppermute | solution.py:300
  22.6 35.2 %all-to-all-start = ((bf16[32,72,512]{2,1,0:T(8,128)(2,1)}), bf16[32,72,512]{2,1,0:T(8,128)(2,1)S(1)}, u32[]{:S(2)}, u32[]{:S(2)}) async-start(bf16[32,72,512]{2,1,0:T(8,128)(2,1)} %bitcast.9), calls=%async_computation | async-start | bytes 4718592 | tf_op jit(solution)/shard_map/all_to_all | solution.py:305
  29.4 25.7 %copy-start = (bf16[2,352,128]{2,1,0:T(8,128)(2,1)}, bf16[2,352,128]{2,1,0:T(8,128)(2,1)S(1)}, u32[]{:S(2)}) copy-start(bf16[2,352,128]{2,1,0:T(8,128)(2,1)S(1)} %pad_maximum_fusion.1.p0) | copy-start | bytes 540676
  29.4 9.3 %collective-permute-start.4 = (bf16[2,352,128]{2,1,0:T(8,128)(2,1)S(1)}, bf16[2,352,128]{2,1,0:T(8,128)(2,1)S(1)}, u32[]{:S(2)}, u32[]{:S(2)}) collective-permute-start(bf16[2,352,128]{2,1,0:T(8,128)(2,1)S(1)} %pad_maximum_fusion.1.p0), channel_id=1, source_target_pairs={{0,192},{32,224},{64,128},{96,160},{128,64},{160,96},{192,0},{224,... | collective-permute-start | bytes 540680 | tf_op jit(solution)/shard_map/ppermute | solution.py:300
  31.3 16.2 %collective-permute-start.3 = (bf16[2,352,128]{2,1,0:T(8,128)(2,1)S(1)}, bf16[2,352,128]{2,1,0:T(8,128)(2,1)S(1)}, u32[]{:S(2)}, u32[]{:S(2)}) collective-permute-start(bf16[2,352,128]{2,1,0:T(8,128)(2,1)S(1)} %pad_maximum_fusion.1.p0), channel_id=1, source_target_pairs={{0,128},{32,160},{64,192},{96,224},{128,0},{160,32},{192,64},{224,... | collective-permute-start | bytes 540680 | tf_op jit(solution)/shard_map/ppermute | solution.py:300
  34.2 13.3 %collective-permute-start.2 = (bf16[2,352,128]{2,1,0:T(8,128)(2,1)S(1)}, bf16[2,352,128]{2,1,0:T(8,128)(2,1)S(1)}, u32[]{:S(2)}, u32[]{:S(2)}) collective-permute-start(bf16[2,352,128]{2,1,0:T(8,128)(2,1)S(1)} %pad_maximum_fusion.1.p0), channel_id=1, source_target_pairs={{0,64},{32,96},{64,0},{96,32},{128,192},{160,224},{192,128},{224,1... | collective-permute-start | bytes 540680 | tf_op jit(solution)/shard_map/ppermute | solution.py:300
  38.7 16.4 %copy-start.1 = (bf16[2,352,128]{2,1,0:T(8,128)(2,1)}, bf16[2,352,128]{2,1,0:T(8,128)(2,1)S(1)}, u32[]{:S(2)}) copy-start(bf16[2,352,128]{2,1,0:T(8,128)(2,1)S(1)} %collective-permute-done.4.p3) | copy-start | bytes 540676
  47.5 7.6 %copy-start.2 = (bf16[2,352,128]{2,1,0:T(8,128)(2,1)}, bf16[2,352,128]{2,1,0:T(8,128)(2,1)S(1)}, u32[]{:S(2)}) copy-start(bf16[2,352,128]{2,1,0:T(8,128)(2,1)S(1)} %collective-permute-done.3.p2) | copy-start | bytes 540676
  47.5 7.6 %copy-start.3 = (bf16[2,352,128]{2,1,0:T(8,128)(2,1)}, bf16[2,352,128]{2,1,0:T(8,128)(2,1)S(1)}, u32[]{:S(2)}) copy-start(bf16[2,352,128]{2,1,0:T(8,128)(2,1)S(1)} %collective-permute-done.2.p1) | copy-start | bytes 540676
  48.5 6.0 %collective-permute-start.5 = (bf16[8,352,128]{2,1,0:T(8,128)(2,1)}, bf16[8,352,128]{2,1,0:T(8,128)(2,1)}, u32[]{:S(2)}, u32[]{:S(2)}) collective-permute-start(bf16[8,352,128]{2,1,0:T(8,128)(2,1)} %pad_maximum_fusion), channel_id=1, source_target_pairs={{0,32},{32,0},{64,96},{96,64},{128,160},{160,128},{192,224},{224,1... | collective-permute-start | bytes 2162696 | tf_op jit(solution)/shard_map/ppermute | solution.py:300
  67.2 8.6 %collective-permute-start.6 = (bf16[8,5,16,128]{3,2,1,0:T(8,128)(2,1)S(1)}, bf16[8,5,16,128]{3,2,1,0:T(8,128)(2,1)S(1)}, u32[]{:S(2)}, u32[]{:S(2)}) collective-permute-start(bf16[8,5,16,128]{3,2,1,0:T(8,128)(2,1)S(1)} %get-tuple-element.14), channel_id=1, source_target_pairs={{0,32},{32,0},{64,96},{96,64},{128,160},{160,128},{192,224},{224,1... | collective-permute-start | bytes 491528 | tf_op jit(solution)/shard_map/ppermute | solution.py:300

commit v9 on v8

--- a/solution.py
+++ b/solution.py
@@ -259,7 +259,7 @@
         in_specs=[hbm],
         out_specs=hbm,
         scratch_shapes=[pltpu.VMEM((8, 128), f32), pltpu.SemaphoreType.DMA],
-        cost_estimate=pl.CostEstimate(flops=11500000000, transcendentals=0, bytes_accessed=0),
+        cost_estimate=pl.CostEstimate(flops=11000000000, transcendentals=0, bytes_accessed=0),
         compiler_params=pltpu.CompilerParams(vmem_limit_bytes=MIB),
         name="arrival",
     )(pltpu.with_memory_space_constraint(last, pltpu.HBM))
@@ -300,9 +300,30 @@
     return lax.ppermute(x, CTX, [(i, i ^ d) for i in range(16)])
 
 
-def gather(x, axes, n):
-    copies = jnp.broadcast_to(x[None], (n, *x.shape)).reshape(n * x.shape[0], *x.shape[1:])
-    return lax.all_to_all(copies, axes, 0, 0, tiled=True)
+def replicate(half, block, copies=None):
+    hbm = pl.BlockSpec(memory_space=pltpu.HBM)
+
+    def spread_kernel(block, *refs):
+        out, sems = refs[-2:]
+        writes = [
+            pltpu.make_async_copy(block, out.at[n, half : half + 1], sems.at[n]) for n in range(16)
+        ]
+        for w in writes:
+            w.start()
+        for w in writes:
+            w.wait()
+
+    operands = (block,) if copies is None else (block, copies)
+    return pl.pallas_call(
+        spread_kernel,
+        out_shape=pltpu.HBM((16, 2, 72, LATENT), bf16),
+        in_specs=[vmem()] + [hbm] * (len(operands) - 1),
+        out_specs=hbm,
+        scratch_shapes=[pltpu.SemaphoreType.DMA((16,))],
+        input_output_aliases={} if copies is None else {1: 0},
+        compiler_params=pltpu.CompilerParams(vmem_limit_bytes=MIB),
+        name=f"spread{half}",
+    )(*operands)
 
 
 def per_device(queries, cache, key_up_weight, value_up_weight, prior_len):
@@ -319,8 +340,8 @@
     mirror = lax.ppermute(shard, ("zq", "zr", "zh"), [(i, 15 - i) for i in range(16)])
     pack2 = jnp.concatenate([pack, swap(pack, 8)], axis=0)
     _, pack2 = lax.optimization_barrier((mirror, pack2))
-    pair = jnp.concatenate([shard, mirror], axis=0)
-    slots = gather(pair, ("x", "y"), 16)
+    copies = replicate(1, mirror, replicate(0, shard))
+    slots = lax.all_to_all(copies.reshape(32, 72, LATENT), ("x", "y"), 0, 0, tiled=True)
     fans = [swap(pack2, d) for d in (2, 4, 6)]
     pack8 = jnp.concatenate([pack2] + fans, axis=0)
 

time: 94.5 us -> 94.7 us (level)
  Pallas kernels: 12.3 us -> 14.8 us
  local copies, waits for them, and re-layouts: 1.71 us -> 0.02 us
    pallas_call x0 -> x2, Pallas kernels: none -> 2.49 us  [replicate(): pl.pallas_call(spread_kernel, out_shape=pltpu.HBM((16, 2, 72, LATENT), bf...]
    broadcast_in_dim x1 -> x0, local copies, waits for them, and re-layouts: 1.69 us -> none  [gather(): jnp.broadcast_to(x[None], (n, *x.shape))]
  transfers between devices with their start and end apart: 8 -> 8, of which waited for: 4 -> 4; matrix products, arithmetic and copies ran while one was open for 3% -> 1% of each run, Pallas kernels for 1% -> 3%
where the time goes in v9:
time: 94.7 us; the launch traced here: 93.2 us
  starting transfers between devices  47.2 us (50%)
  blocking collectives  15.3 us (16%)
  Pallas kernels  14.8 us (16%)
  waiting for transfers between devices  13.9 us (15%)
  other arithmetic  1.07 us (1%)
    ppermute x6, starting transfers between devices, swap(): return lax.ppermute(x, CTX, [(i, i ^ d) for i in range(16)])  28.5 us
    all_to_all x1, blocking collectives, per_device(): spread = lax.all_to_all(merged, ZL, 0, 0, tiled=True)  15.3 us
    ppermute x1, starting transfers between devices, per_device(): lax.ppermute(shard, ('zq', 'zr', 'zh'), [(i, 15 - i) for i in range(16)])  12 us
    ppermute x6, waiting for transfers between devices, swap(): return lax.ppermute(x, CTX, [(i, i ^ d) for i in range(16)])  11.2 us
    pallas_call x1, Pallas kernels, attend(): pl.pallas_call(attention_kernel, out_shape=(shaped((8, HEADS + 1, TOK, 12...  9.39 us
    all_to_all x1, starting transfers between devices, per_device(): lax.all_to_all(copies.reshape(32, 72, LATENT), ('x', 'y'), 0, 0, tiled=True)  6.77 us
    all_to_all x1, waiting for transfers between devices, per_device(): lax.all_to_all(copies.reshape(32, 72, LATENT), ('x', 'y'), 0, 0, tiled=True)  2.68 us
    pallas_call x2, Pallas kernels, replicate(): pl.pallas_call(spread_kernel, out_shape=pltpu.HBM((16, 2, 72, LATENT), bf...  2.49 us
  transfers between devices with their start and end apart: 8, of which 4 were waited for; matrix products, arithmetic and copies ran while one was open for 1% of the time, Pallas kernels for 3%

profile of v9, /device:TPU:1, one launch (start us, length us, event | category | flops | bytes accessed | tf_op | source)
XLA Modules:
  0.0 93.2 jit_solution(15654623009712219181)
XLA Ops:
  0.0 1.0 %prepare.1 = (bf16[1,72,512]{2,1,0:T(8,128)(2,1)S(1)}, bf16[1,352,128]{2,1,0:T(8,128)(2,1)S(1)}) custom-call(bf16[16,768]{1,0:T(8,128)(2,1)} %queries_hbm.1, bf16[64,576]{1,0:T(8,128)(2,1)} %cache_hbm.1, bf16[128,128]{1,0:T(8,128)(2,1)} %bitcast.10, bf16[128,128]{1,0:T(8,128)(2,1)} %bitcast.11), custom_call_target="tpu_custom_call" | custom-call | tf_op jit(solution)/shard_map/prepare/pallas_call | solution.py:77
  1.0 12.0 %collective-permute-start = (bf16[1,72,512]{2,1,0:T(8,128)(2,1)S(1)}, bf16[1,72,512]{2,1,0:T(8,128)(2,1)S(1)}, u32[]{:S(2)}, u32[]{:S(2)}) collective-permute-start(bf16[1,72,512]{2,1,0:T(8,128)(2,1)S(1)} %get-tuple-element.10.block), channel_id=1, source_target_pairs={{0,449},{1,448},{64,385},{65,384},{128,321},{129,320},{192,257},{1... | collective-permute-start | bytes 221192 | tf_op jit(solution)/shard_map/ppermute | solution.py:340
  13.0 7.9 %collective-permute-start.1 = (bf16[1,352,128]{2,1,0:T(8,128)(2,1)S(1)}, bf16[1,352,128]{2,1,0:T(8,128)(2,1)S(1)}, u32[]{:S(2)}, u32[]{:S(2)}) collective-permute-start(bf16[1,352,128]{2,1,0:T(8,128)(2,1)S(1)} %get-tuple-element.11), channel_id=1, source_target_pairs={{0,256},{32,288},{64,320},{96,352},{128,384},{160,416},{192,448},{... | collective-permute-start | bytes 270344 | tf_op jit(solution)/shard_map/ppermute | solution.py:300
  20.9 1.3 %spread0.1.refs_0_ = bf16[16,2,72,512]{3,2,1,0:T(8,128)(2,1)} custom-call(bf16[1,72,512]{2,1,0:T(8,128)(2,1)S(1)} %get-tuple-element.10.block), custom_call_target="tpu_custom_call" | custom-call | tf_op jit(solution)/shard_map/spread0/pallas_call | solution.py:317
  22.1 0.0 collective-permute-done.block
  22.1 1.2 %spread1.1 = bf16[16,2,72,512]{3,2,1,0:T(8,128)(2,1)} custom-call(bf16[1,72,512]{2,1,0:T(8,128)(2,1)S(1)} %collective-permute-done.block, bf16[16,2,72,512]{3,2,1,0:T(8,128)(2,1)} %spread0.1.refs_0_), custom_call_target="tpu_custom_call", output_to_operand_aliasing={{}: (1, {})} | custom-call | tf_op jit(solution)/shard_map/spread1/pallas_call | solution.py:317
  23.4 6.8 %all-to-all-start = ((bf16[32,72,512]{2,1,0:T(8,128)(2,1)}), bf16[32,72,512]{2,1,0:T(8,128)(2,1)S(1)}, u32[]{:S(2)}, u32[]{:S(2)}) async-start(bf16[32,72,512]{2,1,0:T(8,128)(2,1)} %bitcast.9), calls=%async_computation | async-start | bytes 4718592 | tf_op jit(solution)/shard_map/all_to_all | solution.py:344
  30.1 0.0 collective-permute-done.1
  30.2 0.0 copy-start
  30.2 1.9 %collective-permute-start.4 = (bf16[2,352,128]{2,1,0:T(8,128)(2,1)S(1)}, bf16[2,352,128]{2,1,0:T(8,128)(2,1)S(1)}, u32[]{:S(2)}, u32[]{:S(2)}) collective-permute-start(bf16[2,352,128]{2,1,0:T(8,128)(2,1)S(1)} %pad_maximum_fusion.1.p0), channel_id=1, source_target_pairs={{0,192},{32,224},{64,128},{96,160},{128,64},{160,96},{192,0},{224,... | collective-permute-start | bytes 540680 | tf_op jit(solution)/shard_map/ppermute | solution.py:300
  32.1 2.9 %collective-permute-start.3 = (bf16[2,352,128]{2,1,0:T(8,128)(2,1)S(1)}, bf16[2,352,128]{2,1,0:T(8,128)(2,1)S(1)}, u32[]{:S(2)}, u32[]{:S(2)}) collective-permute-start(bf16[2,352,128]{2,1,0:T(8,128)(2,1)S(1)} %pad_maximum_fusion.1.p0), channel_id=1, source_target_pairs={{0,128},{32,160},{64,192},{96,224},{128,0},{160,32},{192,64},{224,... | collective-permute-start | bytes 540680 | tf_op jit(solution)/shard_map/ppermute | solution.py:300
  35.0 4.4 %collective-permute-start.2 = (bf16[2,352,128]{2,1,0:T(8,128)(2,1)S(1)}, bf16[2,352,128]{2,1,0:T(8,128)(2,1)S(1)}, u32[]{:S(2)}, u32[]{:S(2)}) collective-permute-start(bf16[2,352,128]{2,1,0:T(8,128)(2,1)S(1)} %pad_maximum_fusion.1.p0), channel_id=1, source_target_pairs={{0,64},{32,96},{64,0},{96,32},{128,192},{160,224},{192,128},{224,1... | collective-permute-start | bytes 540680 | tf_op jit(solution)/shard_map/ppermute | solution.py:300
  39.5 0.0 collective-permute-done.4.p3
  39.5 0.0 copy-start.1
  39.5 8.8 %collective-permute-done.3.p2 = bf16[2,352,128]{2,1,0:T(8,128)(2,1)S(1)} collective-permute-done((bf16[2,352,128]{2,1,0:T(8,128)(2,1)S(1)}, bf16[2,352,128]{2,1,0:T(8,128)(2,1)S(1)}, u32[]{:S(2)}, u32[]{:S(2)}) %collective-permute-start.3) | collective-permute-done | bytes 180256 | tf_op jit(solution)/shard_map/ppermute | solution.py:300
  48.3 0.0 copy-start.2
  48.3 0.0 collective-permute-done.2.p1
  48.3 0.0 copy-start.3
  48.3 1.0 %pad_maximum_fusion = bf16[8,352,128]{2,1,0:T(8,128)(2,1)} fusion(bf16[2,352,128]{2,1,0:T(8,128)(2,1)S(1)} %collective-permute-done.4.p3, bf16[2,352,128]{2,1,0:T(8,128)(2,1)S(1)} %collective-permute-done.3.p2, bf16[2,352,128]{2,1,0:T(8,128)(2,1)S(1)} %collective-permute-done.2.p1, bf16[2,352,128]{2,1,0:T(8,128)(2,1)S(1)} %pad_maximum_fusion.1.p0), kind=kLoop, calls=%fused_computation | loop fusion | flops 1081344 | bytes 1441792 | tf_op jit(solution)/shard_map/concatenate | solution.py:346
  49.3 3.8 %collective-permute-start.5 = (bf16[8,352,128]{2,1,0:T(8,128)(2,1)}, bf16[8,352,128]{2,1,0:T(8,128)(2,1)}, u32[]{:S(2)}, u32[]{:S(2)}) collective-permute-start(bf16[8,352,128]{2,1,0:T(8,128)(2,1)} %pad_maximum_fusion), channel_id=1, source_target_pairs={{0,32},{32,0},{64,96},{96,64},{128,160},{160,128},{192,224},{224,1... | collective-permute-start | bytes 2162696 | tf_op jit(solution)/shard_map/ppermute | solution.py:300
  53.8 0.1 pad_add_fusion.place
  53.9 1.4 %collective-permute-done.5.last.p4 = bf16[8,352,128]{2,1,0:T(8,128)(2,1)} collective-permute-done((bf16[8,352,128]{2,1,0:T(8,128)(2,1)}, bf16[8,352,128]{2,1,0:T(8,128)(2,1)}, u32[]{:S(2)}, u32[]{:S(2)}) %collective-permute-start.5) | collective-permute-done | bytes 720928 | tf_op jit(solution)/shard_map/ppermute | solution.py:300
  55.3 0.6 arrival.1.token
  55.9 0.0 copy-done
  55.9 0.0 copy-done.1
  55.9 0.0 copy-done.2
  55.9 0.0 copy-done.3
  55.9 2.7 %all-to-all-done.chunk = bf16[32,72,512]{2,1,0:T(8,128)(2,1)S(1)} async-done(((bf16[32,72,512]{2,1,0:T(8,128)(2,1)}), bf16[32,72,512]{2,1,0:T(8,128)(2,1)S(1)}, u32[]{:S(2)}, u32[]{:S(2)}) %all-to-all-start) | async-done | bytes 2359328 | tf_op jit(solution)/shard_map/all_to_all | solution.py:344
  58.6 9.4 %attention.1 = (bf16[8,5,16,128]{3,2,1,0:T(8,128)(2,1)S(1)}, bf16[8,5,16,128]{3,2,1,0:T(8,128)(2,1)S(1)}) custom-call(s32[3]{0:T(128)S(1)} %pad_add_fusion.place, f32[8,128]{1,0:T(8,128)} %arrival.1.token, bf16[2,352,128]{2,1,0:T(8,128)(2,1)} %copy-done, bf16[2,352,128]{2,1,0:T(8,128)(2,1)} %copy-done.3, bf16[2,352,128]{2,1,0:T(8,128)(2,1)} %copy-done.2, ...), custom_call_target="tpu_custom_call" | custom-call | tf_op jit(solution)/shard_map/attention/pallas_call | solution.py:225
  68.0 7.6 %collective-permute-start.6 = (bf16[8,5,16,128]{3,2,1,0:T(8,128)(2,1)S(1)}, bf16[8,5,16,128]{3,2,1,0:T(8,128)(2,1)S(1)}, u32[]{:S(2)}, u32[]{:S(2)}) collective-permute-start(bf16[8,5,16,128]{3,2,1,0:T(8,128)(2,1)S(1)} %get-tuple-element.14), channel_id=1, source_target_pairs={{0,32},{32,0},{64,96},{96,64},{128,160},{160,128},{192,224},{224,1... | collective-permute-start | bytes 491528 | tf_op jit(solution)/shard_map/ppermute | solution.py:300
  75.6 1.0 %collective-permute-done.6.b = bf16[8,5,16,128]{3,2,1,0:T(8,128)(2,1)S(1)} collective-permute-done((bf16[8,5,16,128]{3,2,1,0:T(8,128)(2,1)S(1)}, bf16[8,5,16,128]{3,2,1,0:T(8,128)(2,1)S(1)}, u32[]{:S(2)}, u32[]{:S(2)}) %collective-permute-start.6) | collective-permute-done | bytes 163872 | tf_op jit(solution)/shard_map/ppermute | solution.py:300
  76.6 0.5 pair.1
  77.1 15.3 %all_to_all.10.x = bf16[8,5,16,128]{3,2,1,0:T(8,128)(2,1)S(1)} all-to-all(bf16[8,5,16,128]{3,2,1,0:T(8,128)(2,1)S(1)} %pair.1), channel_id=1, replica_groups=mesh['zq'=2,'zr'=4,'co'=2,'x'=4,'y'=4,'zh'=2] {'zq','zr'}, dimensions={0} | all-to-all | bytes 327680 | tf_op jit(solution)/shard_map/all_to_all | solution.py:351
  92.3 0.9 final.1
  (1 shorter events, 0.0 us)
Async XLA Ops:
  1.0 21.1 %collective-permute-start = (bf16[1,72,512]{2,1,0:T(8,128)(2,1)S(1)}, bf16[1,72,512]{2,1,0:T(8,128)(2,1)S(1)}, u32[]{:S(2)}, u32[]{:S(2)}) collective-permute-start(bf16[1,72,512]{2,1,0:T(8,128)(2,1)S(1)} %get-tuple-element.10.block), channel_id=1, source_target_pairs={{0,449},{1,448},{64,385},{65,384},{128,321},{129,320},{192,257},{1... | collective-permute-start | bytes 221192 | tf_op jit(solution)/shard_map/ppermute | solution.py:340
  13.0 17.2 %collective-permute-start.1 = (bf16[1,352,128]{2,1,0:T(8,128)(2,1)S(1)}, bf16[1,352,128]{2,1,0:T(8,128)(2,1)S(1)}, u32[]{:S(2)}, u32[]{:S(2)}) collective-permute-start(bf16[1,352,128]{2,1,0:T(8,128)(2,1)S(1)} %get-tuple-element.11), channel_id=1, source_target_pairs={{0,256},{32,288},{64,320},{96,352},{128,384},{160,416},{192,448},{... | collective-permute-start | bytes 270344 | tf_op jit(solution)/shard_map/ppermute | solution.py:300
  23.4 35.2 %all-to-all-start = ((bf16[32,72,512]{2,1,0:T(8,128)(2,1)}), bf16[32,72,512]{2,1,0:T(8,128)(2,1)S(1)}, u32[]{:S(2)}, u32[]{:S(2)}) async-start(bf16[32,72,512]{2,1,0:T(8,128)(2,1)} %bitcast.9), calls=%async_computation | async-start | bytes 4718592 | tf_op jit(solution)/shard_map/all_to_all | solution.py:344
  30.2 25.7 %copy-start = (bf16[2,352,128]{2,1,0:T(8,128)(2,1)}, bf16[2,352,128]{2,1,0:T(8,128)(2,1)S(1)}, u32[]{:S(2)}) copy-start(bf16[2,352,128]{2,1,0:T(8,128)(2,1)S(1)} %pad_maximum_fusion.1.p0) | copy-start | bytes 540676
  30.2 9.3 %collective-permute-start.4 = (bf16[2,352,128]{2,1,0:T(8,128)(2,1)S(1)}, bf16[2,352,128]{2,1,0:T(8,128)(2,1)S(1)}, u32[]{:S(2)}, u32[]{:S(2)}) collective-permute-start(bf16[2,352,128]{2,1,0:T(8,128)(2,1)S(1)} %pad_maximum_fusion.1.p0), channel_id=1, source_target_pairs={{0,192},{32,224},{64,128},{96,160},{128,64},{160,96},{192,0},{224,... | collective-permute-start | bytes 540680 | tf_op jit(solution)/shard_map/ppermute | solution.py:300
  32.1 16.2 %collective-permute-start.3 = (bf16[2,352,128]{2,1,0:T(8,128)(2,1)S(1)}, bf16[2,352,128]{2,1,0:T(8,128)(2,1)S(1)}, u32[]{:S(2)}, u32[]{:S(2)}) collective-permute-start(bf16[2,352,128]{2,1,0:T(8,128)(2,1)S(1)} %pad_maximum_fusion.1.p0), channel_id=1, source_target_pairs={{0,128},{32,160},{64,192},{96,224},{128,0},{160,32},{192,64},{224,... | collective-permute-start | bytes 540680 | tf_op jit(solution)/shard_map/ppermute | solution.py:300
  35.0 13.3 %collective-permute-start.2 = (bf16[2,352,128]{2,1,0:T(8,128)(2,1)S(1)}, bf16[2,352,128]{2,1,0:T(8,128)(2,1)S(1)}, u32[]{:S(2)}, u32[]{:S(2)}) collective-permute-start(bf16[2,352,128]{2,1,0:T(8,128)(2,1)S(1)} %pad_maximum_fusion.1.p0), channel_id=1, source_target_pairs={{0,64},{32,96},{64,0},{96,32},{128,192},{160,224},{192,128},{224,1... | collective-permute-start | bytes 540680 | tf_op jit(solution)/shard_map/ppermute | solution.py:300
  39.5 16.4 %copy-start.1 = (bf16[2,352,128]{2,1,0:T(8,128)(2,1)}, bf16[2,352,128]{2,1,0:T(8,128)(2,1)S(1)}, u32[]{:S(2)}) copy-start(bf16[2,352,128]{2,1,0:T(8,128)(2,1)S(1)} %collective-permute-done.4.p3) | copy-start | bytes 540676
  48.3 7.6 %copy-start.2 = (bf16[2,352,128]{2,1,0:T(8,128)(2,1)}, bf16[2,352,128]{2,1,0:T(8,128)(2,1)S(1)}, u32[]{:S(2)}) copy-start(bf16[2,352,128]{2,1,0:T(8,128)(2,1)S(1)} %collective-permute-done.3.p2) | copy-start | bytes 540676
  48.3 7.6 %copy-start.3 = (bf16[2,352,128]{2,1,0:T(8,128)(2,1)}, bf16[2,352,128]{2,1,0:T(8,128)(2,1)S(1)}, u32[]{:S(2)}) copy-start(bf16[2,352,128]{2,1,0:T(8,128)(2,1)S(1)} %collective-permute-done.2.p1) | copy-start | bytes 540676
  49.3 6.0 %collective-permute-start.5 = (bf16[8,352,128]{2,1,0:T(8,128)(2,1)}, bf16[8,352,128]{2,1,0:T(8,128)(2,1)}, u32[]{:S(2)}, u32[]{:S(2)}) collective-permute-start(bf16[8,352,128]{2,1,0:T(8,128)(2,1)} %pad_maximum_fusion), channel_id=1, source_target_pairs={{0,32},{32,0},{64,96},{96,64},{128,160},{160,128},{192,224},{224,1... | collective-permute-start | bytes 2162696 | tf_op jit(solution)/shard_map/ppermute | solution.py:300
  68.0 8.6 %collective-permute-start.6 = (bf16[8,5,16,128]{3,2,1,0:T(8,128)(2,1)S(1)}, bf16[8,5,16,128]{3,2,1,0:T(8,128)(2,1)S(1)}, u32[]{:S(2)}, u32[]{:S(2)}) collective-permute-start(bf16[8,5,16,128]{3,2,1,0:T(8,128)(2,1)S(1)} %get-tuple-element.14), channel_id=1, source_target_pairs={{0,32},{32,0},{64,96},{96,64},{128,160},{160,128},{192,224},{224,1... | collective-permute-start | bytes 491528 | tf_op jit(solution)/shard_map/ppermute | solution.py:300

commit v10 on v8

--- a/solution.py
+++ b/solution.py
@@ -36,7 +36,7 @@
         kernel,
         out_shape=shape,
         in_specs=[vmem()] * n_in,
-        out_specs=vmem(),
+        out_specs=jax.tree.map(lambda _: vmem(), shape),
         compiler_params=pltpu.CompilerParams(vmem_limit_bytes=8 * MIB),
         name=name,
     )
@@ -152,7 +152,7 @@
     return t[..., k : k + 1] + t[..., k + 1 : k + 2] + t[..., k + 2 : k + 3]
 
 
-def attention_kernel(place, token, p0, p1, p2, p3, p4, chunk, keep, send, keys, turns, parts, *scratch):
+def attention_kernel(place, token, p0, p1, p2, p3, p4, chunk, out, keys, turns, parts, *scratch):
     me, zh, prior = place[0], place[1], place[2]
     zl, co = lax.shift_right_logical(me, 1), lax.bitwise_and(me, 1)
     tiles, pieces, panel, lats, rots, values, sems = scratch
@@ -215,18 +215,19 @@
     tile = pack_lse(lses, (ROWS, 128))
     for g in range(16):
         parts[g, HEADS] = tile[TOK * g : TOK * (g + 1)]
+    mine = lax.bitwise_and(me, 8)
     for g in range(8):
-        keep[g] = parts[g * 2 + co]
-        send[g] = parts[g * 2 + 1 - co]
+        for j in range(2):
+            out[g, j] = parts[lax.bitwise_xor(mine, 8 * j) + g]
 
 
 def attend(place, slots, *pieces):
     hbm = pl.BlockSpec(memory_space=pltpu.HBM)
     return pl.pallas_call(
         attention_kernel,
-        out_shape=(shaped((8, HEADS + 1, TOK, 128)),) * 2,
+        out_shape=shaped((8, 2, HEADS + 1, TOK, 128)),
         in_specs=[pl.BlockSpec(memory_space=pltpu.SMEM)] + [hbm] * 6 + [vmem()],
-        out_specs=(vmem(), vmem()),
+        out_specs=vmem(),
         scratch_shapes=[
             pltpu.VMEM((2, SLOTS, LATENT), bf16),
             pltpu.VMEM((SLOTS, 2 * ROT), bf16),
@@ -278,20 +279,17 @@
     return values, lses
 
 
-def pair_kernel(a, b, out):
-    rows = 8 * TOK
-    blocks = [
-        jnp.concatenate([r[:, h].reshape(1, rows, 128) for r in (a, b)], axis=0)
-        for h in range(HEADS + 1)
-    ]
-    values, lses = merge_heads(blocks)
-    for h in range(HEADS):
-        out[:, h] = values[h].astype(bf16).reshape(8, TOK, 128)
-    out[:, HEADS] = pack_lse(lses, (rows, 128)).reshape(8, TOK, 128)
-
-
-def final_kernel(x, out):
-    values, _ = merge_heads([x[:, h] for h in range(HEADS + 1)])
+def middle_kernel(x, mine, other):
+    for j, out in enumerate((mine, other)):
+        values, lses = merge_heads([x[:, j, h] for h in range(HEADS + 1)])
+        for h in range(HEADS):
+            out[h] = values[h].astype(bf16)
+        out[HEADS] = pack_lse(lses, (TOK, 128))
+
+
+def final_kernel(a, b, out):
+    blocks = [jnp.concatenate([r[h : h + 1] for r in (a, b)], axis=0) for h in range(HEADS + 1)]
+    values, _ = merge_heads(blocks)
     for h in range(HEADS):
         out[:, h * VALUE : (h + 1) * VALUE] = values[h].astype(bf16)
 
@@ -325,10 +323,10 @@
     pack8 = jnp.concatenate([pack2] + fans, axis=0)
 
     last = swap(pack8, 1)
-    keep, send = attend(place, slots, arrival(last), pack2, *fans, last)
-    merged = call(pair_kernel, shaped((8, HEADS + 1, TOK, 128)), 2, "pair")(keep, swap(send, 1))
-    spread = lax.all_to_all(merged, ZL, 0, 0, tiled=True)
-    return call(final_kernel, shaped((TOK, HEADS * VALUE)), 1, "final")(spread)
+    part = attend(place, slots, arrival(last), pack2, *fans, last)
+    part = lax.all_to_all(part, ("zr", "co"), 0, 0, tiled=True)
+    mine, other = call(middle_kernel, (shaped((HEADS + 1, TOK, 128)),) * 2, 1, "middle")(part)
+    return call(final_kernel, shaped((TOK, HEADS * VALUE)), 2, "final")(mine, swap(other, 8))
 
 
 def solution(mesh):

time: 94.5 us -> 96 us (1.016); the launches traced: 92.9 us -> 95.5 us
  blocking collectives: 15.8 us -> 18.4 us
  starting transfers between devices: 47.2 us -> 44.8 us
  local copies, waits for them, and re-layouts: 1.71 us -> 3.89 us
    all_to_all x1, blocking collectives: 15.8 us -> 18.4 us  [per_device(): part = lax.all_to_all(part, ('zr', 'co'), 0, 0, tiled=True)]
    ppermute x6, starting transfers between devices: 28.5 us -> 26.1 us  [swap(): return lax.ppermute(x, CTX, [(i, i ^ d) for i in range(16)])]
    ppermute x6, waiting for transfers between devices: 11.2 us -> 13.5 us  [swap(): return lax.ppermute(x, CTX, [(i, i ^ d) for i in range(16)])]
    unnamed x8 -> x10, local copies, waits for them, and re-layouts: 0.02 us -> 2.2 us
    all_to_all x1, waiting for transfers between devices: 2.68 us -> 0.66 us  [gather(): return lax.all_to_all(copies, axes, 0, 0, tiled=True)]
where the time goes in v10:
time: 96 us; the launch traced here: 95.5 us
  starting transfers between devices  44.8 us (47%)
  blocking collectives  18.4 us (19%)
  waiting for transfers between devices  14.2 us (15%)
  Pallas kernels  12.3 us (13%)
  local copies, waits for them, and re-layouts  3.89 us (4%)
  other arithmetic  1.07 us (1%)
    ppermute x6, starting transfers between devices, swap(): return lax.ppermute(x, CTX, [(i, i ^ d) for i in range(16)])  26.1 us
    all_to_all x1, blocking collectives, per_device(): part = lax.all_to_all(part, ('zr', 'co'), 0, 0, tiled=True)  18.4 us
    ppermute x6, waiting for transfers between devices, swap(): return lax.ppermute(x, CTX, [(i, i ^ d) for i in range(16)])  13.5 us
    ppermute x1, starting transfers between devices, per_device(): lax.ppermute(shard, ('zq', 'zr', 'zh'), [(i, 15 - i) for i in range(16)])  12 us
    pallas_call x1, Pallas kernels, attend(): pl.pallas_call(attention_kernel, out_shape=shaped((8, 2, HEADS + 1, TOK,...  9.36 us
    all_to_all x1, starting transfers between devices, gather(): return lax.all_to_all(copies, axes, 0, 0, tiled=True)  6.75 us
    unnamed x10, local copies, waits for them, and re-layouts  2.2 us
  transfers between devices with their start and end apart: 8, of which 4 were waited for; matrix products, arithmetic and copies ran while one was open for 3% of the time, Pallas kernels for 1%

profile of v10, /device:TPU:1, one launch (start us, length us, event | category | flops | bytes accessed | tf_op | source)
XLA Modules:
  0.0 95.5 jit_solution(14826736787548873179)
XLA Ops:
  0.0 1.0 %prepare.1 = (bf16[1,72,512]{2,1,0:T(8,128)(2,1)S(1)}, bf16[1,352,128]{2,1,0:T(8,128)(2,1)S(1)}) custom-call(bf16[16,768]{1,0:T(8,128)(2,1)} %queries_hbm.1, bf16[64,576]{1,0:T(8,128)(2,1)} %cache_hbm.1, bf16[128,128]{1,0:T(8,128)(2,1)} %bitcast.10, bf16[128,128]{1,0:T(8,128)(2,1)} %bitcast.11), custom_call_target="tpu_custom_call" | custom-call | tf_op jit(solution)/shard_map/prepare/pallas_call | solution.py:77
  1.0 12.0 %collective-permute-start = (bf16[1,72,512]{2,1,0:T(8,128)(2,1)S(1)}, bf16[1,72,512]{2,1,0:T(8,128)(2,1)S(1)}, u32[]{:S(2)}, u32[]{:S(2)}) collective-permute-start(bf16[1,72,512]{2,1,0:T(8,128)(2,1)S(1)} %get-tuple-element.10), channel_id=1, source_target_pairs={{0,449},{1,448},{64,385},{65,384},{128,321},{129,320},{192,257},{1... | collective-permute-start | bytes 221192 | tf_op jit(solution)/shard_map/ppermute | solution.py:317
  13.0 7.9 %collective-permute-start.1 = (bf16[1,352,128]{2,1,0:T(8,128)(2,1)S(1)}, bf16[1,352,128]{2,1,0:T(8,128)(2,1)S(1)}, u32[]{:S(2)}, u32[]{:S(2)}) collective-permute-start(bf16[1,352,128]{2,1,0:T(8,128)(2,1)S(1)} %get-tuple-element.11), channel_id=1, source_target_pairs={{0,256},{32,288},{64,320},{96,352},{128,384},{160,416},{192,448},{... | collective-permute-start | bytes 270344 | tf_op jit(solution)/shard_map/ppermute | solution.py:298
  20.9 0.0 collective-permute-done
  20.9 1.7 %broadcast_in_dim.2 = bf16[16,2,72,512]{3,2,1,0:T(8,128)(2,1)} broadcast(bf16[2,72,512]{2,1,0:T(8,128)(2,1)S(1)} %pad_maximum_fusion.2), dimensions={1,2,3} | broadcast | bytes 2506752 | tf_op jit(solution)/shard_map/broadcast_in_dim | solution.py:302
  22.6 6.8 %all-to-all-start = ((bf16[32,72,512]{2,1,0:T(8,128)(2,1)}), bf16[32,72,512]{2,1,0:T(8,128)(2,1)S(1)}, u32[]{:S(2)}, u32[]{:S(2)}) async-start(bf16[32,72,512]{2,1,0:T(8,128)(2,1)} %bitcast.9), calls=%async_computation | async-start | bytes 4718592 | tf_op jit(solution)/shard_map/all_to_all | solution.py:303
  29.3 0.0 collective-permute-done.1
  29.4 0.0 copy-start
  29.4 1.9 %collective-permute-start.4 = (bf16[2,352,128]{2,1,0:T(8,128)(2,1)S(1)}, bf16[2,352,128]{2,1,0:T(8,128)(2,1)S(1)}, u32[]{:S(2)}, u32[]{:S(2)}) collective-permute-start(bf16[2,352,128]{2,1,0:T(8,128)(2,1)S(1)} %pad_maximum_fusion.1.p0), channel_id=1, source_target_pairs={{0,192},{32,224},{64,128},{96,160},{128,64},{160,96},{192,0},{224,... | collective-permute-start | bytes 540680 | tf_op jit(solution)/shard_map/ppermute | solution.py:298
  31.3 2.9 %collective-permute-start.3 = (bf16[2,352,128]{2,1,0:T(8,128)(2,1)S(1)}, bf16[2,352,128]{2,1,0:T(8,128)(2,1)S(1)}, u32[]{:S(2)}, u32[]{:S(2)}) collective-permute-start(bf16[2,352,128]{2,1,0:T(8,128)(2,1)S(1)} %pad_maximum_fusion.1.p0), channel_id=1, source_target_pairs={{0,128},{32,160},{64,192},{96,224},{128,0},{160,32},{192,64},{224,... | collective-permute-start | bytes 540680 | tf_op jit(solution)/shard_map/ppermute | solution.py:298
  34.2 4.4 %collective-permute-start.2 = (bf16[2,352,128]{2,1,0:T(8,128)(2,1)S(1)}, bf16[2,352,128]{2,1,0:T(8,128)(2,1)S(1)}, u32[]{:S(2)}, u32[]{:S(2)}) collective-permute-start(bf16[2,352,128]{2,1,0:T(8,128)(2,1)S(1)} %pad_maximum_fusion.1.p0), channel_id=1, source_target_pairs={{0,64},{32,96},{64,0},{96,32},{128,192},{160,224},{192,128},{224,1... | collective-permute-start | bytes 540680 | tf_op jit(solution)/shard_map/ppermute | solution.py:298
  38.7 0.0 collective-permute-done.4.p3
  38.7 0.0 copy-start.2
  38.7 8.8 %collective-permute-done.3.p2 = bf16[2,352,128]{2,1,0:T(8,128)(2,1)S(1)} collective-permute-done((bf16[2,352,128]{2,1,0:T(8,128)(2,1)S(1)}, bf16[2,352,128]{2,1,0:T(8,128)(2,1)S(1)}, u32[]{:S(2)}, u32[]{:S(2)}) %collective-permute-start.3) | collective-permute-done | bytes 180256 | tf_op jit(solution)/shard_map/ppermute | solution.py:298
  47.5 0.0 copy-start.3
  47.5 0.0 collective-permute-done.2.p1
  47.5 0.7 copy-done.3
  48.2 0.0 copy-start.4
  48.2 0.7 copy-done.4
  48.9 1.0 %pad_maximum_fusion = bf16[8,352,128]{2,1,0:T(8,128)(2,1)} fusion(bf16[2,352,128]{2,1,0:T(8,128)(2,1)S(1)} %collective-permute-done.4.p3, bf16[2,352,128]{2,1,0:T(8,128)(2,1)S(1)} %collective-permute-done.3.p2, bf16[2,352,128]{2,1,0:T(8,128)(2,1)S(1)} %collective-permute-done.2.p1, bf16[2,352,128]{2,1,0:T(8,128)(2,1)S(1)} %pad_maximum_fusion.1.p0), kind=kLoop, calls=%fused_computation | loop fusion | flops 1081344 | bytes 1441792 | tf_op jit(solution)/shard_map/concatenate | solution.py:323
  49.8 3.8 %collective-permute-start.5 = (bf16[8,352,128]{2,1,0:T(8,128)(2,1)}, bf16[8,352,128]{2,1,0:T(8,128)(2,1)S(1)}, u32[]{:S(2)}, u32[]{:S(2)}) collective-permute-start(bf16[8,352,128]{2,1,0:T(8,128)(2,1)} %pad_maximum_fusion), channel_id=1, source_target_pairs={{0,32},{32,0},{64,96},{96,64},{128,160},{160,128},{192,224},{224,1... | collective-permute-start | bytes 2162696 | tf_op jit(solution)/shard_map/ppermute | solution.py:298
  54.3 0.1 pad_add_fusion.place
  54.4 1.3 %collective-permute-done.5.last.p4 = bf16[8,352,128]{2,1,0:T(8,128)(2,1)S(1)} collective-permute-done((bf16[8,352,128]{2,1,0:T(8,128)(2,1)}, bf16[8,352,128]{2,1,0:T(8,128)(2,1)S(1)}, u32[]{:S(2)}, u32[]{:S(2)}) %collective-permute-start.5) | collective-permute-done | bytes 720928 | tf_op jit(solution)/shard_map/ppermute | solution.py:298
  55.6 0.0 copy-start.1
  55.6 0.9 copy-done.1
  56.5 0.6 arrival.1.token
  57.1 0.0 copy-done
  57.1 0.0 copy-done.2
  57.1 0.7 all-to-all-done.chunk
  57.8 9.4 %attention.1 = bf16[8,2,5,16,128]{4,3,2,1,0:T(8,128)(2,1)S(1)} custom-call(s32[3]{0:T(128)S(1)} %pad_add_fusion.place, f32[8,128]{1,0:T(8,128)} %arrival.1.token, bf16[2,352,128]{2,1,0:T(8,128)(2,1)} %copy-done, bf16[2,352,128]{2,1,0:T(8,128)(2,1)} %copy-done.4, bf16[2,352,128]{2,1,0:T(8,128)(2,1)} %copy-done.3, bf16[2,352,128]{2,1,0:T(8,128)(2,1)} %copy-done.2, ...), custom_call_target="tpu_custom_call" | custom-call | tf_op jit(solution)/shard_map/attention/pallas_call | solution.py:226
  67.2 18.4 %all_to_all.10.x = bf16[8,2,5,16,128]{4,3,2,1,0:T(8,128)(2,1)S(1)} all-to-all(bf16[8,2,5,16,128]{4,3,2,1,0:T(8,128)(2,1)S(1)} %attention.1), channel_id=1, replica_groups=mesh['zq'=2,'zr'=4,'co'=2,'x'=4,'y'=4,'zh'=2] {'zr','co'}, dimensions={0} | all-to-all | bytes 655360 | tf_op jit(solution)/shard_map/all_to_all | solution.py:327
  85.6 0.5 middle.1
  86.1 5.2 %collective-permute-start.6 = (bf16[5,16,128]{2,1,0:T(8,128)(2,1)S(1)}, bf16[5,16,128]{2,1,0:T(8,128)(2,1)S(1)}, u32[]{:S(2)}, u32[]{:S(2)}) collective-permute-start(bf16[5,16,128]{2,1,0:T(8,128)(2,1)S(1)} %get-tuple-element.14), channel_id=1, source_target_pairs={{0,256},{32,288},{64,320},{96,352},{128,384},{160,416},{192,448},{... | collective-permute-start | bytes 61448 | tf_op jit(solution)/shard_map/ppermute | solution.py:298
  91.3 3.4 %collective-permute-done.6.b = bf16[5,16,128]{2,1,0:T(8,128)(2,1)S(1)} collective-permute-done((bf16[5,16,128]{2,1,0:T(8,128)(2,1)S(1)}, bf16[5,16,128]{2,1,0:T(8,128)(2,1)S(1)}, u32[]{:S(2)}, u32[]{:S(2)}) %collective-permute-start.6) | collective-permute-done | bytes 20512 | tf_op jit(solution)/shard_map/ppermute | solution.py:298
  94.7 0.8 final.1
  (2 shorter events, 0.0 us)
Async XLA Ops:
  1.0 19.8 %collective-permute-start = (bf16[1,72,512]{2,1,0:T(8,128)(2,1)S(1)}, bf16[1,72,512]{2,1,0:T(8,128)(2,1)S(1)}, u32[]{:S(2)}, u32[]{:S(2)}) collective-permute-start(bf16[1,72,512]{2,1,0:T(8,128)(2,1)S(1)} %get-tuple-element.10), channel_id=1, source_target_pairs={{0,449},{1,448},{64,385},{65,384},{128,321},{129,320},{192,257},{1... | collective-permute-start | bytes 221192 | tf_op jit(solution)/shard_map/ppermute | solution.py:317
  13.0 16.4 %collective-permute-start.1 = (bf16[1,352,128]{2,1,0:T(8,128)(2,1)S(1)}, bf16[1,352,128]{2,1,0:T(8,128)(2,1)S(1)}, u32[]{:S(2)}, u32[]{:S(2)}) collective-permute-start(bf16[1,352,128]{2,1,0:T(8,128)(2,1)S(1)} %get-tuple-element.11), channel_id=1, source_target_pairs={{0,256},{32,288},{64,320},{96,352},{128,384},{160,416},{192,448},{... | collective-permute-start | bytes 270344 | tf_op jit(solution)/shard_map/ppermute | solution.py:298
  22.6 35.2 %all-to-all-start = ((bf16[32,72,512]{2,1,0:T(8,128)(2,1)}), bf16[32,72,512]{2,1,0:T(8,128)(2,1)S(1)}, u32[]{:S(2)}, u32[]{:S(2)}) async-start(bf16[32,72,512]{2,1,0:T(8,128)(2,1)} %bitcast.9), calls=%async_computation | async-start | bytes 4718592 | tf_op jit(solution)/shard_map/all_to_all | solution.py:303
  29.4 27.7 %copy-start = (bf16[2,352,128]{2,1,0:T(8,128)(2,1)}, bf16[2,352,128]{2,1,0:T(8,128)(2,1)S(1)}, u32[]{:S(2)}) copy-start(bf16[2,352,128]{2,1,0:T(8,128)(2,1)S(1)} %pad_maximum_fusion.1.p0) | copy-start | bytes 540676
  29.4 9.3 %collective-permute-start.4 = (bf16[2,352,128]{2,1,0:T(8,128)(2,1)S(1)}, bf16[2,352,128]{2,1,0:T(8,128)(2,1)S(1)}, u32[]{:S(2)}, u32[]{:S(2)}) collective-permute-start(bf16[2,352,128]{2,1,0:T(8,128)(2,1)S(1)} %pad_maximum_fusion.1.p0), channel_id=1, source_target_pairs={{0,192},{32,224},{64,128},{96,160},{128,64},{160,96},{192,0},{224,... | collective-permute-start | bytes 540680 | tf_op jit(solution)/shard_map/ppermute | solution.py:298
  31.3 16.2 %collective-permute-start.3 = (bf16[2,352,128]{2,1,0:T(8,128)(2,1)S(1)}, bf16[2,352,128]{2,1,0:T(8,128)(2,1)S(1)}, u32[]{:S(2)}, u32[]{:S(2)}) collective-permute-start(bf16[2,352,128]{2,1,0:T(8,128)(2,1)S(1)} %pad_maximum_fusion.1.p0), channel_id=1, source_target_pairs={{0,128},{32,160},{64,192},{96,224},{128,0},{160,32},{192,64},{224,... | collective-permute-start | bytes 540680 | tf_op jit(solution)/shard_map/ppermute | solution.py:298
  34.2 13.3 %collective-permute-start.2 = (bf16[2,352,128]{2,1,0:T(8,128)(2,1)S(1)}, bf16[2,352,128]{2,1,0:T(8,128)(2,1)S(1)}, u32[]{:S(2)}, u32[]{:S(2)}) collective-permute-start(bf16[2,352,128]{2,1,0:T(8,128)(2,1)S(1)} %pad_maximum_fusion.1.p0), channel_id=1, source_target_pairs={{0,64},{32,96},{64,0},{96,32},{128,192},{160,224},{192,128},{224,1... | collective-permute-start | bytes 540680 | tf_op jit(solution)/shard_map/ppermute | solution.py:298
  38.7 18.4 %copy-start.2 = (bf16[2,352,128]{2,1,0:T(8,128)(2,1)}, bf16[2,352,128]{2,1,0:T(8,128)(2,1)S(1)}, u32[]{:S(2)}) copy-start(bf16[2,352,128]{2,1,0:T(8,128)(2,1)S(1)} %collective-permute-done.4.p3) | copy-start | bytes 540676
  47.5 0.7 copy-start.3
  48.2 0.7 copy-start.4
  49.8 5.8 %collective-permute-start.5 = (bf16[8,352,128]{2,1,0:T(8,128)(2,1)}, bf16[8,352,128]{2,1,0:T(8,128)(2,1)S(1)}, u32[]{:S(2)}, u32[]{:S(2)}) collective-permute-start(bf16[8,352,128]{2,1,0:T(8,128)(2,1)} %pad_maximum_fusion), channel_id=1, source_target_pairs={{0,32},{32,0},{64,96},{96,64},{128,160},{160,128},{192,224},{224,1... | collective-permute-start | bytes 2162696 | tf_op jit(solution)/shard_map/ppermute | solution.py:298
  55.6 0.9 copy-start.1
  86.1 8.6 %collective-permute-start.6 = (bf16[5,16,128]{2,1,0:T(8,128)(2,1)S(1)}, bf16[5,16,128]{2,1,0:T(8,128)(2,1)S(1)}, u32[]{:S(2)}, u32[]{:S(2)}) collective-permute-start(bf16[5,16,128]{2,1,0:T(8,128)(2,1)S(1)} %get-tuple-element.14), channel_id=1, source_target_pairs={{0,256},{32,288},{64,320},{96,352},{128,384},{160,416},{192,448},{... | collective-permute-start | bytes 61448 | tf_op jit(solution)/shard_map/ppermute | solution.py:298

commit v11 on v8

--- a/solution.py
+++ b/solution.py
@@ -198,12 +198,13 @@
         for s in scores[1:]:
             peak = jnp.maximum(peak, s)
         peak = peak.max(axis=1, keepdims=True)
-        total = jnp.zeros((4 * ROWS, 1), f32)
+        weight = None
         acc = jnp.zeros((4 * ROWS, LATENT), f32)
         for s, (half, cut) in zip(scores, blocks):
             p = jnp.exp2(s - peak)
-            total = total + p.sum(axis=1, keepdims=True)
+            weight = p if weight is None else weight + p
             acc = acc + jnp.dot(p.astype(bf16), keys[half, cut : cut + 512], preferred_element_type=f32)
+        total = weight.sum(axis=1, keepdims=True)
         latent = (acc / total).astype(bf16)
         lse = peak + jnp.log2(total)
         for i, h in enumerate(group):

time: 94.5 us -> 94.9 us (level)
  no operation moved by 1% of the time
where the time goes in v11:
time: 94.9 us; the launch traced here: 93.3 us
  starting transfers between devices  47.2 us (50%)
  blocking collectives  15.8 us (17%)
  waiting for transfers between devices  13.9 us (15%)
  Pallas kernels  12.7 us (13%)
  local copies, waits for them, and re-layouts  1.71 us (2%)
  other arithmetic  1.09 us (1%)
    ppermute x6, starting transfers between devices, swap(): return lax.ppermute(x, CTX, [(i, i ^ d) for i in range(16)])  28.5 us
    all_to_all x1, blocking collectives, per_device(): spread = lax.all_to_all(merged, ZL, 0, 0, tiled=True)  15.8 us
    ppermute x1, starting transfers between devices, per_device(): lax.ppermute(shard, ('zq', 'zr', 'zh'), [(i, 15 - i) for i in range(16)])  12 us
    ppermute x6, waiting for transfers between devices, swap(): return lax.ppermute(x, CTX, [(i, i ^ d) for i in range(16)])  11.2 us
    pallas_call x1, Pallas kernels, attend(): pl.pallas_call(attention_kernel, out_shape=(shaped((8, HEADS + 1, TOK, 12...  9.79 us
    all_to_all x1, starting transfers between devices, gather(): return lax.all_to_all(copies, axes, 0, 0, tiled=True)  6.75 us
    all_to_all x1, waiting for transfers between devices, gather(): return lax.all_to_all(copies, axes, 0, 0, tiled=True)  2.68 us
  transfers between devices with their start and end apart: 8, of which 4 were waited for; matrix products, arithmetic and copies ran while one was open for 3% of the time, Pallas kernels for 1%

profile of v11, /device:TPU:1, one launch (start us, length us, event | category | flops | bytes accessed | tf_op | source)
XLA Modules:
  0.0 93.3 jit_solution(16603324466172500875)
XLA Ops:
  0.0 1.0 %prepare.1 = (bf16[1,72,512]{2,1,0:T(8,128)(2,1)S(1)}, bf16[1,352,128]{2,1,0:T(8,128)(2,1)S(1)}) custom-call(bf16[16,768]{1,0:T(8,128)(2,1)} %queries_hbm.1, bf16[64,576]{1,0:T(8,128)(2,1)} %cache_hbm.1, bf16[128,128]{1,0:T(8,128)(2,1)} %bitcast.10, bf16[128,128]{1,0:T(8,128)(2,1)} %bitcast.11), custom_call_target="tpu_custom_call" | custom-call | tf_op jit(solution)/shard_map/prepare/pallas_call | solution.py:77
  1.0 12.0 %collective-permute-start = (bf16[1,72,512]{2,1,0:T(8,128)(2,1)S(1)}, bf16[1,72,512]{2,1,0:T(8,128)(2,1)S(1)}, u32[]{:S(2)}, u32[]{:S(2)}) collective-permute-start(bf16[1,72,512]{2,1,0:T(8,128)(2,1)S(1)} %get-tuple-element.10), channel_id=1, source_target_pairs={{0,449},{1,448},{64,385},{65,384},{128,321},{129,320},{192,257},{1... | collective-permute-start | bytes 221192 | tf_op jit(solution)/shard_map/ppermute | solution.py:320
  13.0 7.9 %collective-permute-start.1 = (bf16[1,352,128]{2,1,0:T(8,128)(2,1)S(1)}, bf16[1,352,128]{2,1,0:T(8,128)(2,1)S(1)}, u32[]{:S(2)}, u32[]{:S(2)}) collective-permute-start(bf16[1,352,128]{2,1,0:T(8,128)(2,1)S(1)} %get-tuple-element.11), channel_id=1, source_target_pairs={{0,256},{32,288},{64,320},{96,352},{128,384},{160,416},{192,448},{... | collective-permute-start | bytes 270344 | tf_op jit(solution)/shard_map/ppermute | solution.py:301
  20.9 0.0 collective-permute-done
  20.9 1.7 %broadcast_in_dim.2 = bf16[16,2,72,512]{3,2,1,0:T(8,128)(2,1)} broadcast(bf16[2,72,512]{2,1,0:T(8,128)(2,1)S(1)} %pad_maximum_fusion.2), dimensions={1,2,3} | broadcast | bytes 2506752 | tf_op jit(solution)/shard_map/broadcast_in_dim | solution.py:305
  22.6 6.8 %all-to-all-start = ((bf16[32,72,512]{2,1,0:T(8,128)(2,1)}), bf16[32,72,512]{2,1,0:T(8,128)(2,1)S(1)}, u32[]{:S(2)}, u32[]{:S(2)}) async-start(bf16[32,72,512]{2,1,0:T(8,128)(2,1)} %bitcast.9), calls=%async_computation | async-start | bytes 4718592 | tf_op jit(solution)/shard_map/all_to_all | solution.py:306
  29.4 0.0 collective-permute-done.1
  29.4 0.0 copy-start
  29.4 1.9 %collective-permute-start.4 = (bf16[2,352,128]{2,1,0:T(8,128)(2,1)S(1)}, bf16[2,352,128]{2,1,0:T(8,128)(2,1)S(1)}, u32[]{:S(2)}, u32[]{:S(2)}) collective-permute-start(bf16[2,352,128]{2,1,0:T(8,128)(2,1)S(1)} %pad_maximum_fusion.1.p0), channel_id=1, source_target_pairs={{0,192},{32,224},{64,128},{96,160},{128,64},{160,96},{192,0},{224,... | collective-permute-start | bytes 540680 | tf_op jit(solution)/shard_map/ppermute | solution.py:301
  31.3 2.9 %collective-permute-start.3 = (bf16[2,352,128]{2,1,0:T(8,128)(2,1)S(1)}, bf16[2,352,128]{2,1,0:T(8,128)(2,1)S(1)}, u32[]{:S(2)}, u32[]{:S(2)}) collective-permute-start(bf16[2,352,128]{2,1,0:T(8,128)(2,1)S(1)} %pad_maximum_fusion.1.p0), channel_id=1, source_target_pairs={{0,128},{32,160},{64,192},{96,224},{128,0},{160,32},{192,64},{224,... | collective-permute-start | bytes 540680 | tf_op jit(solution)/shard_map/ppermute | solution.py:301
  34.2 4.4 %collective-permute-start.2 = (bf16[2,352,128]{2,1,0:T(8,128)(2,1)S(1)}, bf16[2,352,128]{2,1,0:T(8,128)(2,1)S(1)}, u32[]{:S(2)}, u32[]{:S(2)}) collective-permute-start(bf16[2,352,128]{2,1,0:T(8,128)(2,1)S(1)} %pad_maximum_fusion.1.p0), channel_id=1, source_target_pairs={{0,64},{32,96},{64,0},{96,32},{128,192},{160,224},{192,128},{224,1... | collective-permute-start | bytes 540680 | tf_op jit(solution)/shard_map/ppermute | solution.py:301
  38.7 0.0 collective-permute-done.4.p3
  38.7 0.0 copy-start.1
  38.7 8.8 %collective-permute-done.3.p2 = bf16[2,352,128]{2,1,0:T(8,128)(2,1)S(1)} collective-permute-done((bf16[2,352,128]{2,1,0:T(8,128)(2,1)S(1)}, bf16[2,352,128]{2,1,0:T(8,128)(2,1)S(1)}, u32[]{:S(2)}, u32[]{:S(2)}) %collective-permute-start.3) | collective-permute-done | bytes 180256 | tf_op jit(solution)/shard_map/ppermute | solution.py:301
  47.5 0.0 copy-start.2
  47.5 0.0 collective-permute-done.2.p1
  47.5 0.0 copy-start.3
  47.5 1.0 %pad_maximum_fusion = bf16[8,352,128]{2,1,0:T(8,128)(2,1)} fusion(bf16[2,352,128]{2,1,0:T(8,128)(2,1)S(1)} %collective-permute-done.4.p3, bf16[2,352,128]{2,1,0:T(8,128)(2,1)S(1)} %collective-permute-done.3.p2, bf16[2,352,128]{2,1,0:T(8,128)(2,1)S(1)} %collective-permute-done.2.p1, bf16[2,352,128]{2,1,0:T(8,128)(2,1)S(1)} %pad_maximum_fusion.1.p0), kind=kLoop, calls=%fused_computation | loop fusion | flops 1081344 | bytes 1441792 | tf_op jit(solution)/shard_map/concatenate | solution.py:326
  48.5 3.8 %collective-permute-start.5 = (bf16[8,352,128]{2,1,0:T(8,128)(2,1)}, bf16[8,352,128]{2,1,0:T(8,128)(2,1)}, u32[]{:S(2)}, u32[]{:S(2)}) collective-permute-start(bf16[8,352,128]{2,1,0:T(8,128)(2,1)} %pad_maximum_fusion), channel_id=1, source_target_pairs={{0,32},{32,0},{64,96},{96,64},{128,160},{160,128},{192,224},{224,1... | collective-permute-start | bytes 2162696 | tf_op jit(solution)/shard_map/ppermute | solution.py:301
  53.0 0.1 pad_add_fusion.place
  53.1 1.4 %collective-permute-done.5.last.p4 = bf16[8,352,128]{2,1,0:T(8,128)(2,1)} collective-permute-done((bf16[8,352,128]{2,1,0:T(8,128)(2,1)}, bf16[8,352,128]{2,1,0:T(8,128)(2,1)}, u32[]{:S(2)}, u32[]{:S(2)}) %collective-permute-start.5) | collective-permute-done | bytes 720928 | tf_op jit(solution)/shard_map/ppermute | solution.py:301
  54.5 0.6 arrival.1.token
  55.1 0.0 copy-done
  55.1 0.0 copy-done.1
  55.1 0.0 copy-done.2
  55.1 0.0 copy-done.3
  55.1 2.7 %all-to-all-done.chunk = bf16[32,72,512]{2,1,0:T(8,128)(2,1)S(1)} async-done(((bf16[32,72,512]{2,1,0:T(8,128)(2,1)}), bf16[32,72,512]{2,1,0:T(8,128)(2,1)S(1)}, u32[]{:S(2)}, u32[]{:S(2)}) %all-to-all-start) | async-done | bytes 2359328 | tf_op jit(solution)/shard_map/all_to_all | solution.py:306
  57.8 9.8 %attention.1 = (bf16[8,5,16,128]{3,2,1,0:T(8,128)(2,1)S(1)}, bf16[8,5,16,128]{3,2,1,0:T(8,128)(2,1)S(1)}) custom-call(s32[3]{0:T(128)S(1)} %pad_add_fusion.place, f32[8,128]{1,0:T(8,128)} %arrival.1.token, bf16[2,352,128]{2,1,0:T(8,128)(2,1)} %copy-done, bf16[2,352,128]{2,1,0:T(8,128)(2,1)} %copy-done.3, bf16[2,352,128]{2,1,0:T(8,128)(2,1)} %copy-done.2, ...), custom_call_target="tpu_custom_call" | custom-call | tf_op jit(solution)/shard_map/attention/pallas_call | solution.py:226
  67.6 7.6 %collective-permute-start.6 = (bf16[8,5,16,128]{3,2,1,0:T(8,128)(2,1)S(1)}, bf16[8,5,16,128]{3,2,1,0:T(8,128)(2,1)S(1)}, u32[]{:S(2)}, u32[]{:S(2)}) collective-permute-start(bf16[8,5,16,128]{3,2,1,0:T(8,128)(2,1)S(1)} %get-tuple-element.14), channel_id=1, source_target_pairs={{0,32},{32,0},{64,96},{96,64},{128,160},{160,128},{192,224},{224,1... | collective-permute-start | bytes 491528 | tf_op jit(solution)/shard_map/ppermute | solution.py:301
  75.2 1.0 %collective-permute-done.6.b = bf16[8,5,16,128]{3,2,1,0:T(8,128)(2,1)S(1)} collective-permute-done((bf16[8,5,16,128]{3,2,1,0:T(8,128)(2,1)S(1)}, bf16[8,5,16,128]{3,2,1,0:T(8,128)(2,1)S(1)}, u32[]{:S(2)}, u32[]{:S(2)}) %collective-permute-start.6) | collective-permute-done | bytes 163872 | tf_op jit(solution)/shard_map/ppermute | solution.py:301
  76.2 0.5 pair.1
  76.6 15.8 %all_to_all.10.x = bf16[8,5,16,128]{3,2,1,0:T(8,128)(2,1)S(1)} all-to-all(bf16[8,5,16,128]{3,2,1,0:T(8,128)(2,1)S(1)} %pair.1), channel_id=1, replica_groups=mesh['zq'=2,'zr'=4,'co'=2,'x'=4,'y'=4,'zh'=2] {'zq','zr'}, dimensions={0} | all-to-all | bytes 327680 | tf_op jit(solution)/shard_map/all_to_all | solution.py:331
  92.5 0.9 final.1
  (2 shorter events, 0.0 us)
Async XLA Ops:
  1.0 19.8 %collective-permute-start = (bf16[1,72,512]{2,1,0:T(8,128)(2,1)S(1)}, bf16[1,72,512]{2,1,0:T(8,128)(2,1)S(1)}, u32[]{:S(2)}, u32[]{:S(2)}) collective-permute-start(bf16[1,72,512]{2,1,0:T(8,128)(2,1)S(1)} %get-tuple-element.10), channel_id=1, source_target_pairs={{0,449},{1,448},{64,385},{65,384},{128,321},{129,320},{192,257},{1... | collective-permute-start | bytes 221192 | tf_op jit(solution)/shard_map/ppermute | solution.py:320
  13.0 16.4 %collective-permute-start.1 = (bf16[1,352,128]{2,1,0:T(8,128)(2,1)S(1)}, bf16[1,352,128]{2,1,0:T(8,128)(2,1)S(1)}, u32[]{:S(2)}, u32[]{:S(2)}) collective-permute-start(bf16[1,352,128]{2,1,0:T(8,128)(2,1)S(1)} %get-tuple-element.11), channel_id=1, source_target_pairs={{0,256},{32,288},{64,320},{96,352},{128,384},{160,416},{192,448},{... | collective-permute-start | bytes 270344 | tf_op jit(solution)/shard_map/ppermute | solution.py:301
  22.6 35.2 %all-to-all-start = ((bf16[32,72,512]{2,1,0:T(8,128)(2,1)}), bf16[32,72,512]{2,1,0:T(8,128)(2,1)S(1)}, u32[]{:S(2)}, u32[]{:S(2)}) async-start(bf16[32,72,512]{2,1,0:T(8,128)(2,1)} %bitcast.9), calls=%async_computation | async-start | bytes 4718592 | tf_op jit(solution)/shard_map/all_to_all | solution.py:306
  29.4 25.7 %copy-start = (bf16[2,352,128]{2,1,0:T(8,128)(2,1)}, bf16[2,352,128]{2,1,0:T(8,128)(2,1)S(1)}, u32[]{:S(2)}) copy-start(bf16[2,352,128]{2,1,0:T(8,128)(2,1)S(1)} %pad_maximum_fusion.1.p0) | copy-start | bytes 540676
  29.4 9.3 %collective-permute-start.4 = (bf16[2,352,128]{2,1,0:T(8,128)(2,1)S(1)}, bf16[2,352,128]{2,1,0:T(8,128)(2,1)S(1)}, u32[]{:S(2)}, u32[]{:S(2)}) collective-permute-start(bf16[2,352,128]{2,1,0:T(8,128)(2,1)S(1)} %pad_maximum_fusion.1.p0), channel_id=1, source_target_pairs={{0,192},{32,224},{64,128},{96,160},{128,64},{160,96},{192,0},{224,... | collective-permute-start | bytes 540680 | tf_op jit(solution)/shard_map/ppermute | solution.py:301
  31.3 16.2 %collective-permute-start.3 = (bf16[2,352,128]{2,1,0:T(8,128)(2,1)S(1)}, bf16[2,352,128]{2,1,0:T(8,128)(2,1)S(1)}, u32[]{:S(2)}, u32[]{:S(2)}) collective-permute-start(bf16[2,352,128]{2,1,0:T(8,128)(2,1)S(1)} %pad_maximum_fusion.1.p0), channel_id=1, source_target_pairs={{0,128},{32,160},{64,192},{96,224},{128,0},{160,32},{192,64},{224,... | collective-permute-start | bytes 540680 | tf_op jit(solution)/shard_map/ppermute | solution.py:301
  34.2 13.3 %collective-permute-start.2 = (bf16[2,352,128]{2,1,0:T(8,128)(2,1)S(1)}, bf16[2,352,128]{2,1,0:T(8,128)(2,1)S(1)}, u32[]{:S(2)}, u32[]{:S(2)}) collective-permute-start(bf16[2,352,128]{2,1,0:T(8,128)(2,1)S(1)} %pad_maximum_fusion.1.p0), channel_id=1, source_target_pairs={{0,64},{32,96},{64,0},{96,32},{128,192},{160,224},{192,128},{224,1... | collective-permute-start | bytes 540680 | tf_op jit(solution)/shard_map/ppermute | solution.py:301
  38.7 16.4 %copy-start.1 = (bf16[2,352,128]{2,1,0:T(8,128)(2,1)}, bf16[2,352,128]{2,1,0:T(8,128)(2,1)S(1)}, u32[]{:S(2)}) copy-start(bf16[2,352,128]{2,1,0:T(8,128)(2,1)S(1)} %collective-permute-done.4.p3) | copy-start | bytes 540676
  47.5 7.6 %copy-start.2 = (bf16[2,352,128]{2,1,0:T(8,128)(2,1)}, bf16[2,352,128]{2,1,0:T(8,128)(2,1)S(1)}, u32[]{:S(2)}) copy-start(bf16[2,352,128]{2,1,0:T(8,128)(2,1)S(1)} %collective-permute-done.3.p2) | copy-start | bytes 540676
  47.5 7.6 %copy-start.3 = (bf16[2,352,128]{2,1,0:T(8,128)(2,1)}, bf16[2,352,128]{2,1,0:T(8,128)(2,1)S(1)}, u32[]{:S(2)}) copy-start(bf16[2,352,128]{2,1,0:T(8,128)(2,1)S(1)} %collective-permute-done.2.p1) | copy-start | bytes 540676
  48.5 6.0 %collective-permute-start.5 = (bf16[8,352,128]{2,1,0:T(8,128)(2,1)}, bf16[8,352,128]{2,1,0:T(8,128)(2,1)}, u32[]{:S(2)}, u32[]{:S(2)}) collective-permute-start(bf16[8,352,128]{2,1,0:T(8,128)(2,1)} %pad_maximum_fusion), channel_id=1, source_target_pairs={{0,32},{32,0},{64,96},{96,64},{128,160},{160,128},{192,224},{224,1... | collective-permute-start | bytes 2162696 | tf_op jit(solution)/shard_map/ppermute | solution.py:301
  67.6 8.6 %collective-permute-start.6 = (bf16[8,5,16,128]{3,2,1,0:T(8,128)(2,1)S(1)}, bf16[8,5,16,128]{3,2,1,0:T(8,128)(2,1)S(1)}, u32[]{:S(2)}, u32[]{:S(2)}) collective-permute-start(bf16[8,5,16,128]{3,2,1,0:T(8,128)(2,1)S(1)} %get-tuple-element.14), channel_id=1, source_target_pairs={{0,32},{32,0},{64,96},{96,64},{128,160},{160,128},{192,224},{224,1... | collective-permute-start | bytes 491528 | tf_op jit(solution)/shard_map/ppermute | solution.py:301
